TPU v7x, 512 devices: a whole 4x8x8 slice. The times are simulated.
512 devices in a mesh: frames: 8 (over y), bricks: 64 (over z, x, core).
Axes of the slice: x: 4, y: 8, z: 8, core: 2. Of those that a mesh axis runs over, the one named last changes fastest.
Arguments:
- recording: bfloat16 [128, 256, 16, 256], P('frames', 'bricks'), may hold values from -1 to 2
- traces: bfloat16 [128, 2048], P('frames', 'bricks'), may hold values from 0 to 2
- footprints: bfloat16 [2048, 16384], P('bricks'), may hold values from 0 to 1, as said below
- block_owner: int32 [2048, 1], P('bricks'), may hold values from 0 to 63; in each aligned block of 32 rows (0 to 31, 32 to 63, ...) at most 4 rows name the same one
- block_slot: int32 [2048], P('bricks'), may hold values from 0 to 31
Outputs:
- traces_new: float32 [128, 2048], P('frames', 'bricks')
- footprints_new: bfloat16 [2048, 16384], P('bricks')
Inputs may be any that keep to these rules, and one draw needn't show every extreme that they name: `footprints`: each row is positive on exactly 128 voxels forming a run in the slab's flat voxel order taken circularly, and 0 elsewhere; positive entries are at least 0.02. `block_owner`: among the 32 blocks of one slab, at most 4 have the same owner.
All inputs are finite; a program needn't handle non-finite values.
Results may differ from a plain program's by a relative error of at most 0.0033.
Values may be sent and summed in bfloat16 or wider, within the bound.
No kernel may reach another device: no remote copies, remote signals or barrier semaphores. Data moves between devices by JAX's collectives and lax.ppermute only.
A program may use at most 64 MiB of HBM per device.

v0:
```python
import jax
import jax.numpy as jnp
from jax import lax
from jax.sharding import PartitionSpec as P

TIME_STEP = 0.14
EDGE_SCALE = 1.0
HIGHEST = lax.Precision.HIGHEST


def padded_2(cells, sides, width):
    for axis, dim in sides:
        count = lax.axis_size(axis)
        ends = count - 1
        head = lax.slice_in_dim(cells, 0, width, axis=dim)
        tail = lax.slice_in_dim(cells, cells.shape[dim] - width, cells.shape[dim], axis=dim)
        cells = jnp.concatenate(
            [
                lax.ppermute(tail, axis, [(i, (i + 1) % count) for i in range(ends)]),
                cells,
                lax.ppermute(head, axis, [((i + 1) % count, i) for i in range(ends)]),
            ],
            axis=dim,
        )
    return cells


def edge_flux(center, other):
    difference = other - center
    return difference / (1.0 + (difference / EDGE_SCALE) ** 2)


def relax_once(extended):
    center = extended[:, 1:-1]
    padded = jnp.pad(center, ((0, 0), (0, 0), (1, 1), (1, 1)))
    summed_flux = edge_flux(center, extended[:, 2:]) + edge_flux(center, extended[:, :-2])
    summed_flux = (
        summed_flux
        + edge_flux(center, padded[:, :, 2:, 1:-1])
        + edge_flux(center, padded[:, :, :-2, 1:-1])
    )
    summed_flux = (
        summed_flux
        + edge_flux(center, padded[:, :, 1:-1, 2:])
        + edge_flux(center, padded[:, :, 1:-1, :-2])
    )
    return center + TIME_STEP * summed_flux


def denoise(recording):
    current = recording.astype(jnp.float32)
    for sweep in range(3):
        extended = padded_2(current, (("bricks", 1),), 1)
        current = relax_once(extended)
    return current


def contract_first(left, right, precision=None):
    return lax.dot_general(
        left,
        right,
        (((0,), (0,)), ((), ())),
        precision=precision,
        preferred_element_type=jnp.float32,
    )


def finish_rows(foot_rows, product_rows, gram_rows, diag_rows, foot_all):
    current = foot_rows.astype(jnp.float32)
    gradient = product_rows - jnp.dot(gram_rows, foot_all.astype(jnp.float32), precision=HIGHEST)
    stepped = jnp.where(
        current > 0, jnp.maximum(current + gradient / (diag_rows + 1.0)[:, None], 0.0), 0.0
    )
    return stepped.astype(jnp.bfloat16)


def shards(recording, traces, footprints, block_owner, block_slot):
    frame_count = recording.shape[0]
    voxels = footprints.shape[1]
    owned = traces.shape[1]
    n_bricks = lax.axis_size("bricks")
    all_comps = owned * n_bricks
    denoised = denoise(recording).astype(jnp.bfloat16).reshape(frame_count, voxels)
    owner = block_owner[:, 0]
    component = owner * owned + block_slot
    selector = (component[None, :] == jnp.arange(all_comps, dtype=jnp.int32)[:, None]).astype(
        jnp.bfloat16
    )
    all_prior = lax.all_gather(traces, "bricks", axis=1, tiled=True)
    slot_traces = jnp.dot(all_prior, selector, preferred_element_type=jnp.float32)
    correlation = lax.dot_general(
        footprints, footprints, (((1,), (1,)), ((), ())), preferred_element_type=jnp.float32
    )
    projected = lax.dot_general(
        denoised, footprints, (((1,), (1,)), ((), ())), preferred_element_type=jnp.float32
    )
    partial_value = projected - jnp.dot(slot_traces, correlation, precision=HIGHEST)
    diag_part = jnp.diagonal(correlation)
    selector_wide = selector.astype(jnp.float32)
    dense = lax.dot_general(
        partial_value,
        selector_wide,
        (((1,), (1,)), ((), ())),
        precision=HIGHEST,
        preferred_element_type=jnp.float32,
    )
    dense_diag = lax.dot_general(
        diag_part[None, :],
        selector_wide,
        (((1,), (1,)), ((), ())),
        precision=HIGHEST,
        preferred_element_type=jnp.float32,
    )
    summed, diag_sum = (
        lax.psum_scatter(dense, "bricks", scatter_dimension=1, tiled=True),
        lax.psum_scatter(dense_diag, "bricks", scatter_dimension=1, tiled=True),
    )
    traces_new = jnp.maximum(0.0, traces.astype(jnp.float32) + summed / (diag_sum + 1.0))
    new_bf = traces_new.astype(jnp.bfloat16)
    all_new = lax.all_gather(new_bf, "bricks", axis=1, tiled=True)
    slot_new = jnp.dot(all_new, selector, preferred_element_type=jnp.float32)
    new_slots_bf = slot_new.astype(jnp.bfloat16)
    gram_part = contract_first(slot_new, slot_new, HIGHEST)
    product_part = contract_first(new_slots_bf, denoised)
    product, gram = lax.psum((product_part, gram_part), "frames")
    footprints_new = finish_rows(footprints, product, gram, jnp.diagonal(gram), footprints)
    return (traces_new, footprints_new)


def solution(mesh):
    return jax.shard_map(
        shards,
        mesh=mesh,
        in_specs=(
            P("frames", "bricks", None, None),
            P("frames", "bricks"),
            P("bricks", None),
            P("bricks", None),
            P("bricks"),
        ),
        out_specs=(P("frames", "bricks"), P("bricks", None)),
        check_vma=False,
    )
```

profile of v0, /device:TPU:1, one launch (start us, length us, event | category | flops | bytes accessed | tf_op | source)
XLA Modules:
  0.0 476.8 jit_solution(13456563481450966813)
XLA Ops:
  7.2 1.1 fusion.28
  8.3 4.5 collective-permute-start.1
  12.8 5.6 %collective-permute-start = (f32[16,1,16,256]{3,2,1,0:T(8,128)S(1)}, f32[16,1,16,256]{3,2,1,0:T(8,128)S(1)}, u32[]{:S(2)}, u32[]{:S(2)}) collective-permute-start(f32[16,1,16,256]{3,2,1,0:T(8,128)S(1)} %get-tuple-element.8), channel_id=1, source_target_pairs={{1,0},{2,1},{3,2},{4,3},{5,4},{6,5},{7,6},{8,7},{9,8},{10,9},{11,1... | collective-permute-start | bytes 786440 | tf_op jit(solution)/shard_map/ppermute | solution.py:21
  18.4 2.0 fusion.29
  20.5 0.7 gather_fusion
  21.3 1.7 convert_add_fusion
  23.0 1.9 collective-permute-start.3
  24.9 2.4 collective-permute-start.2
  27.4 1.6 convolution_bitcast_fusion
  29.0 53.4 %all-gather = bf16[64,32,16]{1,2,0:T(8,128)(2,1)S(1)} all-gather(bf16[1,32,16]{1,2,0:T(8,128)(2,1)S(1)} %bitcast.48), channel_id=1, replica_groups=mesh['frames'=8,'bricks'=64] {'bricks'}, dimensions={0}, use_global_device_ids=true | all-gather | bytes 66560 | tf_op jit(solution)/shard_map/all_gather | solution.py:89
  82.8 1.6 multiply_add_fusion
  84.5 2.1 collective-permute-start.5
  86.6 2.4 collective-permute-start.4
  89.9 4.4 collective-permute-done.4
  94.3 1.6 add_convert_fusion
  96.6 1.6 convolution_bitcast_fusion.1
  98.3 82.2 %reduce-scatter.9.cloned.1.call-done = f32[32,1]{1,0:T(8,128)} async-done(((f32[2048,1]{1,0:T(8,128)}), f32[32,1]{1,0:T(8,128)}) %reduce-scatter.9.cloned.1.call-update) | async-done | bytes 144
  181.3 151.4 %reduce-scatter.7.cloned.1.call-done = f32[32,16]{1,0:T(8,128)} async-done(((f32[2048,16]{1,0:T(8,128)}), f32[32,16]{1,0:T(8,128)}) %reduce-scatter.7.cloned.1.call-update) | async-done | bytes 2064
  332.6 0.8 copy.12
  334.0 48.8 %all-gather.1 = bf16[64,32,16]{1,2,0:T(8,128)(2,1)S(1)} all-gather(bf16[1,32,16]{1,2,0:T(8,128)(2,1)S(1)} %get-tuple-element.2), channel_id=1, replica_groups=mesh['frames'=8,'bricks'=64] {'bricks'}, dimensions={0}, use_global_device_ids=true | all-gather | bytes 66560 | tf_op jit(solution)/shard_map/all_gather | solution.py:120
  383.5 1.8 fusion.23
  385.5 24.2 %psum.15 = f32[32,32]{1,0:T(8,128)S(1)} all-reduce(f32[32,32]{1,0:T(8,128)S(1)} %fusion.31), channel_id=1, replica_groups=mesh['frames'=8,'bricks'=64] {'frames'}, use_global_device_ids=true, to_apply=%region_3.4 | all-reduce | flops 1024 | bytes 8192 | tf_op jit(solution)/shard_map/psum | solution.py:125
  410.4 55.9 %all-reduce.5.cloned.1.call-done = f32[32,16384]{1,0:T(8,128)} async-done(((f32[32,16384]{1,0:T(8,128)}), f32[32,16384]{1,0:T(8,128)}) %all-reduce.5.cloned.1.call-update) | async-done | bytes 2097168 | tf_op jit(solution)/shard_map/psum | solution.py:125
  466.3 4.0 fusion.4
  (41 shorter events, 5.3 us)
Async XLA Ops:
  7.2 13.2 %copy-start.1 = (bf16[16,4,16,256]{3,2,1,0:T(8,128)(2,1)S(1)}, bf16[16,4,16,256]{3,2,1,0:T(8,128)(2,1)}, u32[]{:S(2)}) copy-start(bf16[16,4,16,256]{3,2,1,0:T(8,128)(2,1)} %param.5) | copy-start | bytes 1572868
  7.2 173.3 %reduce-scatter.9.cloned.1.call-start = ((), (), s32[]{:S(2)}) async-start(), calls=%async_computation.4 | async-start | bytes 1064960
  8.3 13.0 %collective-permute-start.1 = (f32[16,1,16,256]{3,2,1,0:T(8,128)S(1)}, f32[16,1,16,256]{3,2,1,0:T(8,128)S(1)}, u32[]{:S(2)}, u32[]{:S(2)}) collective-permute-start(f32[16,1,16,256]{3,2,1,0:T(8,128)S(1)} %get-tuple-element.9), channel_id=1, source_target_pairs={{0,1},{1,2},{2,3},{3,4},{4,5},{5,6},{6,7},{7,8},{8,9},{9,10},{10,1... | collective-permute-start | bytes 786440 | tf_op jit(solution)/shard_map/ppermute | solution.py:19
  12.8 8.4 %copy-start.3 = (s32[32]{0:T(128)S(1)}, s32[32]{0:T(128)}, u32[]{:S(2)}) copy-start(s32[32]{0:T(128)} %param.9) | copy-start | bytes 388
  12.8 8.4 %copy-start.4 = (s32[32,1]{0,1:T(1,128)S(1)}, s32[32,1]{0,1:T(1,128)}, u32[]{:S(2)}) copy-start(s32[32,1]{0,1:T(1,128)} %param.8) | copy-start | bytes 388
  12.8 8.4 %collective-permute-start = (f32[16,1,16,256]{3,2,1,0:T(8,128)S(1)}, f32[16,1,16,256]{3,2,1,0:T(8,128)S(1)}, u32[]{:S(2)}, u32[]{:S(2)}) collective-permute-start(f32[16,1,16,256]{3,2,1,0:T(8,128)S(1)} %get-tuple-element.8), channel_id=1, source_target_pairs={{1,0},{2,1},{3,2},{4,3},{5,4},{6,5},{7,6},{8,7},{9,8},{10,9},{11,1... | collective-permute-start | bytes 786440 | tf_op jit(solution)/shard_map/ppermute | solution.py:21
  22.9 6.1 %copy-start.2 = (bf16[16,32]{1,0:T(8,128)(2,1)S(1)}, bf16[16,32]{1,0:T(8,128)(2,1)}, u32[]{:S(2)}) copy-start(bf16[16,32]{1,0:T(8,128)(2,1)} %param.6) | copy-start | bytes 3076
  23.0 59.8 %collective-permute-start.3 = (f32[16,1,16,256]{3,2,1,0:T(8,128)S(1)}, f32[16,1,16,256]{3,2,1,0:T(8,128)S(1)}, u32[]{:S(2)}, u32[]{:S(2)}) collective-permute-start(f32[16,1,16,256]{3,2,1,0:T(8,128)S(1)} %get-tuple-element.7), channel_id=1, source_target_pairs={{0,1},{1,2},{2,3},{3,4},{4,5},{5,6},{6,7},{7,8},{8,9},{9,10},{10,1... | collective-permute-start | bytes 786440 | tf_op jit(solution)/shard_map/ppermute | solution.py:19
  24.9 57.9 %collective-permute-start.2 = (f32[16,1,16,256]{3,2,1,0:T(8,128)S(1)}, f32[16,1,16,256]{3,2,1,0:T(8,128)S(1)}, u32[]{:S(2)}, u32[]{:S(2)}) collective-permute-start(f32[16,1,16,256]{3,2,1,0:T(8,128)S(1)} %get-tuple-element.6), channel_id=1, source_target_pairs={{1,0},{2,1},{3,2},{4,3},{5,4},{6,5},{7,6},{8,7},{9,8},{10,9},{11,1... | collective-permute-start | bytes 786440 | tf_op jit(solution)/shard_map/ppermute | solution.py:21
  29.0 303.7 %reduce-scatter.7.cloned.1.call-start = ((), (), s32[]{:S(2)}) async-start(), calls=%async_computation.3 | async-start | bytes 1064960
  84.5 11.7 %copy-start = (bf16[32,16384]{1,0:T(8,128)(2,1)S(1)}, bf16[32,16384]{1,0:T(8,128)(2,1)}, u32[]{:S(2)}) copy-start(bf16[32,16384]{1,0:T(8,128)(2,1)} %param.7) | copy-start | bytes 3145732
  84.5 5.4 %collective-permute-start.5 = (f32[16,1,16,256]{3,2,1,0:T(8,128)S(1)}, f32[16,1,16,256]{3,2,1,0:T(8,128)S(1)}, u32[]{:S(2)}, u32[]{:S(2)}) collective-permute-start(f32[16,1,16,256]{3,2,1,0:T(8,128)S(1)} %get-tuple-element.5), channel_id=1, source_target_pairs={{0,1},{1,2},{2,3},{3,4},{4,5},{5,6},{6,7},{7,8},{8,9},{9,10},{10,1... | collective-permute-start | bytes 786440 | tf_op jit(solution)/shard_map/ppermute | solution.py:19
  86.6 7.7 %collective-permute-start.4 = (f32[16,1,16,256]{3,2,1,0:T(8,128)S(1)}, f32[16,1,16,256]{3,2,1,0:T(8,128)S(1)}, u32[]{:S(2)}, u32[]{:S(2)}) collective-permute-start(f32[16,1,16,256]{3,2,1,0:T(8,128)S(1)} %get-tuple-element.4), channel_id=1, source_target_pairs={{1,0},{2,1},{3,2},{4,3},{5,4},{6,5},{7,6},{8,7},{9,8},{10,9},{11,1... | collective-permute-start | bytes 786440 | tf_op jit(solution)/shard_map/ppermute | solution.py:21
  98.2 368.1 %all-reduce.5.cloned.1.call-start = ((), (), s32[]{:S(2)}) async-start(), calls=%async_computation.2 | async-start | bytes 4194304 | tf_op jit(solution)/shard_map/psum | solution.py:125
Sparse Core Ops, SparseCore 0:
  29.1 151.3 reduce-scatter.8
  185.6 146.9 reduce-scatter.6
  385.4 80.8 all-reduce.4
where the time goes:
time: 480 us; the launch traced here: 477 us
  waiting for transfers between devices  294 us (61%)
  blocking collectives  126 us (26%)
  starting transfers between devices  19 us (4%)
  between operations  14 us (3%)
  matrix products  12.2 us (3%)
  other arithmetic  6.39 us (1%)
    unnamed x5, waiting for transfers between devices  234 us
    psum x1, waiting for transfers between devices, shards(): product, gram = lax.psum((product_part, gram_part), 'frames')  55.9 us
    all_gather x1, blocking collectives, shards(): all_prior = lax.all_gather(traces, 'bricks', axis=1, tiled=True)  53.4 us
    all_gather x1, blocking collectives, shards(): all_new = lax.all_gather(new_bf, 'bricks', axis=1, tiled=True)  48.8 us
    psum x1, blocking collectives, shards(): product, gram = lax.psum((product_part, gram_part), 'frames')  24.2 us
    ppermute x3, starting transfers between devices, padded_2(): lax.ppermute(head, axis, [((i + 1) % count, i) for i in range(ends)])  10.4 us
  transfers between devices with their start and end apart: 9, of which 5 were waited for; matrix products, arithmetic and copies ran while one was open for 3% of the time, Pallas kernels for 0%

commit v1 on v0

v1 whole, which is shorter than its diff:
```python
import jax
import jax.numpy as jnp
from jax import lax
from jax.experimental import pallas as pl
from jax.experimental.pallas import tpu as pltpu
from jax.sharding import PartitionSpec as P

TIME_STEP = 0.14
HIGHEST = lax.Precision.HIGHEST
LANES = 128


def flux_of(difference):
    return difference / (1.0 + difference * difference)


def halo_planes(recording, width):
    count = lax.axis_size("bricks")
    planes = recording.shape[1]
    tail = lax.slice_in_dim(recording, planes - width, planes, axis=1)
    head = lax.slice_in_dim(recording, 0, width, axis=1)
    low = lax.ppermute(tail, "bricks", [(i, i + 1) for i in range(count - 1)])
    high = lax.ppermute(head, "bricks", [(i + 1, i) for i in range(count - 1)])
    return low, high


def run_starts(footprints):
    inside = footprints > 0
    before = jnp.roll(inside, 1, axis=1)
    place = lax.broadcasted_iota(jnp.int32, footprints.shape, 1)
    return jnp.sum(jnp.where(inside & ~before, place, 0), axis=1, dtype=jnp.int32)


def windows_kernel(starts, foot, windows, corr):
    blocks, voxels = foot.shape
    tiles = voxels // LANES
    lane = lax.broadcasted_iota(jnp.int32, (blocks, LANES), 1)
    acc = jnp.zeros((blocks, LANES), jnp.float32)
    for k in range(blocks):
        start = starts[k]
        first = start // LANES
        second = (first + 1) % tiles
        offset = start - first * LANES
        one = foot[:, pl.ds(pl.multiple_of(first * LANES, LANES), LANES)].astype(jnp.float32)
        two = foot[:, pl.ds(pl.multiple_of(second * LANES, LANES), LANES)].astype(jnp.float32)
        window = jnp.where(lane >= offset, one, two)
        windows[k] = window
        column = jnp.sum(window * window[k : k + 1], axis=1, keepdims=True)
        acc = jnp.where(lane == k, column, acc)
    corr[...] = acc


def foot_windows(starts, footprints):
    blocks, voxels = footprints.shape
    vmem = pl.BlockSpec(memory_space=pltpu.VMEM)
    return pl.pallas_call(
        windows_kernel,
        in_specs=[pl.BlockSpec(memory_space=pltpu.SMEM), vmem],
        out_specs=[vmem, vmem],
        out_shape=[
            jax.ShapeDtypeStruct((blocks, blocks, LANES), jnp.float32),
            jax.ShapeDtypeStruct((blocks, LANES), jnp.float32),
        ],
        name="windows",
    )(starts, footprints)


def relax(planes, low_keep, high_keep, masks):
    first_row, last_row, first_col, last_col = masks
    across = [flux_of(planes[i + 1] - planes[i]) for i in range(len(planes) - 1)]
    out = []
    for i in range(1, len(planes) - 1):
        u = planes[i]
        edge = flux_of(-u)
        rows, cols = u.shape
        nxt = jnp.where(last_row, 0.0, pltpu.roll(u, rows - 1, 0))
        down = flux_of(nxt - u)
        up = jnp.where(first_row, -edge, pltpu.roll(down, 1, 0))
        nxt = jnp.where(last_col, 0.0, pltpu.roll(u, cols - 1, 1))
        right = flux_of(nxt - u)
        left = jnp.where(first_col, -edge, pltpu.roll(right, 1, 1))
        total = (across[i] - across[i - 1]) + (down - up) + (right - left)
        out.append(u + TIME_STEP * total)
    return out


def denoise_kernel(starts, keep, rec, low, high, windows, voxel_windows, projected, field):
    frames, planes, rows, cols = rec.shape
    width = low.shape[1]
    halves = cols // LANES
    low_keep = keep[0]
    high_keep = keep[1]
    row = lax.broadcasted_iota(jnp.int32, (rows, cols), 0)
    col = lax.broadcasted_iota(jnp.int32, (rows, cols), 1)
    masks = (row == 0, row == rows - 1, col == 0, col == cols - 1)

    def one_frame(f, carry):
        u = [low[f, i].astype(jnp.float32) for i in range(width)]
        u = u + [rec[f, i].astype(jnp.float32) for i in range(planes)]
        u = u + [high[f, i].astype(jnp.float32) for i in range(width)]
        for sweep in range(width):
            u = relax(u, low_keep, high_keep, masks)
            extra = width - 1 - sweep
            if extra:
                u = (
                    [v * low_keep for v in u[:extra]]
                    + u[extra : extra + planes]
                    + [v * high_keep for v in u[extra + planes :]]
                )
        for i in range(planes):
            rounded = u[i].astype(jnp.bfloat16).astype(jnp.float32)
            for h in range(halves):
                at = pl.multiple_of(f * (planes * rows) + i * rows, rows)
                field[h, pl.ds(at, rows), :] = rounded[:, h * LANES : (h + 1) * LANES]
        return carry

    lax.fori_loop(0, frames, one_frame, 0)
    blocks = windows.shape[0]
    tiles = planes * rows * halves
    lane = lax.broadcasted_iota(jnp.int32, (frames, LANES), 1)
    acc = jnp.zeros((frames, LANES), jnp.float32)
    for k in range(blocks):
        start = starts[k]
        first = start // LANES
        second = (first + 1) % tiles
        offset = start - first * LANES
        one = field[first % halves, pl.ds(first // halves, frames, stride=planes * rows), :]
        two = field[second % halves, pl.ds(second // halves, frames, stride=planes * rows), :]
        window = jnp.where(lane >= offset, one, two)
        voxel_windows[k] = window
        column = jnp.sum(window * windows[k, k : k + 1, :], axis=1, keepdims=True)
        acc = jnp.where(lane == k, column, acc)
    projected[...] = acc


def denoise_windows(starts, keep, recording, low, high, windows):
    frames, planes, rows, cols = recording.shape
    blocks = windows.shape[0]
    vmem = pl.BlockSpec(memory_space=pltpu.VMEM)
    smem = pl.BlockSpec(memory_space=pltpu.SMEM)
    return pl.pallas_call(
        denoise_kernel,
        in_specs=[smem, smem, vmem, vmem, vmem, vmem],
        out_specs=[vmem, vmem],
        out_shape=[
            jax.ShapeDtypeStruct((blocks, frames, LANES), jnp.float32),
            jax.ShapeDtypeStruct((frames, LANES), jnp.float32),
        ],
        scratch_shapes=[pltpu.VMEM((cols // LANES, frames * planes * rows, LANES), jnp.float32)],
        cost_estimate=pl.CostEstimate(flops=10**9, transcendentals=0, bytes_accessed=20 * 10**6),
        name="denoise",
    )(starts, keep, recording, low, high, windows)


def finish_kernel(starts, products, gram, windows, out):
    blocks, voxels = out.shape
    tiles = voxels // LANES
    lane = lax.broadcasted_iota(jnp.int32, (blocks, LANES), 1)
    row = lax.broadcasted_iota(jnp.int32, (blocks, LANES), 0)
    out[...] = jnp.zeros(out.shape, out.dtype)
    product = jnp.sum(products[...], axis=0)
    for k in range(blocks):
        start = starts[k]
        first = start // LANES
        second = (first + 1) % tiles
        offset = start - first * LANES
        spread = jnp.sum(windows[k] * gram[:, k : k + 1], axis=0, keepdims=True)
        current = windows[k, k : k + 1, :]
        gradient = product[k : k + 1, :] - spread
        stepped = jnp.maximum(current + gradient / (gram[k : k + 1, k : k + 1] + 1.0), 0.0)
        stepped = jnp.where(current > 0, stepped, 0.0)
        at = pl.ds(pl.multiple_of(first * LANES, LANES), LANES)
        old = out[:, at].astype(jnp.float32)
        out[:, at] = jnp.where((row == k) & (lane >= offset), stepped, old).astype(out.dtype)
        at = pl.ds(pl.multiple_of(second * LANES, LANES), LANES)
        old = out[:, at].astype(jnp.float32)
        out[:, at] = jnp.where((row == k) & (lane < offset), stepped, old).astype(out.dtype)


def finish(starts, products, gram, windows, voxels):
    blocks = windows.shape[0]
    vmem = pl.BlockSpec(memory_space=pltpu.VMEM)
    return pl.pallas_call(
        finish_kernel,
        in_specs=[pl.BlockSpec(memory_space=pltpu.SMEM), vmem, vmem, vmem],
        out_specs=vmem,
        out_shape=jax.ShapeDtypeStruct((blocks, voxels), jnp.bfloat16),
        name="finish",
    )(starts, products, gram, windows)


def to_all(piece, axis):
    count = lax.axis_size(axis)
    return lax.all_to_all(jnp.broadcast_to(piece[None], (count,) + piece.shape), axis, 0, 0)


def shards(recording, traces, footprints, block_owner, block_slot):
    frames, owned = traces.shape
    blocks, voxels = footprints.shape
    owners = lax.axis_size("bricks")
    position = lax.axis_index("bricks")
    low, high = halo_planes(recording, 3)
    keep = jnp.stack([position > 0, position < owners - 1]).astype(jnp.float32)
    starts = run_starts(footprints)
    windows, corr = foot_windows(starts, footprints)
    corr = corr[:, :blocks]
    diag = jnp.diagonal(corr)
    owner = block_owner[:, 0]
    component = owner * owned + block_slot

    diag_high = diag.astype(jnp.bfloat16)
    diag_low = (diag - diag_high.astype(jnp.float32)).astype(jnp.bfloat16)
    extra = jnp.stack(
        [owner.astype(jnp.bfloat16), block_slot.astype(jnp.bfloat16), diag_high, diag_low]
    )
    piece = jnp.concatenate([traces.reshape(-1), extra.reshape(-1)]).reshape(-1, LANES)
    piece = jnp.pad(piece, ((0, -piece.shape[0] % 8), (0, 0)))
    prior = to_all(piece, "bricks").reshape(owners, -1).astype(jnp.float32)
    cells = frames * owned
    prior_traces = prior[:, :cells].reshape(owners, frames, owned)
    extras = prior[:, cells : cells + 4 * blocks].reshape(owners, 4, blocks)
    all_owner = extras[:, 0].reshape(-1).astype(jnp.int32)
    all_slot = extras[:, 1].reshape(-1).astype(jnp.int32)
    all_comp = all_owner * owned + all_slot
    all_diag = (extras[:, 2] + extras[:, 3]).reshape(-1)

    voxel_windows, projected = denoise_windows(starts, keep, recording, low, high, windows)
    projected = projected[:, :blocks]

    pick_owner = (owner[:, None] == jnp.arange(owners, dtype=jnp.int32)[None, :]).astype(jnp.bfloat16)
    rows = jnp.dot(
        pick_owner,
        prior[:, :cells].astype(jnp.bfloat16),
        preferred_element_type=jnp.float32,
    ).reshape(blocks, frames, owned)
    pick_slot = block_slot[:, None] == jnp.arange(owned, dtype=jnp.int32)[None, :]
    slot_prior = jnp.sum(jnp.where(pick_slot[:, None, :], rows, 0.0), axis=2).T

    partial_value = projected - jnp.dot(slot_prior, corr, precision=HIGHEST)
    gathered = to_all(partial_value.T.reshape(-1, LANES), "bricks").reshape(owners * blocks, frames)

    mine = position * owned + jnp.arange(owned, dtype=jnp.int32)
    target = jnp.concatenate([mine, component])
    match = (target[:, None] == all_comp[None, :]).astype(jnp.float32)
    summed = jnp.dot(match, gathered, precision=HIGHEST)
    diag_sum = jnp.dot(match, all_diag[:, None], precision=HIGHEST)
    before = jnp.concatenate([traces.astype(jnp.float32).T, slot_prior.T])
    after = jnp.maximum(0.0, before + summed / (diag_sum + 1.0)).T
    traces_new = after[:, :owned]
    slot_new = after[:, owned:].astype(jnp.bfloat16).astype(jnp.float32)

    product_part = jnp.sum(voxel_windows * slot_new.T[:, :, None], axis=1)
    sent = jnp.concatenate(
        [product_part, slot_new.reshape(-1, LANES), jnp.zeros((4, LANES), jnp.float32)]
    )
    shared = to_all(sent, "frames")
    groups = shared.shape[0]
    all_slots = shared[:, blocks : blocks + 4].reshape(groups * frames, blocks)
    gram = lax.dot_general(
        all_slots.astype(jnp.bfloat16),
        all_slots.astype(jnp.bfloat16),
        (((0,), (0,)), ((), ())),
        preferred_element_type=jnp.float32,
    )
    footprints_new = finish(starts, shared[:, :blocks], gram, windows, voxels)
    return (traces_new, footprints_new)


def solution(mesh):
    return jax.shard_map(
        shards,
        mesh=mesh,
        in_specs=(
            P("frames", "bricks", None, None),
            P("frames", "bricks"),
            P("bricks", None),
            P("bricks", None),
            P("bricks"),
        ),
        out_specs=(P("frames", "bricks"), P("bricks", None)),
        check_vma=False,
    )
```

time: 480 us -> 94.5 us (0.20)
  waiting for transfers between devices: 294 us -> 14.8 us
  blocking collectives: 126 us -> 15.2 us
  Pallas kernels: 0 us -> 16.2 us
  starting transfers between devices: 19 us -> 33.1 us
  between operations: 14 us -> 0.88 us
  matrix products: 12.2 us -> 3.19 us
    unnamed x5 -> x0, waiting for transfers between devices: 234 us -> none
    all_gather x2 -> x0, blocking collectives: 102 us -> none  [the longest x1 53.4 us: shards(): all_prior = lax.all_gather(traces, 'bricks', axis=1, tiled=True)]
    psum x1 -> x0, waiting for transfers between devices: 55.9 us -> none  [shards(): product, gram = lax.psum((product_part, gram_part), 'frames')]
    all_to_all x0 -> x2, starting transfers between devices: none -> 27.5 us  [to_all(): lax.all_to_all(jnp.broadcast_to(piece[None], (count,) + piece.shape), axi...]
    psum x1 -> x0, blocking collectives: 24.2 us -> none  [shards(): product, gram = lax.psum((product_part, gram_part), 'frames')]
    pallas_call x0 -> x3, Pallas kernels: none -> 16.2 us  [the longest x1 11.2 us: denoise_windows(): pl.pallas_call(denoise_kernel, in_specs=[smem, smem, vmem, vmem, vmem, vm...]
    all_to_all x0 -> x1, blocking collectives: none -> 15.2 us  [to_all(): lax.all_to_all(jnp.broadcast_to(piece[None], (count,) + piece.shape), axi...]
    all_to_all x0 -> x2, waiting for transfers between devices: none -> 14.8 us  [to_all(): lax.all_to_all(jnp.broadcast_to(piece[None], (count,) + piece.shape), axi...]
  transfers between devices with their start and end apart: 9 -> 4, of which waited for: 5 -> 2; matrix products, arithmetic and copies ran while one was open for 3% -> 3% of each run, Pallas kernels for 0% -> 0%
where the time goes in v1:
time: 94.5 us; the launch traced here: 94 us
  starting transfers between devices  33.1 us (35%)
  Pallas kernels  16.2 us (17%)
  blocking collectives  15.2 us (16%)
  waiting for transfers between devices  14.8 us (16%)
  local copies, waits for them, and re-layouts  6.25 us (7%)
  other arithmetic  4.27 us (5%)
  matrix products  3.19 us (3%)
    all_to_all x2, starting transfers between devices, to_all(): lax.all_to_all(jnp.broadcast_to(piece[None], (count,) + piece.shape), axi...  27.5 us
    all_to_all x1, blocking collectives, to_all(): lax.all_to_all(jnp.broadcast_to(piece[None], (count,) + piece.shape), axi...  15.2 us
    all_to_all x2, waiting for transfers between devices, to_all(): lax.all_to_all(jnp.broadcast_to(piece[None], (count,) + piece.shape), axi...  14.8 us
    pallas_call x1, Pallas kernels, denoise_windows(): pl.pallas_call(denoise_kernel, in_specs=[smem, smem, vmem, vmem, vmem, vm...  11.2 us
    ppermute x1, starting transfers between devices, halo_planes(): low = lax.ppermute(tail, 'bricks', [(i, i + 1) for i in range(count - 1)])  3.2 us
    pallas_call x1, Pallas kernels, finish(): pl.pallas_call(finish_kernel, in_specs=[pl.BlockSpec(memory_space=pltpu.S...  2.64 us
    pallas_call x1, Pallas kernels, foot_windows(): pl.pallas_call(windows_kernel, in_specs=[pl.BlockSpec(memory_space=pltpu....  2.43 us
    ppermute x1, starting transfers between devices, halo_planes(): high = lax.ppermute(head, 'bricks', [(i + 1, i) for i in range(count - 1)])  2.36 us
  transfers between devices with their start and end apart: 4, of which 2 were waited for; matrix products, arithmetic and copies ran while one was open for 3% of the time, Pallas kernels for 0%

profile of v1, /device:TPU:1, one launch (start us, length us, event | category | flops | bytes accessed | tf_op | source)
XLA Modules:
  0.0 94.0 jit_solution(17664261673243246013)
XLA Ops:
  0.7 1.6 %broadcast_compare_fusion = pred[32,16384]{1,0:T(8,128)(4,1)S(1)} fusion(bf16[32,16384]{1,0:T(8,128)(2,1)} %foot.1), kind=kLoop, calls=%fused_computation.12 | loop fusion | flops 524288 | bytes 1572864 | tf_op jit(solution)/shard_map/gt | solution.py:28
  2.3 1.3 %select_reduce_fusion.starts = s32[32]{0:T(128)} fusion(pred[32,16383]{1,0:T(8,128)(4,1)S(1)} %bitcast.47, pred[32,1]{1,0:T(8,128)(4,1)S(1)} %slice.72, bf16[32,16384]{1,0:T(8,128)(2,1)S(1)} %copy-done.1), kind=kLoop, calls=%fused_computation.1 | loop fusion | flops 4194272 | bytes 1572992 | tf_op jit(solution)/shard_map/reduce_sum | solution.py:31
  3.7 2.4 %windows.1 = (f32[32,32,128]{2,1,0:T(8,128)}, f32[32,128]{1,0:T(8,128)}) custom-call(s32[32]{0:T(128)} %select_reduce_fusion.starts, bf16[32,16384]{1,0:T(8,128)(2,1)} %foot.1), custom_call_target="tpu_custom_call" | custom-call | tf_op jit(solution)/shard_map/windows/pallas_call | solution.py:56
  6.1 1.5 %gather_fusion = f32[32]{0:T(128)S(1)} fusion(f32[32,32]{1,0:T(8,128)} %bitcast.46, s32[32]{0:T(128)S(1)} %or_bitcast_fusion), kind=kCustom, calls=%fused_computation | custom fusion | bytes 512 | tf_op jit(solution)/shard_map/jit(diagonal)/cond/branch_0_fun/gather | solution.py:207
  7.8 0.7 broadcast_in_dim.32
  8.5 14.8 %all-to-all-start = ((bf16[64,8,128]{2,1,0:T(8,128)(2,1)}), bf16[64,8,128]{2,1,0:T(8,128)(2,1)S(1)}, u32[]{:S(2)}, u32[]{:S(2)}) async-start(bf16[64,8,128]{2,1,0:T(8,128)(2,1)} %broadcast_in_dim.32), calls=%async_computation | async-start | bytes 262144 | tf_op jit(solution)/shard_map/all_to_all | solution.py:194
  23.4 2.4 %collective-permute-start.1 = (bf16[16,3,16,256]{3,2,1,0:T(8,128)(2,1)S(1)}, bf16[16,3,16,256]{3,2,1,0:T(8,128)(2,1)S(1)}, u32[]{:S(2)}, u32[]{:S(2)}) collective-permute-start(bf16[16,3,16,256]{3,2,1,0:T(8,128)(2,1)S(1)} %get-tuple-element.10), channel_id=1, source_target_pairs={{1,0},{2,1},{3,2},{4,3},{5,4},{6,5},{7,6},{8,7},{9,8},{10,9},{11,1... | collective-permute-start | bytes 1179656 | tf_op jit(solution)/shard_map/ppermute | solution.py:23
  25.8 3.2 %collective-permute-start = (bf16[16,3,16,256]{3,2,1,0:T(8,128)(2,1)S(1)}, bf16[16,3,16,256]{3,2,1,0:T(8,128)(2,1)S(1)}, u32[]{:S(2)}, u32[]{:S(2)}) collective-permute-start(bf16[16,3,16,256]{3,2,1,0:T(8,128)(2,1)S(1)} %get-tuple-element.11), channel_id=1, source_target_pairs={{0,1},{1,2},{2,3},{3,4},{4,5},{5,6},{6,7},{7,8},{8,9},{9,10},{10,1... | collective-permute-start | bytes 1179656 | tf_op jit(solution)/shard_map/ppermute | solution.py:22
  29.1 0.7 add_convert_fusion.keep
  29.9 4.5 %all-to-all-done = bf16[64,8,128]{2,1,0:T(8,128)(2,1)S(1)} async-done(((bf16[64,8,128]{2,1,0:T(8,128)(2,1)}), bf16[64,8,128]{2,1,0:T(8,128)(2,1)S(1)}, u32[]{:S(2)}, u32[]{:S(2)}) %all-to-all-start) | async-done | bytes 131104 | tf_op jit(solution)/shard_map/all_to_all | solution.py:194
  34.4 0.2 copy.12
  35.2 0.7 copy-done.8
  36.0 11.2 %denoise.1 = (f32[32,16,128]{2,1,0:T(8,128)}, f32[16,128]{1,0:T(8,128)}) custom-call(s32[32]{0:T(128)} %select_reduce_fusion.starts, f32[2]{0:T(128)} %add_convert_fusion.keep, bf16[16,4,16,256]{3,2,1,0:T(8,128)(2,1)} %rec.1, bf16[16,3,16,256]{3,2,1,0:T(8,128)(2,1)} %copy-done.9, bf16[16,3,16,256]{3,2,1,0:T(8,128)(2,1)} %copy-done.8, ...), custom_call_target="tpu_custom_call" | custom-call | flops 1000000000 | bytes 20000000 | tf_op jit(solution)/shard_map/denoise/pallas_call | solution.py:141
  47.2 0.9 subtract_bitcast_fusion
  48.2 0.7 broadcast_in_dim.54
  48.9 12.7 %all-to-all-start.1 = ((f32[64,4,128]{2,1,0:T(4,128)}), f32[64,4,128]{2,1,0:T(4,128)S(1)}, u32[]{:S(2)}, u32[]{:S(2)}) async-start(f32[64,4,128]{2,1,0:T(4,128)} %broadcast_in_dim.54), calls=%async_computation.1 | async-start | bytes 262144 | tf_op jit(solution)/shard_map/all_to_all | solution.py:194
  62.1 0.4 fusion.4
  62.5 10.3 %all-to-all-done.1 = f32[64,4,128]{2,1,0:T(4,128)S(1)} async-done(((f32[64,4,128]{2,1,0:T(4,128)}), f32[64,4,128]{2,1,0:T(4,128)S(1)}, u32[]{:S(2)}, u32[]{:S(2)}) %all-to-all-start.1) | async-done | bytes 131104 | tf_op jit(solution)/shard_map/all_to_all | solution.py:194
  72.8 0.3 reshape.119
  73.1 1.0 %fusion.3 = f32[16,64]{1,0:T(8,128)S(1)} fusion(f32[2048,16]{1,0:T(8,128)S(1)} %reshape.119, s32[2048]{0:T(1024)S(1)} %add.47, s32[64]{0:T(128)S(1)} %pad_add_fusion, f32[32,16]{0,1:T(8,128)S(1)} %copy.13, f32[32,16]{0,1:T(8,128)S(1)} %convert_bitcast_fusion, f32[64]{0:T(128)S(1)} %fusion.4), kind=kOutput, calls=%fused_computation.7 | convolution fusion | flops 25300992 | bytes 147968 | tf_op jit(solution)/shard_map/dot_general | solution.py:245
  74.6 15.2 %all_to_all.15 = f32[8,40,128]{2,1,0:T(8,128)S(1)} all-to-all(f32[8,40,128]{2,1,0:T(8,128)S(1)} %broadcast_in_dim.56), channel_id=1, replica_groups=mesh['frames'=8,'bricks'=64] {'frames'}, dimensions={0} | all-to-all | bytes 327680 | tf_op jit(solution)/shard_map/all_to_all | solution.py:194
  89.9 0.8 fusion.24.gram
  90.7 0.7 slice.82.products
  91.4 2.6 %finish.1 = bf16[32,16384]{1,0:T(8,128)(2,1)} custom-call(s32[32]{0:T(128)} %select_reduce_fusion.starts, f32[8,32,128]{2,1,0:T(8,128)} %slice.82.products, f32[32,32]{1,0:T(8,128)} %fusion.24.gram, f32[32,32,128]{2,1,0:T(8,128)} %get-tuple-element.7.windows), custom_call_target="tpu_custom_call" | custom-call | tf_op jit(solution)/shard_map/finish/pallas_call | solution.py:183
  (61 shorter events, 2.4 us)
Async XLA Ops:
  0.6 1.7 %copy-start.1 = (bf16[32,16384]{1,0:T(8,128)(2,1)S(1)}, bf16[32,16384]{1,0:T(8,128)(2,1)}, u32[]{:S(2)}) copy-start(bf16[32,16384]{1,0:T(8,128)(2,1)} %foot.1) | copy-start | bytes 3145732
  3.7 3.9 %copy-start.6 = (s32[32,1]{0,1:T(1,128)S(1)}, s32[32,1]{0,1:T(1,128)}, u32[]{:S(2)}) copy-start(s32[32,1]{0,1:T(1,128)} %param.8) | copy-start | bytes 388
  3.7 3.9 %copy-start.5 = (bf16[16,32]{1,0:T(8,128)(2,1)S(1)}, bf16[16,32]{1,0:T(8,128)(2,1)}, u32[]{:S(2)}) copy-start(bf16[16,32]{1,0:T(8,128)(2,1)} %param.6) | copy-start | bytes 3076
  3.7 4.0 %copy-start.7 = (s32[32]{0:T(128)S(1)}, s32[32]{0:T(128)}, u32[]{:S(2)}) copy-start(s32[32]{0:T(128)} %param.9) | copy-start | bytes 388
  3.7 19.7 %copy-start.2 = (bf16[16,4,16,256]{3,2,1,0:T(8,128)(2,1)S(1)}, bf16[16,4,16,256]{3,2,1,0:T(8,128)(2,1)}, u32[]{:S(2)}) copy-start(bf16[16,4,16,256]{3,2,1,0:T(8,128)(2,1)} %rec.1) | copy-start | bytes 1572868
  8.5 25.9 %all-to-all-start = ((bf16[64,8,128]{2,1,0:T(8,128)(2,1)}), bf16[64,8,128]{2,1,0:T(8,128)(2,1)S(1)}, u32[]{:S(2)}, u32[]{:S(2)}) async-start(bf16[64,8,128]{2,1,0:T(8,128)(2,1)} %broadcast_in_dim.32), calls=%async_computation | async-start | bytes 262144 | tf_op jit(solution)/shard_map/all_to_all | solution.py:194
  23.4 11.7 %collective-permute-start.1 = (bf16[16,3,16,256]{3,2,1,0:T(8,128)(2,1)S(1)}, bf16[16,3,16,256]{3,2,1,0:T(8,128)(2,1)S(1)}, u32[]{:S(2)}, u32[]{:S(2)}) collective-permute-start(bf16[16,3,16,256]{3,2,1,0:T(8,128)(2,1)S(1)} %get-tuple-element.10), channel_id=1, source_target_pairs={{1,0},{2,1},{3,2},{4,3},{5,4},{6,5},{7,6},{8,7},{9,8},{10,9},{11,1... | collective-permute-start | bytes 1179656 | tf_op jit(solution)/shard_map/ppermute | solution.py:23
  25.8 9.4 %collective-permute-start = (bf16[16,3,16,256]{3,2,1,0:T(8,128)(2,1)S(1)}, bf16[16,3,16,256]{3,2,1,0:T(8,128)(2,1)S(1)}, u32[]{:S(2)}, u32[]{:S(2)}) collective-permute-start(bf16[16,3,16,256]{3,2,1,0:T(8,128)(2,1)S(1)} %get-tuple-element.11), channel_id=1, source_target_pairs={{0,1},{1,2},{2,3},{3,4},{4,5},{5,6},{6,7},{7,8},{8,9},{9,10},{10,1... | collective-permute-start | bytes 1179656 | tf_op jit(solution)/shard_map/ppermute | solution.py:22
  35.1 0.7 copy-start.8
  35.2 0.9 copy-start.9
  36.0 11.2 %copy-start = (f32[32,128]{1,0:T(8,128)S(1)}, f32[32,128]{1,0:T(8,128)}, u32[]{:S(2)}) copy-start(f32[32,128]{1,0:T(8,128)} %get-tuple-element.6) | copy-start | bytes 49156
  48.9 23.8 %all-to-all-start.1 = ((f32[64,4,128]{2,1,0:T(4,128)}), f32[64,4,128]{2,1,0:T(4,128)S(1)}, u32[]{:S(2)}, u32[]{:S(2)}) async-start(f32[64,4,128]{2,1,0:T(4,128)} %broadcast_in_dim.54), calls=%async_computation.1 | async-start | bytes 262144 | tf_op jit(solution)/shard_map/all_to_all | solution.py:194
  62.5 11.9 %copy-start.3 = (f32[32,16,128]{2,1,0:T(8,128)S(1)}, f32[32,16,128]{2,1,0:T(8,128)}, u32[]{:S(2)}) copy-start(f32[32,16,128]{2,1,0:T(8,128)} %get-tuple-element.9) | copy-start | bytes 786436
  74.1 19.9 %copy-start.4 = (f32[16,64]{1,0:T(8,128)}, f32[16,64]{1,0:T(8,128)S(1)}, u32[]{:S(2)}) copy-start(f32[16,64]{1,0:T(8,128)S(1)} %fusion.3) | copy-start | bytes 12292

commit v2 on v0

v2 whole, which is shorter than its diff:
```python
import jax
import jax.numpy as jnp
from jax import lax
from jax.experimental import pallas as pl
from jax.experimental.pallas import tpu as pltpu
from jax.sharding import PartitionSpec as P


TIME_STEP = 0.14
HIGHEST = lax.Precision.HIGHEST
LANES = 128
SUBLANES = 8
F32 = jnp.float32
BF16 = jnp.bfloat16
VMEM = pl.BlockSpec(memory_space=pltpu.VMEM)
SMEM = pl.BlockSpec(memory_space=pltpu.SMEM)


def iota(shape, axis):
    return lax.broadcasted_iota(jnp.int32, shape, axis)


def onehot(mask):
    return jnp.where(mask, 1.0, 0.0).astype(BF16)


def split_run(start, tiles):
    first = start >> 7
    return first, (first + 1) & (tiles - 1), start & (LANES - 1)


def lane_tile(index):
    return pl.ds(pl.multiple_of(index * LANES, LANES), LANES)


def two_terms(value):
    high = value.astype(BF16).astype(F32)
    return high, value - high


def prepare_kernel(base, foot, starts, windows, compact, corr, piece):
    blocks, voxels = foot.shape
    tiles = voxels // LANES
    acc = jnp.zeros((blocks, LANES), BF16)
    for t in range(1, tiles):
        cell = foot[:, t * LANES : (t + 1) * LANES]
        acc = acc + jnp.where(cell > 0, jnp.asarray(t, BF16), jnp.asarray(0, BF16))
    tile_of = acc.astype(F32)
    lowest = jnp.min(tile_of, axis=1, keepdims=True)
    highest = jnp.max(tile_of, axis=1, keepdims=True)
    first_tile = jnp.where(highest - lowest > 1.5, highest, lowest)
    behind = jnp.sum(jnp.where(tile_of != first_tile, 1.0, 0.0), axis=1, keepdims=True)
    begin = (first_tile * LANES + behind).astype(jnp.int32)
    lane = iota((blocks, LANES), 1)
    row = iota((blocks, LANES), 0)
    sums = jnp.zeros((blocks, LANES), F32)
    for k in range(blocks):
        start = begin[k, 0]
        starts[k] = start
        first, second, offset = split_run(start, tiles)
        one = foot[:, lane_tile(first)].astype(F32)
        two = foot[:, lane_tile(second)].astype(F32)
        window = jnp.where(lane >= offset, one, two)
        windows[k] = window.astype(BF16)
        own = window[k : k + 1]
        compact[k : k + 1, :] = own
        sums = jnp.where(lane == k, jnp.sum(window * own, axis=1, keepdims=True), sums)
    corr[...] = sums
    diag = jnp.sum(jnp.where(lane == row, sums, 0.0), axis=1, keepdims=True)
    placed = jnp.where(lane == 2 * SUBLANES + row % SUBLANES, diag, 0.0)
    groups = blocks // SUBLANES
    rows = [
        jnp.sum(placed[q * SUBLANES : (q + 1) * SUBLANES], axis=0, keepdims=True)
        for q in range(groups)
    ]
    terms = [two_terms(r) for r in rows]
    part = jnp.concatenate([t[0] for t in terms] + [t[1] for t in terms], axis=0)
    whole = (base[...] + part).astype(BF16)
    piece[...] = jnp.broadcast_to(whole[None], piece.shape)


def prepare(base, footprints, owners):
    blocks, _ = footprints.shape
    return pl.pallas_call(
        prepare_kernel,
        in_specs=[VMEM, VMEM],
        out_specs=[SMEM, VMEM, VMEM, VMEM, VMEM],
        out_shape=[
            jax.ShapeDtypeStruct((blocks,), jnp.int32),
            jax.ShapeDtypeStruct((blocks, blocks, LANES), BF16),
            jax.ShapeDtypeStruct((blocks, LANES), F32),
            jax.ShapeDtypeStruct((blocks, LANES), F32),
            jax.ShapeDtypeStruct((owners, SUBLANES, LANES), BF16),
        ],
        name="prepare",
    )(base, footprints)


def flux_of(difference):
    return difference / (1.0 + difference * difference)


def relax(planes, masks):
    first_row, last_row, first_col, last_col = masks
    across = [
        [[flux_of(planes[i + 1][z][y] - planes[i][z][y]) for y in range(2)] for z in range(2)]
        for i in range(len(planes) - 1)
    ]
    out = []
    for i in range(1, len(planes) - 1):
        u = planes[i]
        edge = [[flux_of(u[0][0]), flux_of(u[0][1])], [flux_of(u[1][0]), None]]
        total = [[across[i][z][y] - across[i - 1][z][y] for y in range(2)] for z in range(2)]
        for y in range(2):
            low = pltpu.roll(u[0][y], SUBLANES - 1, 0)
            high = pltpu.roll(u[1][y], SUBLANES - 1, 0)
            down_low = flux_of(jnp.where(last_row, high, low) - u[0][y])
            down_high = flux_of(jnp.where(last_row, 0.0, high) - u[1][y])
            up_low = pltpu.roll(down_low, 1, 0)
            up_high = pltpu.roll(down_high, 1, 0)
            total[0][y] = total[0][y] + (down_low - jnp.where(first_row, edge[0][y], up_low))
            total[1][y] = total[1][y] + (down_high - jnp.where(first_row, up_low, up_high))
        for z in range(2):
            low = pltpu.roll(u[z][0], LANES - 1, 1)
            high = pltpu.roll(u[z][1], LANES - 1, 1)
            right_low = flux_of(jnp.where(last_col, high, low) - u[z][0])
            right_high = flux_of(jnp.where(last_col, 0.0, high) - u[z][1])
            left_low = pltpu.roll(right_low, 1, 1)
            left_high = pltpu.roll(right_high, 1, 1)
            total[z][0] = total[z][0] + (right_low - jnp.where(first_col, edge[z][0], left_low))
            total[z][1] = total[z][1] + (right_high - jnp.where(first_col, left_low, left_high))
        out.append([[u[z][y] + TIME_STEP * total[z][y] for y in range(2)] for z in range(2)])
    return out


def quarters(plane):
    wide = plane.astype(F32)
    return [
        [wide[z * SUBLANES : (z + 1) * SUBLANES, y * LANES : (y + 1) * LANES] for y in range(2)]
        for z in range(2)
    ]


def scaled(plane, keep):
    return [[cell * keep for cell in line] for line in plane]


def denoise_kernel(starts, rec, low, high, compact, voxel_windows, projected, field):
    frames, planes, rows, _ = rec.shape
    width = low.shape[1]
    position = lax.axis_index("bricks")
    low_keep = jnp.where(position > 0, 1.0, 0.0)
    high_keep = jnp.where(position < lax.axis_size("bricks") - 1, 1.0, 0.0)
    row = iota((SUBLANES, LANES), 0)
    col = iota((SUBLANES, LANES), 1)
    masks = (row == 0, row == SUBLANES - 1, col == 0, col == LANES - 1)

    def one_frame(f, carry):
        u = [quarters(low[f, i]) for i in range(width)]
        u = u + [quarters(rec[f, i]) for i in range(planes)]
        u = u + [quarters(high[f, i]) for i in range(width)]
        for sweep in range(width):
            u = relax(u, masks)
            extra = width - 1 - sweep
            if extra:
                u = (
                    [scaled(v, low_keep) for v in u[:extra]]
                    + u[extra : extra + planes]
                    + [scaled(v, high_keep) for v in u[extra + planes :]]
                )
        for i in range(planes):
            for z in range(2):
                for y in range(2):
                    at = pl.multiple_of(f * (planes * rows) + i * rows + z * SUBLANES, SUBLANES)
                    field[y, pl.ds(at, SUBLANES), :] = u[i][z][y].astype(BF16).astype(F32)
        return carry

    lax.fori_loop(0, frames, one_frame, 0)
    blocks = compact.shape[0]
    tiles = planes * rows * 2
    lane = iota((frames, LANES), 1)
    acc = jnp.zeros((frames, LANES), F32)
    for k in range(blocks):
        first, second, offset = split_run(starts[k], tiles)
        one = field[first & 1, pl.ds(first >> 1, frames, stride=planes * rows), :]
        two = field[second & 1, pl.ds(second >> 1, frames, stride=planes * rows), :]
        window = jnp.where(lane >= offset, one, two)
        voxel_windows[k] = window
        column = jnp.sum(window * compact[k : k + 1, :], axis=1, keepdims=True)
        acc = jnp.where(lane == k, column, acc)
    projected[...] = acc


def denoise_windows(starts, recording, low, high, compact):
    frames, planes, rows, _ = recording.shape
    blocks = compact.shape[0]
    return pl.pallas_call(
        denoise_kernel,
        in_specs=[SMEM, VMEM, VMEM, VMEM, VMEM],
        out_specs=[VMEM, VMEM],
        out_shape=[
            jax.ShapeDtypeStruct((blocks, frames, LANES), F32),
            jax.ShapeDtypeStruct((frames, LANES), F32),
        ],
        scratch_shapes=[pltpu.VMEM((2, frames * planes * rows, LANES), F32)],
        name="denoise",
    )(starts, recording, low, high, compact)


def combine_kernel(prior, labels, projected, corr, piece, slot_prior):
    owners = prior.shape[0]
    blocks = corr.shape[0]
    frames = projected.shape[0]
    span = owners * SUBLANES
    flat = prior[...].astype(F32).reshape(span, LANES).astype(BF16)
    owner = labels[:, 0:1]
    slot = labels[:, 1:2]
    source = iota((blocks, span), 1)
    pick = jnp.concatenate(
        [onehot(source == owner * SUBLANES + i) for i in range(SUBLANES)], axis=0
    )
    found = jnp.dot(pick, flat, preferred_element_type=F32)
    lane = iota((blocks, LANES), 1)
    wanted = (lane >= LANES // 2) & (lane % blocks == slot)
    parts = [
        jnp.where(wanted, found[i * blocks : (i + 1) * blocks], 0.0).astype(BF16)
        for i in range(SUBLANES)
    ]
    wide = SUBLANES * LANES
    here = iota((wide, LANES), 0)
    frame_of = (here // LANES) * 2 + (here % LANES - LANES // 2) // blocks
    frame_of = jnp.where(here % LANES >= LANES // 2, frame_of, -1)
    spread = onehot(frame_of == iota((wide, LANES), 1) % frames)
    earlier = jnp.dot(jnp.concatenate(parts, axis=1), spread, preferred_element_type=F32)
    slot_prior[...] = earlier
    repeat = jnp.where(
        iota((frames, LANES), 0) == iota((frames, LANES), 1) % frames, 1.0, 0.0
    )
    tiled = lax.dot_general(
        projected[...],
        repeat,
        (((0,), (0,)), ((), ())),
        precision=HIGHEST,
        preferred_element_type=F32,
    )[:blocks]
    value = tiled - jnp.dot(
        corr[:, :blocks], earlier, precision=HIGHEST, preferred_element_type=F32
    )
    row = iota((blocks, LANES), 0)
    value = jnp.where(lane // frames == row % SUBLANES, value, 0.0)
    lines = [
        jnp.sum(value[q * SUBLANES : (q + 1) * SUBLANES], axis=0, keepdims=True)
        for q in range(blocks // SUBLANES)
    ]
    terms = [two_terms(v) for v in lines]
    whole = jnp.concatenate([t[0] for t in terms] + [t[1] for t in terms], axis=0).astype(BF16)
    piece[...] = jnp.broadcast_to(whole[None], piece.shape)


def combine(prior, labels, projected, corr):
    blocks = corr.shape[0]
    return pl.pallas_call(
        combine_kernel,
        in_specs=[VMEM, VMEM, VMEM, VMEM],
        out_specs=[VMEM, VMEM],
        out_shape=[
            jax.ShapeDtypeStruct(prior.shape, BF16),
            jax.ShapeDtypeStruct((blocks, LANES), F32),
        ],
        name="combine",
    )(prior, labels, projected, corr)


def update_kernel(prior, gathered, labels, traces, slot_prior, voxel_windows, traces_new, sent):
    owners = prior.shape[0]
    blocks = slot_prior.shape[0]
    frames, owned = traces.shape
    span = owners * SUBLANES
    flat = prior[...].astype(F32).reshape(span, LANES).astype(BF16)
    values = gathered[...].astype(F32).reshape(span, LANES).astype(BF16)
    lead = 4 * SUBLANES
    picks = onehot(iota((lead, LANES), 0) == iota((lead, LANES), 1))
    lists = lax.dot_general(
        picks, flat, (((1,), (1,)), ((), ())), preferred_element_type=F32
    )
    comps = lists[:SUBLANES] * float(owned) + lists[SUBLANES : 2 * SUBLANES]
    diags = lists[2 * SUBLANES : 3 * SUBLANES]
    position = lax.axis_index("bricks")
    asked = labels[:, 0:1] * owned + labels[:, 1:2]
    held = position * owned + iota((owned, 1), 0)
    target = jnp.concatenate([asked, held], axis=0).astype(F32)
    count = blocks + owned
    matches = []
    weight = jnp.zeros((count, span), F32)
    for j in range(SUBLANES):
        match = comps[j : j + 1] == target
        matches.append(onehot(match))
        weight = weight + jnp.where(match, diags[j : j + 1], 0.0)
    weight = jnp.sum(weight, axis=1, keepdims=True)
    sums = jnp.dot(jnp.concatenate(matches, axis=0), values, preferred_element_type=F32)
    group = iota((count, LANES), 1) // frames
    total = jnp.zeros((count, LANES), F32)
    for j in range(SUBLANES):
        total = jnp.where(group == j, sums[j * count : (j + 1) * count], total)
    shift = LANES // 2
    while shift >= frames:
        total = total + pltpu.roll(total, shift, 1)
        shift //= 2
    repeat = onehot(iota((frames, LANES), 0) == iota((frames, LANES), 1) % frames)
    mine = lax.dot_general(
        traces[...], repeat, (((0,), (0,)), ((), ())), preferred_element_type=F32
    )
    before = jnp.concatenate([slot_prior[...], mine], axis=0)
    after = jnp.maximum(0.0, before + total / (weight + 1.0))
    padded = jnp.concatenate([after, jnp.zeros((LANES - count, LANES), F32)], axis=0)
    turned = padded.T
    traces_new[...] = turned[:frames, blocks:count]
    slots = turned[:frames].astype(BF16).astype(F32)
    lane = iota((SUBLANES, LANES), 1)
    packed = jnp.where(
        lane < blocks,
        slots[:SUBLANES],
        jnp.where(lane < 2 * blocks, pltpu.roll(slots[SUBLANES:], blocks, 1), 0.0),
    )
    for k in range(blocks):
        line = jnp.sum(voxel_windows[k] * slots[:, k : k + 1], axis=0, keepdims=True)
        for g in range(sent.shape[0]):
            sent[g, k : k + 1, :] = line
    for g in range(sent.shape[0]):
        sent[g, blocks : blocks + SUBLANES, :] = packed


def update(prior, gathered, labels, traces, slot_prior, voxel_windows, groups):
    blocks = slot_prior.shape[0]
    return pl.pallas_call(
        update_kernel,
        in_specs=[VMEM] * 6,
        out_specs=[VMEM, VMEM],
        out_shape=[
            jax.ShapeDtypeStruct(traces.shape, F32),
            jax.ShapeDtypeStruct((groups, blocks + SUBLANES, LANES), F32),
        ],
        name="update",
    )(prior, gathered, labels, traces, slot_prior, voxel_windows)


def finish_kernel(starts, shared, windows, compact, out):
    blocks, voxels = out.shape
    tiles = voxels // LANES
    groups = shared.shape[0]
    lane = iota((blocks, LANES), 1)
    row = iota((blocks, LANES), 0)
    out[...] = jnp.zeros(out.shape, out.dtype)
    product = shared[0, :blocks, :]
    for g in range(1, groups):
        product = product + shared[g, :blocks, :]
    slots = jnp.concatenate([shared[g, blocks:, :] for g in range(groups)], axis=0).astype(BF16)
    both = lax.dot_general(slots, slots, (((0,), (0,)), ((), ())), preferred_element_type=F32)
    gram = both[:blocks] + pltpu.roll(both[blocks : 2 * blocks], LANES - blocks, 1)
    norm = jnp.sum(jnp.where(lane == row, gram, 0.0), axis=1, keepdims=True) + 1.0
    spread = jnp.concatenate(
        [
            jnp.sum(windows[k].astype(F32) * gram[:, k : k + 1], axis=0, keepdims=True)
            for k in range(blocks)
        ],
        axis=0,
    )
    current = compact[...]
    stepped = jnp.maximum(current + (product - spread) / norm, 0.0)
    stepped = jnp.where(current > 0, stepped, 0.0)
    for k in range(blocks):
        first, second, offset = split_run(starts[k], tiles)
        for index, part in ((first, lane >= offset), (second, lane < offset)):
            at = lane_tile(index)
            old = out[:, at].astype(F32)
            out[:, at] = jnp.where((row == k) & part, stepped, old).astype(out.dtype)


def finish(starts, shared, windows, compact, voxels):
    blocks = windows.shape[0]
    return pl.pallas_call(
        finish_kernel,
        in_specs=[SMEM, VMEM, VMEM, VMEM],
        out_specs=VMEM,
        out_shape=jax.ShapeDtypeStruct((blocks, voxels), BF16),
        name="finish",
    )(starts, shared, windows, compact)


def halo_planes(recording, width):
    count = lax.axis_size("bricks")
    planes = recording.shape[1]
    tail = lax.slice_in_dim(recording, planes - width, planes, axis=1)
    head = lax.slice_in_dim(recording, 0, width, axis=1)
    low = lax.ppermute(tail, "bricks", [(i, i + 1) for i in range(count - 1)])
    high = lax.ppermute(head, "bricks", [(i + 1, i) for i in range(count - 1)])
    return low, high


def label_piece(traces, labels):
    blocks = labels.shape[0]
    lists = labels.T.reshape(2, blocks // SUBLANES, SUBLANES).astype(F32)
    lists = jnp.concatenate([lists, lists], axis=1)
    gap = jnp.zeros((SUBLANES, LANES // 2 - 2 * SUBLANES), F32)
    return jnp.concatenate(
        [lists[0], lists[1], gap, traces.astype(F32).reshape(SUBLANES, -1)], axis=1
    )


def shards(recording, traces, footprints, block_owner, block_slot):
    voxels = footprints.shape[1]
    owners = lax.axis_size("bricks")
    groups = lax.axis_size("frames")
    low, high = halo_planes(recording, 3)
    labels = jnp.concatenate([block_owner, block_slot[:, None]], axis=1)
    base = label_piece(traces, labels)
    starts, windows, compact, corr, piece = prepare(base, footprints, owners)
    prior = lax.all_to_all(piece, "bricks", 0, 0)
    voxel_windows, projected = denoise_windows(starts, recording, low, high, compact)
    partials, slot_prior = combine(prior, labels, projected, corr)
    gathered = lax.all_to_all(partials, "bricks", 0, 0)
    traces_new, sent = update(prior, gathered, labels, traces, slot_prior, voxel_windows, groups)
    shared = lax.all_to_all(sent, "frames", 0, 0)
    footprints_new = finish(starts, shared, windows, compact, voxels)
    return (traces_new, footprints_new)


def solution(mesh):
    return jax.shard_map(
        shards,
        mesh=mesh,
        in_specs=(
            P("frames", "bricks", None, None),
            P("frames", "bricks"),
            P("bricks", None),
            P("bricks", None),
            P("bricks"),
        ),
        out_specs=(P("frames", "bricks"), P("bricks", None)),
        check_vma=False,
    )
```

time: 480 us -> 85.2 us (0.18)
  waiting for transfers between devices: 294 us -> 0.01 us
  blocking collectives: 126 us -> 37 us
  Pallas kernels: 0 us -> 20.6 us
  between operations: 14 us -> 0.73 us
  matrix products: 12.2 us -> 0 us
  other arithmetic: 6.39 us -> 0.69 us
    unnamed x5 -> x0, waiting for transfers between devices: 234 us -> none
    all_gather x2 -> x0, blocking collectives: 102 us -> none  [the longest x1 53.4 us: shards(): all_prior = lax.all_gather(traces, 'bricks', axis=1, tiled=True)]
    psum x1 -> x0, waiting for transfers between devices: 55.9 us -> none  [shards(): product, gram = lax.psum((product_part, gram_part), 'frames')]
    all_to_all x0 -> x2, blocking collectives: none -> 37 us  [the longest x1 21.5 us: shards(): gathered = lax.all_to_all(partials, 'bricks', 0, 0)]
    psum x1 -> x0, blocking collectives: 24.2 us -> none  [shards(): product, gram = lax.psum((product_part, gram_part), 'frames')]
    pallas_call x0 -> x5, Pallas kernels: none -> 20.6 us  [the longest x1 10.2 us: denoise_windows(): pl.pallas_call(denoise_kernel, in_specs=[SMEM, VMEM, VMEM, VMEM, VMEM], o...]
    all_to_all x0 -> x1, starting transfers between devices: none -> 11.2 us  [shards(): prior = lax.all_to_all(piece, 'bricks', 0, 0)]
    dot_general x8 -> x0, matrix products: 9.04 us -> none  [the longest x1 3.95 us: finish_rows(): jnp.dot(gram_rows, foot_all.astype(jnp.float32), precision=HIGHEST)]
  transfers between devices with their start and end apart: 9 -> 3, of which waited for: 5 -> 0; matrix products, arithmetic and copies ran while one was open for 3% -> 2% of each run, Pallas kernels for 0% -> 15%
where the time goes in v2:
time: 85.2 us; the launch traced here: 84.7 us
  blocking collectives  37 us (43%)
  starting transfers between devices  21.2 us (25%)
  Pallas kernels  20.6 us (24%)
  local copies, waits for them, and re-layouts  4.35 us (5%)
    all_to_all x1, blocking collectives, shards(): gathered = lax.all_to_all(partials, 'bricks', 0, 0)  21.5 us
    all_to_all x1, blocking collectives, shards(): shared = lax.all_to_all(sent, 'frames', 0, 0)  15.5 us
    all_to_all x1, starting transfers between devices, shards(): prior = lax.all_to_all(piece, 'bricks', 0, 0)  11.2 us
    pallas_call x1, Pallas kernels, denoise_windows(): pl.pallas_call(denoise_kernel, in_specs=[SMEM, VMEM, VMEM, VMEM, VMEM], o...  10.2 us
    ppermute x1, starting transfers between devices, halo_planes(): high = lax.ppermute(head, 'bricks', [(i + 1, i) for i in range(count - 1)])  5.56 us
    ppermute x1, starting transfers between devices, halo_planes(): low = lax.ppermute(tail, 'bricks', [(i, i + 1) for i in range(count - 1)])  4.5 us
    pallas_call x1, Pallas kernels, finish(): pl.pallas_call(finish_kernel, in_specs=[SMEM, VMEM, VMEM, VMEM], out_spec...  2.78 us
    pallas_call x1, Pallas kernels, update(): pl.pallas_call(update_kernel, in_specs=[VMEM] * 6, out_specs=[VMEM, VMEM]...  2.75 us
  transfers between devices with their start and end apart: 3, of which 0 were waited for; matrix products, arithmetic and copies ran while one was open for 2% of the time, Pallas kernels for 15%

profile of v2, /device:TPU:1, one launch (start us, length us, event | category | flops | bytes accessed | tf_op | source)
XLA Modules:
  0.0 84.7 jit_solution(8187734413720311453)
XLA Ops:
  0.6 1.2 %fusion.3 = (bf16[16,3,16,256]{3,2,1,0:T(8,128)(2,1)S(1)}, bf16[16,3,16,256]{3,2,1,0:T(8,128)(2,1)S(1)}) fusion(bf16[16,4,16,256]{3,2,1,0:T(8,128)(2,1)} %rec.1), kind=kLoop, calls=%fused_computation.9 | loop fusion | bytes 1572864 | tf_op jit(solution)/shard_map/slice | solution.py:394
  1.8 4.5 %collective-permute-start = (bf16[16,3,16,256]{3,2,1,0:T(8,128)(2,1)S(1)}, bf16[16,3,16,256]{3,2,1,0:T(8,128)(2,1)S(1)}, u32[]{:S(2)}, u32[]{:S(2)}) collective-permute-start(bf16[16,3,16,256]{3,2,1,0:T(8,128)(2,1)S(1)} %get-tuple-element.25), channel_id=1, source_target_pairs={{0,1},{1,2},{2,3},{3,4},{4,5},{5,6},{6,7},{7,8},{8,9},{9,10},{10,1... | collective-permute-start | bytes 1179656 | tf_op jit(solution)/shard_map/ppermute | solution.py:395
  6.4 0.0 copy-start.4
  6.4 0.0 copy-start.5
  6.4 5.6 %collective-permute-start.1 = (bf16[16,3,16,256]{3,2,1,0:T(8,128)(2,1)S(1)}, bf16[16,3,16,256]{3,2,1,0:T(8,128)(2,1)S(1)}, u32[]{:S(2)}, u32[]{:S(2)}) collective-permute-start(bf16[16,3,16,256]{3,2,1,0:T(8,128)(2,1)S(1)} %get-tuple-element.24), channel_id=1, source_target_pairs={{1,0},{2,1},{3,2},{4,3},{5,4},{6,5},{7,6},{8,7},{9,8},{10,9},{11,1... | collective-permute-start | bytes 1179656 | tf_op jit(solution)/shard_map/ppermute | solution.py:396
  12.0 0.1 convert_element_type.12
  12.1 0.7 copy-done.3
  12.8 0.1 reshape.15
  12.8 0.1 pad.2.clone
  12.9 0.7 pad_maximum_fusion.1.base
  13.6 2.7 %prepare.1 = (s32[32]{0:T(128)}, bf16[32,32,128]{2,1,0:T(8,128)(2,1)}, f32[32,128]{1,0:T(8,128)}, f32[32,128]{1,0:T(8,128)}, bf16[64,8,128]{2,1,0:T(8,128)(2,1)}) custom-call(f32[8,128]{1,0:T(8,128)} %pad_maximum_fusion.1.base, bf16[32,16384]{1,0:T(8,128)(2,1)} %foot.1), custom_call_target="tpu_custom_call" | custom-call | tf_op jit(solution)/shard_map/prepare/pallas_call | solution.py:84
  16.3 11.2 %all-to-all-start = ((bf16[64,8,128]{2,1,0:T(8,128)(2,1)}), bf16[64,8,128]{2,1,0:T(8,128)(2,1)S(1)}, u32[]{:S(2)}, u32[]{:S(2)}) async-start(bf16[64,8,128]{2,1,0:T(8,128)(2,1)} %get-tuple-element.13), calls=%async_computation | async-start | bytes 262144 | tf_op jit(solution)/shard_map/all_to_all | solution.py:418
  27.5 0.7 copy.10.labels
  28.2 0.0 collective-permute-done.low
  28.2 0.7 copy-done.1
  28.9 0.1 copy-done.2
  29.1 10.2 %denoise.1 = (f32[32,16,128]{2,1,0:T(8,128)}, f32[16,128]{1,0:T(8,128)}) custom-call(s32[32]{0:T(128)} %get-tuple-element.14.starts, bf16[16,4,16,256]{3,2,1,0:T(8,128)(2,1)} %rec.1, bf16[16,3,16,256]{3,2,1,0:T(8,128)(2,1)} %copy-done.1, bf16[16,3,16,256]{3,2,1,0:T(8,128)(2,1)} %copy-done.2, f32[32,128]{1,0:T(8,128)} %get-tuple-element.15.compact), custom_call_target="tpu_custom_call" | custom-call | tf_op jit(solution)/shard_map/denoise/pallas_call | solution.py:197
  39.3 0.0 all-to-all-done.prior
  39.3 0.7 copy-done
  39.9 2.2 %combine.1 = (bf16[64,8,128]{2,1,0:T(8,128)(2,1)}, f32[32,128]{1,0:T(8,128)}) custom-call(bf16[64,8,128]{2,1,0:T(8,128)(2,1)} %copy-done, s32[32,2]{1,0:T(8,128)} %copy.10.labels, f32[16,128]{1,0:T(8,128)} %get-tuple-element.16.projected, f32[32,128]{1,0:T(8,128)} %get-tuple-element.17.corr), custom_call_target="tpu_custom_call" | custom-call | tf_op jit(solution)/shard_map/combine/pallas_call | solution.py:262
  42.1 21.5 %all_to_all.15.gathered = bf16[64,8,128]{2,1,0:T(8,128)(2,1)} all-to-all(bf16[64,8,128]{2,1,0:T(8,128)(2,1)} %get-tuple-element.18), channel_id=1, replica_groups=mesh['frames'=8,'bricks'=64] {'bricks'}, dimensions={0} | all-to-all | bytes 262144 | tf_op jit(solution)/shard_map/all_to_all | solution.py:421
  63.6 2.7 %update.1 = (f32[16,32]{1,0:T(8,128)}, f32[8,40,128]{2,1,0:T(8,128)}) custom-call(bf16[64,8,128]{2,1,0:T(8,128)(2,1)} %copy-done, bf16[64,8,128]{2,1,0:T(8,128)(2,1)} %all_to_all.15.gathered, s32[32,2]{1,0:T(8,128)} %copy.10.labels, bf16[16,32]{1,0:T(8,128)(2,1)} %traces.1, f32[32,128]{1,0:T(8,128)} %get-tuple-element.19.slot_prior, ...), custom_call_target="tpu_custom_call" | custom-call | tf_op jit(solution)/shard_map/update/pallas_call | solution.py:335
  66.4 15.5 %all_to_all.16.shared = f32[8,40,128]{2,1,0:T(8,128)} all-to-all(f32[8,40,128]{2,1,0:T(8,128)} %get-tuple-element.22), channel_id=1, replica_groups=mesh['frames'=8,'bricks'=64] {'frames'}, dimensions={0} | all-to-all | bytes 327680 | tf_op jit(solution)/shard_map/all_to_all | solution.py:423
  81.9 2.8 %finish.1 = bf16[32,16384]{1,0:T(8,128)(2,1)} custom-call(s32[32]{0:T(128)} %get-tuple-element.14.starts, f32[8,40,128]{2,1,0:T(8,128)} %all_to_all.16.shared, bf16[32,32,128]{2,1,0:T(8,128)(2,1)} %get-tuple-element.23.windows, f32[32,128]{1,0:T(8,128)} %get-tuple-element.15.compact), custom_call_target="tpu_custom_call" | custom-call | tf_op jit(solution)/shard_map/finish/pallas_call | solution.py:381
  (10 shorter events, 0.0 us)
Async XLA Ops:
  1.8 26.4 %collective-permute-start = (bf16[16,3,16,256]{3,2,1,0:T(8,128)(2,1)S(1)}, bf16[16,3,16,256]{3,2,1,0:T(8,128)(2,1)S(1)}, u32[]{:S(2)}, u32[]{:S(2)}) collective-permute-start(bf16[16,3,16,256]{3,2,1,0:T(8,128)(2,1)S(1)} %get-tuple-element.25), channel_id=1, source_target_pairs={{0,1},{1,2},{2,3},{3,4},{4,5},{5,6},{6,7},{7,8},{8,9},{9,10},{10,1... | collective-permute-start | bytes 1179656 | tf_op jit(solution)/shard_map/ppermute | solution.py:395
  6.4 5.6 %copy-start.4 = (s32[32]{0:T(128)S(1)}, s32[32]{0:T(128)}, u32[]{:S(2)}) copy-start(s32[32]{0:T(128)} %param.9) | copy-start | bytes 388
  6.4 5.6 %copy-start.5 = (s32[32,1]{0,1:T(1,128)S(1)}, s32[32,1]{0,1:T(1,128)}, u32[]{:S(2)}) copy-start(s32[32,1]{0,1:T(1,128)} %param.8) | copy-start | bytes 388
  6.4 21.8 %collective-permute-start.1 = (bf16[16,3,16,256]{3,2,1,0:T(8,128)(2,1)S(1)}, bf16[16,3,16,256]{3,2,1,0:T(8,128)(2,1)S(1)}, u32[]{:S(2)}, u32[]{:S(2)}) collective-permute-start(bf16[16,3,16,256]{3,2,1,0:T(8,128)(2,1)S(1)} %get-tuple-element.24), channel_id=1, source_target_pairs={{1,0},{2,1},{3,2},{4,3},{5,4},{6,5},{7,6},{8,7},{9,8},{10,9},{11,1... | collective-permute-start | bytes 1179656 | tf_op jit(solution)/shard_map/ppermute | solution.py:396
  12.1 0.7 copy-start.3
  16.3 22.9 %all-to-all-start = ((bf16[64,8,128]{2,1,0:T(8,128)(2,1)}), bf16[64,8,128]{2,1,0:T(8,128)(2,1)S(1)}, u32[]{:S(2)}, u32[]{:S(2)}) async-start(bf16[64,8,128]{2,1,0:T(8,128)(2,1)} %get-tuple-element.13), calls=%async_computation | async-start | bytes 262144 | tf_op jit(solution)/shard_map/all_to_all | solution.py:418
  28.2 0.7 copy-start.1
  28.2 0.9 %copy-start.2 = (bf16[16,3,16,256]{3,2,1,0:T(8,128)(2,1)}, bf16[16,3,16,256]{3,2,1,0:T(8,128)(2,1)S(1)}, u32[]{:S(2)}) copy-start(bf16[16,3,16,256]{3,2,1,0:T(8,128)(2,1)S(1)} %collective-permute-done.1.high) | copy-start | bytes 1179652
  39.3 0.7 copy-start

commit v3 on v2

--- a/solution.py
+++ b/solution.py
@@ -16,6 +16,14 @@
 SMEM = pl.BlockSpec(memory_space=pltpu.SMEM)
 
 
+def near(array):
+    return pltpu.with_memory_space_constraint(array, pltpu.VMEM)
+
+
+def near_scalar(array):
+    return pltpu.with_memory_space_constraint(array, pltpu.SMEM)
+
+
 def iota(shape, axis):
     return lax.broadcasted_iota(jnp.int32, shape, axis)
 
@@ -38,7 +46,33 @@
     return high, value - high
 
 
-def prepare_kernel(base, foot, starts, windows, compact, corr, piece):
+def label_rows(owner, slot, traces):
+    frames, owned = traces.shape
+    blocks = owner.shape[1]
+    lane = iota((1, LANES), 1)
+    gap = jnp.zeros((1, LANES - blocks), F32)
+    lists = [jnp.concatenate([x[...].astype(F32), gap], axis=1) for x in (owner, slot)]
+    rows = []
+    for q in range(blocks // SUBLANES):
+        first = pltpu.roll(lists[0], (LANES - q * SUBLANES) % LANES, 1)
+        second = pltpu.roll(lists[1], (LANES + SUBLANES - q * SUBLANES) % LANES, 1)
+        rows.append(
+            jnp.where(lane < SUBLANES, first, jnp.where(lane < 2 * SUBLANES, second, 0.0))
+        )
+    wide = jnp.concatenate(
+        [traces[...].astype(F32), jnp.zeros((frames, LANES - owned), F32)], axis=1
+    )
+    lane = iota((SUBLANES, LANES), 1)
+    half = LANES // 2
+    moved = jnp.where(
+        lane < half + owned,
+        pltpu.roll(wide[:SUBLANES], half, 1),
+        pltpu.roll(wide[SUBLANES:], half + owned, 1),
+    )
+    return jnp.concatenate(rows + rows, axis=0) + jnp.where(lane < half, 0.0, moved)
+
+
+def prepare_kernel(owner, slot, traces, foot, starts, windows, compact, corr, piece):
     blocks, voxels = foot.shape
     tiles = voxels // LANES
     acc = jnp.zeros((blocks, LANES), BF16)
@@ -75,25 +109,25 @@
     ]
     terms = [two_terms(r) for r in rows]
     part = jnp.concatenate([t[0] for t in terms] + [t[1] for t in terms], axis=0)
-    whole = (base[...] + part).astype(BF16)
+    whole = (label_rows(owner, slot, traces) + part).astype(BF16)
     piece[...] = jnp.broadcast_to(whole[None], piece.shape)
 
 
-def prepare(base, footprints, owners):
+def prepare(owner, slot, traces, footprints, owners):
     blocks, _ = footprints.shape
     return pl.pallas_call(
         prepare_kernel,
-        in_specs=[VMEM, VMEM],
+        in_specs=[VMEM] * 4,
         out_specs=[SMEM, VMEM, VMEM, VMEM, VMEM],
         out_shape=[
-            jax.ShapeDtypeStruct((blocks,), jnp.int32),
-            jax.ShapeDtypeStruct((blocks, blocks, LANES), BF16),
-            jax.ShapeDtypeStruct((blocks, LANES), F32),
-            jax.ShapeDtypeStruct((blocks, LANES), F32),
-            jax.ShapeDtypeStruct((owners, SUBLANES, LANES), BF16),
+            pltpu.SMEM((blocks,), jnp.int32),
+            pltpu.VMEM((blocks, blocks, LANES), BF16),
+            pltpu.VMEM((blocks, LANES), F32),
+            pltpu.VMEM((blocks, LANES), F32),
+            pltpu.VMEM((owners, SUBLANES, LANES), BF16),
         ],
         name="prepare",
-    )(base, footprints)
+    )(owner, slot, traces, footprints)
 
 
 def flux_of(difference):
@@ -147,7 +181,7 @@
 
 def denoise_kernel(starts, rec, low, high, compact, voxel_windows, projected, field):
     frames, planes, rows, _ = rec.shape
-    width = low.shape[1]
+    width = 3
     position = lax.axis_index("bricks")
     low_keep = jnp.where(position > 0, 1.0, 0.0)
     high_keep = jnp.where(position < lax.axis_size("bricks") - 1, 1.0, 0.0)
@@ -156,7 +190,7 @@
     masks = (row == 0, row == SUBLANES - 1, col == 0, col == LANES - 1)
 
     def one_frame(f, carry):
-        u = [quarters(low[f, i]) for i in range(width)]
+        u = [quarters(low[f, planes - width + i]) for i in range(width)]
         u = u + [quarters(rec[f, i]) for i in range(planes)]
         u = u + [quarters(high[f, i]) for i in range(width)]
         for sweep in range(width):
@@ -199,22 +233,29 @@
         in_specs=[SMEM, VMEM, VMEM, VMEM, VMEM],
         out_specs=[VMEM, VMEM],
         out_shape=[
-            jax.ShapeDtypeStruct((blocks, frames, LANES), F32),
-            jax.ShapeDtypeStruct((frames, LANES), F32),
+            pltpu.VMEM((blocks, frames, LANES), F32),
+            pltpu.VMEM((frames, LANES), F32),
         ],
         scratch_shapes=[pltpu.VMEM((2, frames * planes * rows, LANES), F32)],
         name="denoise",
-    )(starts, recording, low, high, compact)
-
-
-def combine_kernel(prior, labels, projected, corr, piece, slot_prior):
+    )(near_scalar(starts), recording, near(low), near(high), near(compact))
+
+
+def as_column(line):
+    count = line.shape[1]
+    square = (count, count)
+    same = iota(square, 0) == iota(square, 1)
+    return jnp.sum(jnp.where(same, line, 0), axis=1, keepdims=True)
+
+
+def combine_kernel(prior, owner, slot, projected, corr, piece, slot_prior):
     owners = prior.shape[0]
     blocks = corr.shape[0]
     frames = projected.shape[0]
     span = owners * SUBLANES
     flat = prior[...].astype(F32).reshape(span, LANES).astype(BF16)
-    owner = labels[:, 0:1]
-    slot = labels[:, 1:2]
+    owner = as_column(owner[...])
+    slot = as_column(slot[...])
     source = iota((blocks, span), 1)
     pick = jnp.concatenate(
         [onehot(source == owner * SUBLANES + i) for i in range(SUBLANES)], axis=0
@@ -228,7 +269,7 @@
     ]
     wide = SUBLANES * LANES
     here = iota((wide, LANES), 0)
-    frame_of = (here // LANES) * 2 + (here % LANES - LANES // 2) // blocks
+    frame_of = here // LANES + (here % LANES - LANES // 2) // blocks * SUBLANES
     frame_of = jnp.where(here % LANES >= LANES // 2, frame_of, -1)
     spread = onehot(frame_of == iota((wide, LANES), 1) % frames)
     earlier = jnp.dot(jnp.concatenate(parts, axis=1), spread, preferred_element_type=F32)
@@ -257,21 +298,23 @@
     piece[...] = jnp.broadcast_to(whole[None], piece.shape)
 
 
-def combine(prior, labels, projected, corr):
+def combine(prior, owner, slot, projected, corr):
     blocks = corr.shape[0]
     return pl.pallas_call(
         combine_kernel,
-        in_specs=[VMEM, VMEM, VMEM, VMEM],
+        in_specs=[VMEM] * 5,
         out_specs=[VMEM, VMEM],
         out_shape=[
-            jax.ShapeDtypeStruct(prior.shape, BF16),
-            jax.ShapeDtypeStruct((blocks, LANES), F32),
+            pltpu.VMEM(prior.shape, BF16),
+            pltpu.VMEM((blocks, LANES), F32),
         ],
         name="combine",
-    )(prior, labels, projected, corr)
-
-
-def update_kernel(prior, gathered, labels, traces, slot_prior, voxel_windows, traces_new, sent):
+    )(near(prior), owner, slot, near(projected), near(corr))
+
+
+def update_kernel(
+    prior, gathered, owner, slot, traces, slot_prior, voxel_windows, traces_new, sent
+):
     owners = prior.shape[0]
     blocks = slot_prior.shape[0]
     frames, owned = traces.shape
@@ -286,7 +329,7 @@
     comps = lists[:SUBLANES] * float(owned) + lists[SUBLANES : 2 * SUBLANES]
     diags = lists[2 * SUBLANES : 3 * SUBLANES]
     position = lax.axis_index("bricks")
-    asked = labels[:, 0:1] * owned + labels[:, 1:2]
+    asked = as_column(owner[...] * owned + slot[...])
     held = position * owned + iota((owned, 1), 0)
     target = jnp.concatenate([asked, held], axis=0).astype(F32)
     count = blocks + owned
@@ -330,18 +373,18 @@
         sent[g, blocks : blocks + SUBLANES, :] = packed
 
 
-def update(prior, gathered, labels, traces, slot_prior, voxel_windows, groups):
+def update(prior, gathered, owner, slot, traces, slot_prior, voxel_windows, groups):
     blocks = slot_prior.shape[0]
     return pl.pallas_call(
         update_kernel,
-        in_specs=[VMEM] * 6,
+        in_specs=[VMEM] * 7,
         out_specs=[VMEM, VMEM],
         out_shape=[
             jax.ShapeDtypeStruct(traces.shape, F32),
-            jax.ShapeDtypeStruct((groups, blocks + SUBLANES, LANES), F32),
+            pltpu.VMEM((groups, blocks + SUBLANES, LANES), F32),
         ],
         name="update",
-    )(prior, gathered, labels, traces, slot_prior, voxel_windows)
+    )(near(prior), near(gathered), owner, slot, traces, near(slot_prior), near(voxel_windows))
 
 
 def finish_kernel(starts, shared, windows, compact, out):
@@ -384,42 +427,31 @@
         out_specs=VMEM,
         out_shape=jax.ShapeDtypeStruct((blocks, voxels), BF16),
         name="finish",
-    )(starts, shared, windows, compact)
-
-
-def halo_planes(recording, width):
+    )(near_scalar(starts), near(shared), near(windows), near(compact))
+
+
+def halo_planes(recording):
     count = lax.axis_size("bricks")
-    planes = recording.shape[1]
-    tail = lax.slice_in_dim(recording, planes - width, planes, axis=1)
-    head = lax.slice_in_dim(recording, 0, width, axis=1)
-    low = lax.ppermute(tail, "bricks", [(i, i + 1) for i in range(count - 1)])
-    high = lax.ppermute(head, "bricks", [(i + 1, i) for i in range(count - 1)])
+    low = lax.ppermute(recording, "bricks", [(i, i + 1) for i in range(count - 1)])
+    high = lax.ppermute(recording, "bricks", [(i + 1, i) for i in range(count - 1)])
     return low, high
-
-
-def label_piece(traces, labels):
-    blocks = labels.shape[0]
-    lists = labels.T.reshape(2, blocks // SUBLANES, SUBLANES).astype(F32)
-    lists = jnp.concatenate([lists, lists], axis=1)
-    gap = jnp.zeros((SUBLANES, LANES // 2 - 2 * SUBLANES), F32)
-    return jnp.concatenate(
-        [lists[0], lists[1], gap, traces.astype(F32).reshape(SUBLANES, -1)], axis=1
-    )
 
 
 def shards(recording, traces, footprints, block_owner, block_slot):
     voxels = footprints.shape[1]
     owners = lax.axis_size("bricks")
     groups = lax.axis_size("frames")
-    low, high = halo_planes(recording, 3)
-    labels = jnp.concatenate([block_owner, block_slot[:, None]], axis=1)
-    base = label_piece(traces, labels)
-    starts, windows, compact, corr, piece = prepare(base, footprints, owners)
+    low, high = halo_planes(recording)
+    owner = block_owner.T
+    slot = block_slot[None, :]
+    starts, windows, compact, corr, piece = prepare(owner, slot, traces, footprints, owners)
     prior = lax.all_to_all(piece, "bricks", 0, 0)
     voxel_windows, projected = denoise_windows(starts, recording, low, high, compact)
-    partials, slot_prior = combine(prior, labels, projected, corr)
+    partials, slot_prior = combine(prior, owner, slot, projected, corr)
     gathered = lax.all_to_all(partials, "bricks", 0, 0)
-    traces_new, sent = update(prior, gathered, labels, traces, slot_prior, voxel_windows, groups)
+    traces_new, sent = update(
+        prior, gathered, owner, slot, traces, slot_prior, voxel_windows, groups
+    )
     shared = lax.all_to_all(sent, "frames", 0, 0)
     footprints_new = finish(starts, shared, windows, compact, voxels)
     return (traces_new, footprints_new)

time: 85.2 us -> 76.1 us (0.89)
  local copies, waits for them, and re-layouts: 4.35 us -> 0 us
  Pallas kernels: 20.6 us -> 17.4 us
  blocking collectives: 37 us -> 34.7 us
  waiting for transfers between devices: 0.01 us -> 1.77 us
    unnamed x12 -> x0, local copies, waits for them, and re-layouts: 2.22 us -> none
    all_to_all x1, blocking collectives: 21.5 us -> 19.4 us  [shards(): gathered = lax.all_to_all(partials, 'bricks', 0, 0)]
    all_to_all x1, waiting for transfers between devices: 0.01 us -> 1.77 us  [shards(): prior = lax.all_to_all(piece, 'bricks', 0, 0)]
    pallas_call x3, Pallas kernels: 7.68 us -> 6.31 us  [the longest x1 2.8 us: prepare(): pl.pallas_call(prepare_kernel, in_specs=[VMEM] * 4, out_specs=[SMEM, VMEM...]
    slice x1 -> x0, local copies, waits for them, and re-layouts: 1.21 us -> none  [halo_planes(): head = lax.slice_in_dim(recording, 0, width, axis=1)]
    pallas_call x1, Pallas kernels: 2.78 us -> 1.8 us  [finish(): pl.pallas_call(finish_kernel, in_specs=[SMEM, VMEM, VMEM, VMEM], out_spec...]
    pallas_call x1, Pallas kernels: 10.2 us -> 9.3 us  [denoise_windows(): pl.pallas_call(denoise_kernel, in_specs=[SMEM, VMEM, VMEM, VMEM, VMEM], o...]
  transfers between devices with their start and end apart: 3 -> 3, of which waited for: 0 -> 1; matrix products, arithmetic and copies ran while one was open for 2% -> 0% of each run, Pallas kernels for 15% -> 16%
where the time goes in v3:
time: 76.1 us; the launch traced here: 75.7 us
  blocking collectives  34.7 us (46%)
  starting transfers between devices  21.2 us (28%)
  Pallas kernels  17.4 us (23%)
  waiting for transfers between devices  1.77 us (2%)
    all_to_all x1, blocking collectives, shards(): gathered = lax.all_to_all(partials, 'bricks', 0, 0)  19.4 us
    all_to_all x1, blocking collectives, shards(): shared = lax.all_to_all(sent, 'frames', 0, 0)  15.2 us
    all_to_all x1, starting transfers between devices, shards(): prior = lax.all_to_all(piece, 'bricks', 0, 0)  11.1 us
    pallas_call x1, Pallas kernels, denoise_windows(): pl.pallas_call(denoise_kernel, in_specs=[SMEM, VMEM, VMEM, VMEM, VMEM], o...  9.3 us
    ppermute x1, starting transfers between devices, halo_planes(): lax.ppermute(recording, 'bricks', [(i + 1, i) for i in range(count - 1)])  5.57 us
    ppermute x1, starting transfers between devices, halo_planes(): lax.ppermute(recording, 'bricks', [(i, i + 1) for i in range(count - 1)])  4.5 us
    pallas_call x1, Pallas kernels, prepare(): pl.pallas_call(prepare_kernel, in_specs=[VMEM] * 4, out_specs=[SMEM, VMEM...  2.8 us
    pallas_call x1, Pallas kernels, update(): pl.pallas_call(update_kernel, in_specs=[VMEM] * 7, out_specs=[VMEM, VMEM]...  2.2 us
  transfers between devices with their start and end apart: 3, of which 1 were waited for; matrix products, arithmetic and copies ran while one was open for 0% of the time, Pallas kernels for 16%

profile of v3, /device:TPU:1, one launch (start us, length us, event | category | flops | bytes accessed | tf_op | source)
XLA Modules:
  0.0 75.7 jit_solution(10422554670038140558)
XLA Ops:
  0.6 4.5 %collective-permute-start = (bf16[16,4,16,256]{3,2,1,0:T(8,128)(2,1)}, bf16[16,4,16,256]{3,2,1,0:T(8,128)(2,1)S(1)}, u32[]{:S(2)}, u32[]{:S(2)}) collective-permute-start(bf16[16,4,16,256]{3,2,1,0:T(8,128)(2,1)} %rec.1), channel_id=1, source_target_pairs={{0,1},{1,2},{2,3},{3,4},{4,5},{5,6},{6,7},{7,8},{8,9},{9,10},{10,1... | collective-permute-start | bytes 1572872 | tf_op jit(solution)/shard_map/ppermute | solution.py:435
  5.1 5.6 %collective-permute-start.1 = (bf16[16,4,16,256]{3,2,1,0:T(8,128)(2,1)}, bf16[16,4,16,256]{3,2,1,0:T(8,128)(2,1)S(1)}, u32[]{:S(2)}, u32[]{:S(2)}) collective-permute-start(bf16[16,4,16,256]{3,2,1,0:T(8,128)(2,1)} %rec.1), channel_id=1, source_target_pairs={{1,0},{2,1},{3,2},{4,3},{5,4},{6,5},{7,6},{8,7},{9,8},{10,9},{11,1... | collective-permute-start | bytes 1572872 | tf_op jit(solution)/shard_map/ppermute | solution.py:436
  10.7 2.8 %prepare.1 = (s32[32]{0:T(128)S(4)}, bf16[32,32,128]{2,1,0:T(8,128)(2,1)S(1)}, f32[32,128]{1,0:T(8,128)S(1)}, f32[32,128]{1,0:T(8,128)S(1)}, bf16[64,8,128]{2,1,0:T(8,128)(2,1)}) custom-call(s32[1,32]{1,0:T(1,128)} %bitcast.2, s32[1,32]{1,0:T(1,128)} %bitcast.5, bf16[16,32]{1,0:T(8,128)(2,1)} %traces.3, bf16[32,16384]{1,0:T(8,128)(2,1)} %foot.1), custom_call_target="tpu_custom_call" | custom-call | tf_op jit(solution)/shard_map/prepare/pallas_call | solution.py:118
  13.5 11.1 %all-to-all-start = ((bf16[64,8,128]{2,1,0:T(8,128)(2,1)}), bf16[64,8,128]{2,1,0:T(8,128)(2,1)S(1)}, u32[]{:S(2)}, u32[]{:S(2)}) async-start(bf16[64,8,128]{2,1,0:T(8,128)(2,1)} %get-tuple-element.13), calls=%async_computation | async-start | bytes 262144 | tf_op jit(solution)/shard_map/all_to_all | solution.py:448
  24.7 0.0 collective-permute-done.low
  24.7 0.0 collective-permute-done.1.high
  24.7 9.3 %denoise.1 = (f32[32,16,128]{2,1,0:T(8,128)S(1)}, f32[16,128]{1,0:T(8,128)S(1)}) custom-call(s32[32]{0:T(128)S(4)} %get-tuple-element.14.starts, bf16[16,4,16,256]{3,2,1,0:T(8,128)(2,1)} %rec.1, bf16[16,4,16,256]{3,2,1,0:T(8,128)(2,1)S(1)} %collective-permute-done.low, bf16[16,4,16,256]{3,2,1,0:T(8,128)(2,1)S(1)} %collective-permute-done.1.high, ...), custom_call_target="tpu_custom_call" | custom-call | tf_op jit(solution)/shard_map/denoise/pallas_call | solution.py:231
  34.0 1.8 %all-to-all-done.prior = bf16[64,8,128]{2,1,0:T(8,128)(2,1)S(1)} async-done(((bf16[64,8,128]{2,1,0:T(8,128)(2,1)}), bf16[64,8,128]{2,1,0:T(8,128)(2,1)S(1)}, u32[]{:S(2)}, u32[]{:S(2)}) %all-to-all-start) | async-done | bytes 131104 | tf_op jit(solution)/shard_map/all_to_all | solution.py:448
  35.8 1.3 %combine.1 = (bf16[64,8,128]{2,1,0:T(8,128)(2,1)S(1)}, f32[32,128]{1,0:T(8,128)S(1)}) custom-call(bf16[64,8,128]{2,1,0:T(8,128)(2,1)S(1)} %all-to-all-done.prior, s32[1,32]{1,0:T(1,128)} %bitcast.3, s32[1,32]{1,0:T(1,128)} %bitcast.6, f32[16,128]{1,0:T(8,128)S(1)} %get-tuple-element.16.projected, f32[32,128]{1,0:T(8,128)S(1)} %get-tuple-element.17.corr), custom_call_target="tpu_custom_call" | custom-call | tf_op jit(solution)/shard_map/combine/pallas_call | solution.py:303
  37.1 19.4 %all_to_all.15.gathered = bf16[64,8,128]{2,1,0:T(8,128)(2,1)S(1)} all-to-all(bf16[64,8,128]{2,1,0:T(8,128)(2,1)S(1)} %get-tuple-element.18), channel_id=1, replica_groups=mesh['frames'=8,'bricks'=64] {'bricks'}, dimensions={0} | all-to-all | bytes 262144 | tf_op jit(solution)/shard_map/all_to_all | solution.py:451
  56.5 2.2 %update.1 = (f32[16,32]{1,0:T(8,128)}, f32[8,40,128]{2,1,0:T(8,128)S(1)}) custom-call(bf16[64,8,128]{2,1,0:T(8,128)(2,1)S(1)} %all-to-all-done.prior, bf16[64,8,128]{2,1,0:T(8,128)(2,1)S(1)} %all_to_all.15.gathered, s32[1,32]{1,0:T(1,128)} %bitcast.4, s32[1,32]{1,0:T(1,128)} %bitcast.7, bf16[16,32]{1,0:T(8,128)(2,1)} %traces.3, ...), custom_call_target="tpu_custom_call" | custom-call | tf_op jit(solution)/shard_map/update/pallas_call | solution.py:378
  58.7 15.2 %all_to_all.16.shared = f32[8,40,128]{2,1,0:T(8,128)S(1)} all-to-all(f32[8,40,128]{2,1,0:T(8,128)S(1)} %get-tuple-element.22), channel_id=1, replica_groups=mesh['frames'=8,'bricks'=64] {'frames'}, dimensions={0} | all-to-all | bytes 327680 | tf_op jit(solution)/shard_map/all_to_all | solution.py:455
  73.9 1.8 %finish.1 = bf16[32,16384]{1,0:T(8,128)(2,1)} custom-call(s32[32]{0:T(128)S(4)} %get-tuple-element.14.starts, f32[8,40,128]{2,1,0:T(8,128)S(1)} %all_to_all.16.shared, bf16[32,32,128]{2,1,0:T(8,128)(2,1)S(1)} %get-tuple-element.23.windows, f32[32,128]{1,0:T(8,128)S(1)} %get-tuple-element.15.compact), custom_call_target="tpu_custom_call" | custom-call | tf_op jit(solution)/shard_map/finish/pallas_call | solution.py:424
Async XLA Ops:
  0.6 24.0 %collective-permute-start = (bf16[16,4,16,256]{3,2,1,0:T(8,128)(2,1)}, bf16[16,4,16,256]{3,2,1,0:T(8,128)(2,1)S(1)}, u32[]{:S(2)}, u32[]{:S(2)}) collective-permute-start(bf16[16,4,16,256]{3,2,1,0:T(8,128)(2,1)} %rec.1), channel_id=1, source_target_pairs={{0,1},{1,2},{2,3},{3,4},{4,5},{5,6},{6,7},{7,8},{8,9},{9,10},{10,1... | collective-permute-start | bytes 1572872 | tf_op jit(solution)/shard_map/ppermute | solution.py:435
  5.1 19.6 %collective-permute-start.1 = (bf16[16,4,16,256]{3,2,1,0:T(8,128)(2,1)}, bf16[16,4,16,256]{3,2,1,0:T(8,128)(2,1)S(1)}, u32[]{:S(2)}, u32[]{:S(2)}) collective-permute-start(bf16[16,4,16,256]{3,2,1,0:T(8,128)(2,1)} %rec.1), channel_id=1, source_target_pairs={{1,0},{2,1},{3,2},{4,3},{5,4},{6,5},{7,6},{8,7},{9,8},{10,9},{11,1... | collective-permute-start | bytes 1572872 | tf_op jit(solution)/shard_map/ppermute | solution.py:436
  13.5 22.2 %all-to-all-start = ((bf16[64,8,128]{2,1,0:T(8,128)(2,1)}), bf16[64,8,128]{2,1,0:T(8,128)(2,1)S(1)}, u32[]{:S(2)}, u32[]{:S(2)}) async-start(bf16[64,8,128]{2,1,0:T(8,128)(2,1)} %get-tuple-element.13), calls=%async_computation | async-start | bytes 262144 | tf_op jit(solution)/shard_map/all_to_all | solution.py:448

commit v4 on v3

--- a/solution.py
+++ b/solution.py
@@ -14,6 +14,7 @@
 BF16 = jnp.bfloat16
 VMEM = pl.BlockSpec(memory_space=pltpu.VMEM)
 SMEM = pl.BlockSpec(memory_space=pltpu.SMEM)
+PARAMS = pltpu.CompilerParams(vmem_limit_bytes=16 * 2**20)
 
 
 def near(array):
@@ -126,8 +127,9 @@
             pltpu.VMEM((blocks, LANES), F32),
             pltpu.VMEM((owners, SUBLANES, LANES), BF16),
         ],
+        compiler_params=PARAMS,
         name="prepare",
-    )(owner, slot, traces, footprints)
+    )(near(owner), near(slot), near(traces), near(footprints))
 
 
 def flux_of(difference):
@@ -237,8 +239,9 @@
             pltpu.VMEM((frames, LANES), F32),
         ],
         scratch_shapes=[pltpu.VMEM((2, frames * planes * rows, LANES), F32)],
+        compiler_params=PARAMS,
         name="denoise",
-    )(near_scalar(starts), recording, near(low), near(high), near(compact))
+    )(near_scalar(starts), near(recording), near(low), near(high), near(compact))
 
 
 def as_column(line):
@@ -308,8 +311,9 @@
             pltpu.VMEM(prior.shape, BF16),
             pltpu.VMEM((blocks, LANES), F32),
         ],
+        compiler_params=PARAMS,
         name="combine",
-    )(near(prior), owner, slot, near(projected), near(corr))
+    )(near(prior), near(owner), near(slot), near(projected), near(corr))
 
 
 def update_kernel(
@@ -380,14 +384,24 @@
         in_specs=[VMEM] * 7,
         out_specs=[VMEM, VMEM],
         out_shape=[
-            jax.ShapeDtypeStruct(traces.shape, F32),
+            pltpu.VMEM(traces.shape, F32),
             pltpu.VMEM((groups, blocks + SUBLANES, LANES), F32),
         ],
+        compiler_params=PARAMS,
         name="update",
-    )(near(prior), near(gathered), owner, slot, traces, near(slot_prior), near(voxel_windows))
-
-
-def finish_kernel(starts, shared, windows, compact, out):
+    )(
+        near(prior),
+        near(gathered),
+        near(owner),
+        near(slot),
+        near(traces),
+        near(slot_prior),
+        near(voxel_windows),
+    )
+
+
+def finish_kernel(starts, shared, windows, compact, fresh, out, traces_new):
+    traces_new[...] = fresh[...]
     blocks, voxels = out.shape
     tiles = voxels // LANES
     groups = shared.shape[0]
@@ -419,15 +433,19 @@
             out[:, at] = jnp.where((row == k) & part, stepped, old).astype(out.dtype)
 
 
-def finish(starts, shared, windows, compact, voxels):
+def finish(starts, shared, windows, compact, fresh, voxels):
     blocks = windows.shape[0]
     return pl.pallas_call(
         finish_kernel,
-        in_specs=[SMEM, VMEM, VMEM, VMEM],
-        out_specs=VMEM,
-        out_shape=jax.ShapeDtypeStruct((blocks, voxels), BF16),
+        in_specs=[SMEM, VMEM, VMEM, VMEM, VMEM],
+        out_specs=[VMEM, VMEM],
+        out_shape=[
+            jax.ShapeDtypeStruct((blocks, voxels), BF16),
+            jax.ShapeDtypeStruct(fresh.shape, fresh.dtype),
+        ],
+        compiler_params=PARAMS,
         name="finish",
-    )(near_scalar(starts), near(shared), near(windows), near(compact))
+    )(near_scalar(starts), near(shared), near(windows), near(compact), near(fresh))
 
 
 def halo_planes(recording):
@@ -449,11 +467,9 @@
     voxel_windows, projected = denoise_windows(starts, recording, low, high, compact)
     partials, slot_prior = combine(prior, owner, slot, projected, corr)
     gathered = lax.all_to_all(partials, "bricks", 0, 0)
-    traces_new, sent = update(
-        prior, gathered, owner, slot, traces, slot_prior, voxel_windows, groups
-    )
+    fresh, sent = update(prior, gathered, owner, slot, traces, slot_prior, voxel_windows, groups)
     shared = lax.all_to_all(sent, "frames", 0, 0)
-    footprints_new = finish(starts, shared, windows, compact, voxels)
+    footprints_new, traces_new = finish(starts, shared, windows, compact, fresh, voxels)
     return (traces_new, footprints_new)
 
 

time: 76.1 us -> 74.5 us (0.979)
  Pallas kernels: 17.4 us -> 13.2 us
  local copies, waits for them, and re-layouts: 0 us -> 2.58 us
  blocking collectives: 34.7 us -> 33.6 us
  waiting for transfers between devices: 1.77 us -> 2.8 us
    unnamed x0 -> x12, local copies, waits for them, and re-layouts: none -> 2.58 us
    pallas_call x1, Pallas kernels: 2.8 us -> 1.53 us  [prepare(): pl.pallas_call(prepare_kernel, in_specs=[VMEM] * 4, out_specs=[SMEM, VMEM...]
    pallas_call x1, Pallas kernels: 2.2 us -> 0.97 us  [update(): pl.pallas_call(update_kernel, in_specs=[VMEM] * 7, out_specs=[VMEM, VMEM]...]
    pallas_call x1, Pallas kernels: 9.3 us -> 8.27 us  [denoise_windows(): pl.pallas_call(denoise_kernel, in_specs=[SMEM, VMEM, VMEM, VMEM, VMEM], o...]
    all_to_all x1, blocking collectives: 19.4 us -> 18.4 us  [shards(): gathered = lax.all_to_all(partials, 'bricks', 0, 0)]
    all_to_all x1, waiting for transfers between devices: 1.77 us -> 2.79 us  [shards(): prior = lax.all_to_all(piece, 'bricks', 0, 0)]
  transfers between devices with their start and end apart: 3 -> 3, of which waited for: 1 -> 1; matrix products, arithmetic and copies ran while one was open for 0% -> 0% of each run, Pallas kernels for 16% -> 13%
where the time goes in v4:
time: 74.5 us; the launch traced here: 74.1 us
  blocking collectives  33.6 us (45%)
  starting transfers between devices  21.2 us (28%)
  Pallas kernels  13.2 us (18%)
  waiting for transfers between devices  2.8 us (4%)
  local copies, waits for them, and re-layouts  2.58 us (3%)
    all_to_all x1, blocking collectives, shards(): gathered = lax.all_to_all(partials, 'bricks', 0, 0)  18.4 us
    all_to_all x1, blocking collectives, shards(): shared = lax.all_to_all(sent, 'frames', 0, 0)  15.2 us
    all_to_all x1, starting transfers between devices, shards(): prior = lax.all_to_all(piece, 'bricks', 0, 0)  11.1 us
    pallas_call x1, Pallas kernels, denoise_windows(): pl.pallas_call(denoise_kernel, in_specs=[SMEM, VMEM, VMEM, VMEM, VMEM], o...  8.27 us
    ppermute x1, starting transfers between devices, halo_planes(): lax.ppermute(recording, 'bricks', [(i + 1, i) for i in range(count - 1)])  5.57 us
    ppermute x1, starting transfers between devices, halo_planes(): lax.ppermute(recording, 'bricks', [(i, i + 1) for i in range(count - 1)])  4.5 us
    all_to_all x1, waiting for transfers between devices, shards(): prior = lax.all_to_all(piece, 'bricks', 0, 0)  2.79 us
    unnamed x12, local copies, waits for them, and re-layouts  2.58 us
  transfers between devices with their start and end apart: 3, of which 1 were waited for; matrix products, arithmetic and copies ran while one was open for 0% of the time, Pallas kernels for 13%

profile of v4, /device:TPU:1, one launch (start us, length us, event | category | flops | bytes accessed | tf_op | source)
XLA Modules:
  0.0 74.1 jit_solution(14603701614097442849)
XLA Ops:
  0.6 4.5 %collective-permute-start = (bf16[16,4,16,256]{3,2,1,0:T(8,128)(2,1)}, bf16[16,4,16,256]{3,2,1,0:T(8,128)(2,1)S(1)}, u32[]{:S(2)}, u32[]{:S(2)}) collective-permute-start(bf16[16,4,16,256]{3,2,1,0:T(8,128)(2,1)} %rec.1), channel_id=1, source_target_pairs={{0,1},{1,2},{2,3},{3,4},{4,5},{5,6},{6,7},{7,8},{8,9},{9,10},{10,1... | collective-permute-start | bytes 1572872 | tf_op jit(solution)/shard_map/ppermute | solution.py:453
  5.1 5.6 %collective-permute-start.1 = (bf16[16,4,16,256]{3,2,1,0:T(8,128)(2,1)}, bf16[16,4,16,256]{3,2,1,0:T(8,128)(2,1)S(1)}, u32[]{:S(2)}, u32[]{:S(2)}) collective-permute-start(bf16[16,4,16,256]{3,2,1,0:T(8,128)(2,1)} %rec.1), channel_id=1, source_target_pairs={{1,0},{2,1},{3,2},{4,3},{5,4},{6,5},{7,6},{8,7},{9,8},{10,9},{11,1... | collective-permute-start | bytes 1572872 | tf_op jit(solution)/shard_map/ppermute | solution.py:454
  10.7 0.0 copy-start.4
  10.7 0.0 copy-start.5
  10.7 0.6 copy-done.4
  11.4 0.0 copy-done.5
  11.4 0.0 copy-start
  11.4 1.2 %copy-done = bf16[32,16384]{1,0:T(8,128)(2,1)S(1)} copy-done((bf16[32,16384]{1,0:T(8,128)(2,1)S(1)}, bf16[32,16384]{1,0:T(8,128)(2,1)}, u32[]{:S(2)}) %copy-start) | copy-done | bytes 1048600
  12.6 0.0 copy-start.2
  12.6 0.7 copy-done.2
  13.3 1.5 %prepare.1 = (s32[32]{0:T(128)S(4)}, bf16[32,32,128]{2,1,0:T(8,128)(2,1)S(1)}, f32[32,128]{1,0:T(8,128)S(1)}, f32[32,128]{1,0:T(8,128)S(1)}, bf16[64,8,128]{2,1,0:T(8,128)(2,1)}) custom-call(s32[1,32]{1,0:T(1,128)S(1)} %bitcast.2, s32[1,32]{1,0:T(1,128)S(1)} %bitcast.5, bf16[16,32]{1,0:T(8,128)(2,1)S(1)} %copy-done.2, bf16[32,16384]{1,0:T(8,128)(2,1)S(1)} %copy-done), custom_call_target="tpu_custom_call" | custom-call | tf_op jit(solution)/shard_map/prepare/pallas_call | solution.py:119
  14.8 11.1 %all-to-all-start = ((bf16[64,8,128]{2,1,0:T(8,128)(2,1)}), bf16[64,8,128]{2,1,0:T(8,128)(2,1)S(1)}, u32[]{:S(2)}, u32[]{:S(2)}) async-start(bf16[64,8,128]{2,1,0:T(8,128)(2,1)} %get-tuple-element.16), calls=%async_computation | async-start | bytes 262144 | tf_op jit(solution)/shard_map/all_to_all | solution.py:466
  26.0 0.0 collective-permute-done.low
  26.0 0.0 collective-permute-done.1.high
  26.0 0.0 copy-done.1
  26.0 8.3 %denoise.1 = (f32[32,16,128]{2,1,0:T(8,128)S(1)}, f32[16,128]{1,0:T(8,128)S(1)}) custom-call(s32[32]{0:T(128)S(4)} %get-tuple-element.15.starts, bf16[16,4,16,256]{3,2,1,0:T(8,128)(2,1)S(1)} %copy-done.1, bf16[16,4,16,256]{3,2,1,0:T(8,128)(2,1)S(1)} %collective-permute-done.low, bf16[16,4,16,256]{3,2,1,0:T(8,128)(2,1)S(1)} %collective-permute-done.1.high, ...), custom_call_target="tpu_custom_call" | custom-call | tf_op jit(solution)/shard_map/denoise/pallas_call | solution.py:233
  34.3 2.8 %all-to-all-done.prior = bf16[64,8,128]{2,1,0:T(8,128)(2,1)S(1)} async-done(((bf16[64,8,128]{2,1,0:T(8,128)(2,1)}), bf16[64,8,128]{2,1,0:T(8,128)(2,1)S(1)}, u32[]{:S(2)}, u32[]{:S(2)}) %all-to-all-start) | async-done | bytes 131104 | tf_op jit(solution)/shard_map/all_to_all | solution.py:466
  37.1 0.6 combine.1
  37.7 0.0 copy-start.3
  37.7 18.4 %all_to_all.15.gathered = bf16[64,8,128]{2,1,0:T(8,128)(2,1)S(1)} all-to-all(bf16[64,8,128]{2,1,0:T(8,128)(2,1)S(1)} %get-tuple-element.20), channel_id=1, replica_groups=mesh['frames'=8,'bricks'=64] {'bricks'}, dimensions={0} | all-to-all | bytes 262144 | tf_op jit(solution)/shard_map/all_to_all | solution.py:469
  56.1 0.0 copy-done.3
  56.1 1.0 %update.1 = (f32[16,32]{1,0:T(8,128)S(1)}, f32[8,40,128]{2,1,0:T(8,128)S(1)}) custom-call(bf16[64,8,128]{2,1,0:T(8,128)(2,1)S(1)} %all-to-all-done.prior, bf16[64,8,128]{2,1,0:T(8,128)(2,1)S(1)} %all_to_all.15.gathered, s32[1,32]{1,0:T(1,128)S(1)} %bitcast.4, s32[1,32]{1,0:T(1,128)S(1)} %bitcast.7, bf16[16,32]{1,0:T(8,128)(2,1)S(1)} %copy-done.3, ...), custom_call_target="tpu_custom_call" | custom-call | tf_op jit(solution)/shard_map/update/pallas_call | solution.py:382
  57.1 15.2 %all_to_all.16.shared = f32[8,40,128]{2,1,0:T(8,128)S(1)} all-to-all(f32[8,40,128]{2,1,0:T(8,128)S(1)} %get-tuple-element.23), channel_id=1, replica_groups=mesh['frames'=8,'bricks'=64] {'frames'}, dimensions={0} | all-to-all | bytes 327680 | tf_op jit(solution)/shard_map/all_to_all | solution.py:471
  72.3 1.8 %finish.1 = (bf16[32,16384]{1,0:T(8,128)(2,1)}, f32[16,32]{1,0:T(8,128)}) custom-call(s32[32]{0:T(128)S(4)} %get-tuple-element.15.starts, f32[8,40,128]{2,1,0:T(8,128)S(1)} %all_to_all.16.shared, bf16[32,32,128]{2,1,0:T(8,128)(2,1)S(1)} %get-tuple-element.24.windows, f32[32,128]{1,0:T(8,128)S(1)} %get-tuple-element.17.compact, ...), custom_call_target="tpu_custom_call" | custom-call | tf_op jit(solution)/shard_map/finish/pallas_call | solution.py:438
  (1 shorter events, 0.0 us)
Async XLA Ops:
  0.6 25.4 %collective-permute-start = (bf16[16,4,16,256]{3,2,1,0:T(8,128)(2,1)}, bf16[16,4,16,256]{3,2,1,0:T(8,128)(2,1)S(1)}, u32[]{:S(2)}, u32[]{:S(2)}) collective-permute-start(bf16[16,4,16,256]{3,2,1,0:T(8,128)(2,1)} %rec.1), channel_id=1, source_target_pairs={{0,1},{1,2},{2,3},{3,4},{4,5},{5,6},{6,7},{7,8},{8,9},{9,10},{10,1... | collective-permute-start | bytes 1572872 | tf_op jit(solution)/shard_map/ppermute | solution.py:453
  5.1 20.9 %collective-permute-start.1 = (bf16[16,4,16,256]{3,2,1,0:T(8,128)(2,1)}, bf16[16,4,16,256]{3,2,1,0:T(8,128)(2,1)S(1)}, u32[]{:S(2)}, u32[]{:S(2)}) collective-permute-start(bf16[16,4,16,256]{3,2,1,0:T(8,128)(2,1)} %rec.1), channel_id=1, source_target_pairs={{1,0},{2,1},{3,2},{4,3},{5,4},{6,5},{7,6},{8,7},{9,8},{10,9},{11,1... | collective-permute-start | bytes 1572872 | tf_op jit(solution)/shard_map/ppermute | solution.py:454
  10.7 0.7 copy-start.4
  10.7 0.7 copy-start.5
  11.4 1.2 %copy-start = (bf16[32,16384]{1,0:T(8,128)(2,1)S(1)}, bf16[32,16384]{1,0:T(8,128)(2,1)}, u32[]{:S(2)}) copy-start(bf16[32,16384]{1,0:T(8,128)(2,1)} %foot.1) | copy-start | bytes 3145732
  12.6 0.7 copy-start.2
  13.3 12.7 %copy-start.1 = (bf16[16,4,16,256]{3,2,1,0:T(8,128)(2,1)S(1)}, bf16[16,4,16,256]{3,2,1,0:T(8,128)(2,1)}, u32[]{:S(2)}) copy-start(bf16[16,4,16,256]{3,2,1,0:T(8,128)(2,1)} %rec.1) | copy-start | bytes 1572868
  14.8 22.2 %all-to-all-start = ((bf16[64,8,128]{2,1,0:T(8,128)(2,1)}), bf16[64,8,128]{2,1,0:T(8,128)(2,1)S(1)}, u32[]{:S(2)}, u32[]{:S(2)}) async-start(bf16[64,8,128]{2,1,0:T(8,128)(2,1)} %get-tuple-element.16), calls=%async_computation | async-start | bytes 262144 | tf_op jit(solution)/shard_map/all_to_all | solution.py:466
  37.7 18.4 %copy-start.3 = (bf16[16,32]{1,0:T(8,128)(2,1)S(1)}, bf16[16,32]{1,0:T(8,128)(2,1)}, u32[]{:S(2)}) copy-start(bf16[16,32]{1,0:T(8,128)(2,1)} %traces.3) | copy-start | bytes 3076

commit v5 on v4

--- a/solution.py
+++ b/solution.py
@@ -19,6 +19,10 @@
 
 def near(array):
     return pltpu.with_memory_space_constraint(array, pltpu.VMEM)
+
+
+def far(array):
+    return pltpu.with_memory_space_constraint(array, pltpu.HBM)
 
 
 def near_scalar(array):
@@ -129,7 +133,7 @@
         ],
         compiler_params=PARAMS,
         name="prepare",
-    )(near(owner), near(slot), near(traces), near(footprints))
+    )(far(owner), far(slot), far(traces), far(footprints))
 
 
 def flux_of(difference):
@@ -181,7 +185,7 @@
     return [[cell * keep for cell in line] for line in plane]
 
 
-def denoise_kernel(starts, rec, low, high, compact, voxel_windows, projected, field):
+def denoise_kernel(starts, rec, pair, other, compact, voxel_windows, projected, field):
     frames, planes, rows, _ = rec.shape
     width = 3
     position = lax.axis_index("bricks")
@@ -191,7 +195,7 @@
     col = iota((SUBLANES, LANES), 1)
     masks = (row == 0, row == SUBLANES - 1, col == 0, col == LANES - 1)
 
-    def one_frame(f, carry):
+    def one_frame(f, low, high):
         u = [quarters(low[f, planes - width + i]) for i in range(width)]
         u = u + [quarters(rec[f, i]) for i in range(planes)]
         u = u + [quarters(high[f, i]) for i in range(width)]
@@ -209,9 +213,14 @@
                 for y in range(2):
                     at = pl.multiple_of(f * (planes * rows) + i * rows + z * SUBLANES, SUBLANES)
                     field[y, pl.ds(at, SUBLANES), :] = u[i][z][y].astype(BF16).astype(F32)
-        return carry
-
-    lax.fori_loop(0, frames, one_frame, 0)
+
+    odd = position % 2 == 1
+    for is_odd, low, high in ((True, pair, other), (False, other, pair)):
+
+        @pl.when(odd if is_odd else jnp.logical_not(odd))
+        def _(low=low, high=high):
+            pl.loop(0, frames)(lambda f: one_frame(f, low, high))
+
     blocks = compact.shape[0]
     tiles = planes * rows * 2
     lane = iota((frames, LANES), 1)
@@ -227,7 +236,7 @@
     projected[...] = acc
 
 
-def denoise_windows(starts, recording, low, high, compact):
+def denoise_windows(starts, recording, pair, other, compact):
     frames, planes, rows, _ = recording.shape
     blocks = compact.shape[0]
     return pl.pallas_call(
@@ -241,7 +250,7 @@
         scratch_shapes=[pltpu.VMEM((2, frames * planes * rows, LANES), F32)],
         compiler_params=PARAMS,
         name="denoise",
-    )(near_scalar(starts), near(recording), near(low), near(high), near(compact))
+    )(near_scalar(starts), near(recording), near(pair), near(other), near(compact))
 
 
 def as_column(line):
@@ -448,23 +457,25 @@
     )(near_scalar(starts), near(shared), near(windows), near(compact), near(fresh))
 
 
-def halo_planes(recording):
+def swapped(recording):
     count = lax.axis_size("bricks")
-    low = lax.ppermute(recording, "bricks", [(i, i + 1) for i in range(count - 1)])
-    high = lax.ppermute(recording, "bricks", [(i + 1, i) for i in range(count - 1)])
-    return low, high
+    across = [(i, i + 1) for i in range(1, count - 1, 2)]
+    within = [(i, i + 1) for i in range(0, count, 2)]
+    other = lax.ppermute(recording, "bricks", across + [(b, a) for a, b in across])
+    pair = lax.ppermute(recording, "bricks", within + [(b, a) for a, b in within])
+    return pair, other
 
 
 def shards(recording, traces, footprints, block_owner, block_slot):
     voxels = footprints.shape[1]
     owners = lax.axis_size("bricks")
     groups = lax.axis_size("frames")
-    low, high = halo_planes(recording)
+    pair, other = swapped(recording)
     owner = block_owner.T
     slot = block_slot[None, :]
     starts, windows, compact, corr, piece = prepare(owner, slot, traces, footprints, owners)
     prior = lax.all_to_all(piece, "bricks", 0, 0)
-    voxel_windows, projected = denoise_windows(starts, recording, low, high, compact)
+    voxel_windows, projected = denoise_windows(starts, recording, pair, other, compact)
     partials, slot_prior = combine(prior, owner, slot, projected, corr)
     gathered = lax.all_to_all(partials, "bricks", 0, 0)
     fresh, sent = update(prior, gathered, owner, slot, traces, slot_prior, voxel_windows, groups)

time: 74.5 us -> 72.3 us (0.970)
  local copies, waits for them, and re-layouts: 2.58 us -> 0.68 us
  starting transfers between devices: 21.2 us -> 19.6 us
  Pallas kernels: 13.2 us -> 14.5 us
    all_to_all x1, starting transfers between devices: 11.1 us -> 8.9 us  [shards(): prior = lax.all_to_all(piece, 'bricks', 0, 0)]
    unnamed x12 -> x8, local copies, waits for them, and re-layouts: 2.58 us -> 0.68 us
    pallas_call x1, Pallas kernels: 1.53 us -> 2.86 us  [prepare(): pl.pallas_call(prepare_kernel, in_specs=[VMEM] * 4, out_specs=[SMEM, VMEM...]
  transfers between devices with their start and end apart: 3 -> 3, of which waited for: 1 -> 1; matrix products, arithmetic and copies ran while one was open for 0% -> 0% of each run, Pallas kernels for 13% -> 15%
where the time goes in v5:
time: 72.3 us; the launch traced here: 71.9 us
  blocking collectives  33.7 us (47%)
  starting transfers between devices  19.6 us (27%)
  Pallas kernels  14.5 us (20%)
  waiting for transfers between devices  2.78 us (4%)
    all_to_all x1, blocking collectives, shards(): gathered = lax.all_to_all(partials, 'bricks', 0, 0)  18.4 us
    all_to_all x1, blocking collectives, shards(): shared = lax.all_to_all(sent, 'frames', 0, 0)  15.2 us
    all_to_all x1, starting transfers between devices, shards(): prior = lax.all_to_all(piece, 'bricks', 0, 0)  8.9 us
    ppermute x1, starting transfers between devices, swapped(): lax.ppermute(recording, 'bricks', within + [(b, a) for a, b in within])  8.75 us
    pallas_call x1, Pallas kernels, denoise_windows(): pl.pallas_call(denoise_kernel, in_specs=[SMEM, VMEM, VMEM, VMEM, VMEM], o...  8.28 us
    pallas_call x1, Pallas kernels, prepare(): pl.pallas_call(prepare_kernel, in_specs=[VMEM] * 4, out_specs=[SMEM, VMEM...  2.86 us
    all_to_all x1, waiting for transfers between devices, shards(): prior = lax.all_to_all(piece, 'bricks', 0, 0)  2.78 us
    ppermute x1, starting transfers between devices, swapped(): lax.ppermute(recording, 'bricks', across + [(b, a) for a, b in across])  1.92 us
  transfers between devices with their start and end apart: 3, of which 1 were waited for; matrix products, arithmetic and copies ran while one was open for 0% of the time, Pallas kernels for 15%

profile of v5, /device:TPU:1, one launch (start us, length us, event | category | flops | bytes accessed | tf_op | source)
XLA Modules:
  0.0 71.9 jit_solution(629060989224195497)
XLA Ops:
  0.6 8.7 %collective-permute-start = (bf16[16,4,16,256]{3,2,1,0:T(8,128)(2,1)}, bf16[16,4,16,256]{3,2,1,0:T(8,128)(2,1)S(1)}, u32[]{:S(2)}, u32[]{:S(2)}) collective-permute-start(bf16[16,4,16,256]{3,2,1,0:T(8,128)(2,1)} %rec.1), channel_id=1, source_target_pairs={{0,1},{2,3},{4,5},{6,7},{8,9},{10,11},{12,13},{14,15},{16,17},{18,... | collective-permute-start | bytes 1572872 | tf_op jit(solution)/shard_map/ppermute | solution.py:465
  9.4 1.9 %collective-permute-start.1 = (bf16[16,4,16,256]{3,2,1,0:T(8,128)(2,1)}, bf16[16,4,16,256]{3,2,1,0:T(8,128)(2,1)S(1)}, u32[]{:S(2)}, u32[]{:S(2)}) collective-permute-start(bf16[16,4,16,256]{3,2,1,0:T(8,128)(2,1)} %rec.1), channel_id=1, source_target_pairs={{1,2},{3,4},{5,6},{7,8},{9,10},{11,12},{13,14},{15,16},{17,18},{19... | collective-permute-start | bytes 1572872 | tf_op jit(solution)/shard_map/ppermute | solution.py:464
  11.3 0.0 copy-start
  11.3 2.9 %prepare.1 = (s32[32]{0:T(128)S(4)}, bf16[32,32,128]{2,1,0:T(8,128)(2,1)S(1)}, f32[32,128]{1,0:T(8,128)S(1)}, f32[32,128]{1,0:T(8,128)S(1)}, bf16[64,8,128]{2,1,0:T(8,128)(2,1)}) custom-call(s32[1,32]{1,0:T(1,128)} %bitcast.2, s32[1,32]{1,0:T(1,128)} %bitcast.5, bf16[16,32]{1,0:T(8,128)(2,1)} %traces.3, bf16[32,16384]{1,0:T(8,128)(2,1)} %foot.1), custom_call_target="tpu_custom_call" | custom-call | tf_op jit(solution)/shard_map/prepare/pallas_call | solution.py:123
  14.2 8.9 %all-to-all-start = ((bf16[64,8,128]{2,1,0:T(8,128)(2,1)}), bf16[64,8,128]{2,1,0:T(8,128)(2,1)S(1)}, u32[]{:S(2)}, u32[]{:S(2)}) async-start(bf16[64,8,128]{2,1,0:T(8,128)(2,1)} %get-tuple-element.16), calls=%async_computation | async-start | bytes 262144 | tf_op jit(solution)/shard_map/all_to_all | solution.py:477
  23.1 0.0 collective-permute-done.pair
  23.1 0.0 collective-permute-done.1.other
  23.1 0.0 copy-done
  23.1 8.3 %denoise.1 = (f32[32,16,128]{2,1,0:T(8,128)S(1)}, f32[16,128]{1,0:T(8,128)S(1)}) custom-call(s32[32]{0:T(128)S(4)} %get-tuple-element.15.starts, bf16[16,4,16,256]{3,2,1,0:T(8,128)(2,1)S(1)} %copy-done, bf16[16,4,16,256]{3,2,1,0:T(8,128)(2,1)S(1)} %collective-permute-done.pair, bf16[16,4,16,256]{3,2,1,0:T(8,128)(2,1)S(1)} %collective-permute-done.1.other, ...), custom_call_target="tpu_custom_call" | custom-call | tf_op jit(solution)/shard_map/denoise/pallas_call | solution.py:242
  31.4 2.8 %all-to-all-done.prior = bf16[64,8,128]{2,1,0:T(8,128)(2,1)S(1)} async-done(((bf16[64,8,128]{2,1,0:T(8,128)(2,1)}), bf16[64,8,128]{2,1,0:T(8,128)(2,1)S(1)}, u32[]{:S(2)}, u32[]{:S(2)}) %all-to-all-start) | async-done | bytes 131104 | tf_op jit(solution)/shard_map/all_to_all | solution.py:477
  34.2 0.0 copy-start.2
  34.2 0.0 copy-start.3
  34.2 0.7 copy-done.2
  34.8 0.0 copy-done.3
  34.9 0.6 combine.1
  35.5 0.0 copy-start.1
  35.5 18.4 %all_to_all.15.gathered = bf16[64,8,128]{2,1,0:T(8,128)(2,1)S(1)} all-to-all(bf16[64,8,128]{2,1,0:T(8,128)(2,1)S(1)} %get-tuple-element.20), channel_id=1, replica_groups=mesh['frames'=8,'bricks'=64] {'bricks'}, dimensions={0} | all-to-all | bytes 262144 | tf_op jit(solution)/shard_map/all_to_all | solution.py:480
  53.9 0.0 copy-done.1
  53.9 1.0 %update.1 = (f32[16,32]{1,0:T(8,128)S(1)}, f32[8,40,128]{2,1,0:T(8,128)S(1)}) custom-call(bf16[64,8,128]{2,1,0:T(8,128)(2,1)S(1)} %all-to-all-done.prior, bf16[64,8,128]{2,1,0:T(8,128)(2,1)S(1)} %all_to_all.15.gathered, s32[1,32]{1,0:T(1,128)S(1)} %bitcast.4, s32[1,32]{1,0:T(1,128)S(1)} %bitcast.7, bf16[16,32]{1,0:T(8,128)(2,1)S(1)} %copy-done.1, ...), custom_call_target="tpu_custom_call" | custom-call | tf_op jit(solution)/shard_map/update/pallas_call | solution.py:391
  54.9 15.2 %all_to_all.16.shared = f32[8,40,128]{2,1,0:T(8,128)S(1)} all-to-all(f32[8,40,128]{2,1,0:T(8,128)S(1)} %get-tuple-element.23), channel_id=1, replica_groups=mesh['frames'=8,'bricks'=64] {'frames'}, dimensions={0} | all-to-all | bytes 327680 | tf_op jit(solution)/shard_map/all_to_all | solution.py:482
  70.1 1.8 %finish.1 = (bf16[32,16384]{1,0:T(8,128)(2,1)}, f32[16,32]{1,0:T(8,128)}) custom-call(s32[32]{0:T(128)S(4)} %get-tuple-element.15.starts, f32[8,40,128]{2,1,0:T(8,128)S(1)} %all_to_all.16.shared, bf16[32,32,128]{2,1,0:T(8,128)(2,1)S(1)} %get-tuple-element.24.windows, f32[32,128]{1,0:T(8,128)S(1)} %get-tuple-element.17.compact, ...), custom_call_target="tpu_custom_call" | custom-call | tf_op jit(solution)/shard_map/finish/pallas_call | solution.py:447
Async XLA Ops:
  0.6 22.5 %collective-permute-start = (bf16[16,4,16,256]{3,2,1,0:T(8,128)(2,1)}, bf16[16,4,16,256]{3,2,1,0:T(8,128)(2,1)S(1)}, u32[]{:S(2)}, u32[]{:S(2)}) collective-permute-start(bf16[16,4,16,256]{3,2,1,0:T(8,128)(2,1)} %rec.1), channel_id=1, source_target_pairs={{0,1},{2,3},{4,5},{6,7},{8,9},{10,11},{12,13},{14,15},{16,17},{18,... | collective-permute-start | bytes 1572872 | tf_op jit(solution)/shard_map/ppermute | solution.py:465
  9.4 13.7 %collective-permute-start.1 = (bf16[16,4,16,256]{3,2,1,0:T(8,128)(2,1)}, bf16[16,4,16,256]{3,2,1,0:T(8,128)(2,1)S(1)}, u32[]{:S(2)}, u32[]{:S(2)}) collective-permute-start(bf16[16,4,16,256]{3,2,1,0:T(8,128)(2,1)} %rec.1), channel_id=1, source_target_pairs={{1,2},{3,4},{5,6},{7,8},{9,10},{11,12},{13,14},{15,16},{17,18},{19... | collective-permute-start | bytes 1572872 | tf_op jit(solution)/shard_map/ppermute | solution.py:464
  11.3 11.8 %copy-start = (bf16[16,4,16,256]{3,2,1,0:T(8,128)(2,1)S(1)}, bf16[16,4,16,256]{3,2,1,0:T(8,128)(2,1)}, u32[]{:S(2)}) copy-start(bf16[16,4,16,256]{3,2,1,0:T(8,128)(2,1)} %rec.1) | copy-start | bytes 1572868
  14.2 20.0 %all-to-all-start = ((bf16[64,8,128]{2,1,0:T(8,128)(2,1)}), bf16[64,8,128]{2,1,0:T(8,128)(2,1)S(1)}, u32[]{:S(2)}, u32[]{:S(2)}) async-start(bf16[64,8,128]{2,1,0:T(8,128)(2,1)} %get-tuple-element.16), calls=%async_computation | async-start | bytes 262144 | tf_op jit(solution)/shard_map/all_to_all | solution.py:477
  34.2 0.7 copy-start.2
  34.2 0.7 copy-start.3
  35.5 18.4 %copy-start.1 = (bf16[16,32]{1,0:T(8,128)(2,1)S(1)}, bf16[16,32]{1,0:T(8,128)(2,1)}, u32[]{:S(2)}) copy-start(bf16[16,32]{1,0:T(8,128)(2,1)} %traces.3) | copy-start | bytes 3076

commit v6 on v5

--- a/solution.py
+++ b/solution.py
@@ -49,6 +49,13 @@
 def two_terms(value):
     high = value.astype(BF16).astype(F32)
     return high, value - high
+
+
+def as_column(line):
+    count = line.shape[1]
+    square = (count, count)
+    same = iota(square, 0) == iota(square, 1)
+    return jnp.sum(jnp.where(same, line, 0), axis=1, keepdims=True)
 
 
 def label_rows(owner, slot, traces):
@@ -77,7 +84,7 @@
     return jnp.concatenate(rows + rows, axis=0) + jnp.where(lane < half, 0.0, moved)
 
 
-def prepare_kernel(owner, slot, traces, foot, starts, windows, compact, corr, piece):
+def prepare_kernel(owner, slot, traces, foot, starts, windows, compact, corr, labels, piece):
     blocks, voxels = foot.shape
     tiles = voxels // LANES
     acc = jnp.zeros((blocks, LANES), BF16)
@@ -105,6 +112,7 @@
         compact[k : k + 1, :] = own
         sums = jnp.where(lane == k, jnp.sum(window * own, axis=1, keepdims=True), sums)
     corr[...] = sums
+    labels[...] = jnp.where(lane == 0, as_column(owner[...]), as_column(slot[...]))
     diag = jnp.sum(jnp.where(lane == row, sums, 0.0), axis=1, keepdims=True)
     placed = jnp.where(lane == 2 * SUBLANES + row % SUBLANES, diag, 0.0)
     groups = blocks // SUBLANES
@@ -123,12 +131,13 @@
     return pl.pallas_call(
         prepare_kernel,
         in_specs=[VMEM] * 4,
-        out_specs=[SMEM, VMEM, VMEM, VMEM, VMEM],
+        out_specs=[SMEM, VMEM, VMEM, VMEM, VMEM, VMEM],
         out_shape=[
             pltpu.SMEM((blocks,), jnp.int32),
             pltpu.VMEM((blocks, blocks, LANES), BF16),
             pltpu.VMEM((blocks, LANES), F32),
             pltpu.VMEM((blocks, LANES), F32),
+            pltpu.VMEM((blocks, LANES), jnp.int32),
             pltpu.VMEM((owners, SUBLANES, LANES), BF16),
         ],
         compiler_params=PARAMS,
@@ -211,8 +220,8 @@
         for i in range(planes):
             for z in range(2):
                 for y in range(2):
-                    at = pl.multiple_of(f * (planes * rows) + i * rows + z * SUBLANES, SUBLANES)
-                    field[y, pl.ds(at, SUBLANES), :] = u[i][z][y].astype(BF16).astype(F32)
+                    at = pl.ds((i * rows + z * SUBLANES) * frames + f, SUBLANES, stride=frames)
+                    field[y, at, :] = u[i][z][y].astype(BF16).astype(F32)
 
     odd = position % 2 == 1
     for is_odd, low, high in ((True, pair, other), (False, other, pair)):
@@ -227,8 +236,8 @@
     acc = jnp.zeros((frames, LANES), F32)
     for k in range(blocks):
         first, second, offset = split_run(starts[k], tiles)
-        one = field[first & 1, pl.ds(first >> 1, frames, stride=planes * rows), :]
-        two = field[second & 1, pl.ds(second >> 1, frames, stride=planes * rows), :]
+        one = field[first & 1, pl.ds(pl.multiple_of((first >> 1) * frames, frames), frames), :]
+        two = field[second & 1, pl.ds(pl.multiple_of((second >> 1) * frames, frames), frames), :]
         window = jnp.where(lane >= offset, one, two)
         voxel_windows[k] = window
         column = jnp.sum(window * compact[k : k + 1, :], axis=1, keepdims=True)
@@ -253,21 +262,14 @@
     )(near_scalar(starts), near(recording), near(pair), near(other), near(compact))
 
 
-def as_column(line):
-    count = line.shape[1]
-    square = (count, count)
-    same = iota(square, 0) == iota(square, 1)
-    return jnp.sum(jnp.where(same, line, 0), axis=1, keepdims=True)
-
-
-def combine_kernel(prior, owner, slot, projected, corr, piece, slot_prior):
+def combine_kernel(prior, labels, projected, corr, piece, slot_prior):
     owners = prior.shape[0]
     blocks = corr.shape[0]
     frames = projected.shape[0]
     span = owners * SUBLANES
     flat = prior[...].astype(F32).reshape(span, LANES).astype(BF16)
-    owner = as_column(owner[...])
-    slot = as_column(slot[...])
+    owner = labels[:, 0:1]
+    slot = labels[:, 1:2]
     source = iota((blocks, span), 1)
     pick = jnp.concatenate(
         [onehot(source == owner * SUBLANES + i) for i in range(SUBLANES)], axis=0
@@ -310,11 +312,11 @@
     piece[...] = jnp.broadcast_to(whole[None], piece.shape)
 
 
-def combine(prior, owner, slot, projected, corr):
+def combine(prior, labels, projected, corr):
     blocks = corr.shape[0]
     return pl.pallas_call(
         combine_kernel,
-        in_specs=[VMEM] * 5,
+        in_specs=[VMEM] * 4,
         out_specs=[VMEM, VMEM],
         out_shape=[
             pltpu.VMEM(prior.shape, BF16),
@@ -322,11 +324,11 @@
         ],
         compiler_params=PARAMS,
         name="combine",
-    )(near(prior), near(owner), near(slot), near(projected), near(corr))
+    )(near(prior), near(labels), near(projected), near(corr))
 
 
 def update_kernel(
-    prior, gathered, owner, slot, traces, slot_prior, voxel_windows, traces_new, sent
+    prior, gathered, labels, traces, slot_prior, voxel_windows, traces_new, sent
 ):
     owners = prior.shape[0]
     blocks = slot_prior.shape[0]
@@ -342,7 +344,7 @@
     comps = lists[:SUBLANES] * float(owned) + lists[SUBLANES : 2 * SUBLANES]
     diags = lists[2 * SUBLANES : 3 * SUBLANES]
     position = lax.axis_index("bricks")
-    asked = as_column(owner[...] * owned + slot[...])
+    asked = labels[:, 0:1] * owned + labels[:, 1:2]
     held = position * owned + iota((owned, 1), 0)
     target = jnp.concatenate([asked, held], axis=0).astype(F32)
     count = blocks + owned
@@ -386,11 +388,11 @@
         sent[g, blocks : blocks + SUBLANES, :] = packed
 
 
-def update(prior, gathered, owner, slot, traces, slot_prior, voxel_windows, groups):
+def update(prior, gathered, labels, traces, slot_prior, voxel_windows, groups):
     blocks = slot_prior.shape[0]
     return pl.pallas_call(
         update_kernel,
-        in_specs=[VMEM] * 7,
+        in_specs=[VMEM] * 6,
         out_specs=[VMEM, VMEM],
         out_shape=[
             pltpu.VMEM(traces.shape, F32),
@@ -401,8 +403,7 @@
     )(
         near(prior),
         near(gathered),
-        near(owner),
-        near(slot),
+        near(labels),
         near(traces),
         near(slot_prior),
         near(voxel_windows),
@@ -473,12 +474,14 @@
     pair, other = swapped(recording)
     owner = block_owner.T
     slot = block_slot[None, :]
-    starts, windows, compact, corr, piece = prepare(owner, slot, traces, footprints, owners)
+    starts, windows, compact, corr, labels, piece = prepare(owner, slot, traces, footprints, owners)
     prior = lax.all_to_all(piece, "bricks", 0, 0)
     voxel_windows, projected = denoise_windows(starts, recording, pair, other, compact)
-    partials, slot_prior = combine(prior, owner, slot, projected, corr)
+    partials, slot_prior = combine(prior, labels, projected, corr)
     gathered = lax.all_to_all(partials, "bricks", 0, 0)
-    fresh, sent = update(prior, gathered, owner, slot, traces, slot_prior, voxel_windows, groups)
+    fresh, sent = update(
+        prior, gathered, labels, traces, slot_prior, voxel_windows, groups
+    )
     shared = lax.all_to_all(sent, "frames", 0, 0)
     footprints_new, traces_new = finish(starts, shared, windows, compact, fresh, voxels)
     return (traces_new, footprints_new)

time: 72.3 us -> 71.4 us (0.988)
  transfers between devices with their start and end apart: 3 -> 3, of which waited for: 1 -> 1; matrix products, arithmetic and copies ran while one was open for 0% -> 0% of each run, Pallas kernels for 15% -> 16%
where the time goes in v6:
time: 71.4 us; the launch traced here: 71.1 us
  blocking collectives  33.6 us (47%)
  starting transfers between devices  19.6 us (27%)
  Pallas kernels  14.4 us (20%)
  waiting for transfers between devices  2.88 us (4%)
    all_to_all x1, blocking collectives, shards(): gathered = lax.all_to_all(partials, 'bricks', 0, 0)  18.3 us
    all_to_all x1, blocking collectives, shards(): shared = lax.all_to_all(sent, 'frames', 0, 0)  15.2 us
    all_to_all x1, starting transfers between devices, shards(): prior = lax.all_to_all(piece, 'bricks', 0, 0)  8.9 us
    ppermute x1, starting transfers between devices, swapped(): lax.ppermute(recording, 'bricks', within + [(b, a) for a, b in within])  8.75 us
    pallas_call x1, Pallas kernels, denoise_windows(): pl.pallas_call(denoise_kernel, in_specs=[SMEM, VMEM, VMEM, VMEM, VMEM], o...  8.19 us
    all_to_all x1, waiting for transfers between devices, shards(): prior = lax.all_to_all(piece, 'bricks', 0, 0)  2.87 us
    pallas_call x1, Pallas kernels, prepare(): pl.pallas_call(prepare_kernel, in_specs=[VMEM] * 4, out_specs=[SMEM, VMEM...  2.84 us
    ppermute x1, starting transfers between devices, swapped(): lax.ppermute(recording, 'bricks', across + [(b, a) for a, b in across])  1.92 us
  transfers between devices with their start and end apart: 3, of which 1 were waited for; matrix products, arithmetic and copies ran while one was open for 0% of the time, Pallas kernels for 16%

profile of v6, /device:TPU:1, one launch (start us, length us, event | category | flops | bytes accessed | tf_op | source)
XLA Modules:
  0.0 71.1 jit_solution(5648422337765752534)
XLA Ops:
  0.6 8.7 %collective-permute-start = (bf16[16,4,16,256]{3,2,1,0:T(8,128)(2,1)}, bf16[16,4,16,256]{3,2,1,0:T(8,128)(2,1)S(1)}, u32[]{:S(2)}, u32[]{:S(2)}) collective-permute-start(bf16[16,4,16,256]{3,2,1,0:T(8,128)(2,1)} %rec.1), channel_id=1, source_target_pairs={{0,1},{2,3},{4,5},{6,7},{8,9},{10,11},{12,13},{14,15},{16,17},{18,... | collective-permute-start | bytes 1572872 | tf_op jit(solution)/shard_map/ppermute | solution.py:466
  9.4 1.9 %collective-permute-start.1 = (bf16[16,4,16,256]{3,2,1,0:T(8,128)(2,1)}, bf16[16,4,16,256]{3,2,1,0:T(8,128)(2,1)S(1)}, u32[]{:S(2)}, u32[]{:S(2)}) collective-permute-start(bf16[16,4,16,256]{3,2,1,0:T(8,128)(2,1)} %rec.1), channel_id=1, source_target_pairs={{1,2},{3,4},{5,6},{7,8},{9,10},{11,12},{13,14},{15,16},{17,18},{19... | collective-permute-start | bytes 1572872 | tf_op jit(solution)/shard_map/ppermute | solution.py:465
  11.3 0.0 copy-start
  11.3 2.8 %prepare.1 = (s32[32]{0:T(128)S(4)}, bf16[32,32,128]{2,1,0:T(8,128)(2,1)S(1)}, f32[32,128]{1,0:T(8,128)S(1)}, f32[32,128]{1,0:T(8,128)S(1)}, s32[32,128]{1,0:T(8,128)S(1)}, /*index=5*/bf16[64,8,128]{2,1,0:T(8,128)(2,1)}) custom-call(s32[1,32]{1,0:T(1,128)} %bitcast.2, s32[1,32]{1,0:T(1,128)} %bitcast.3, bf16[16,32]{1,0:T(8,128)(2,1)} %traces.3, ...), custom_call_target="tpu_custom_call" | custom-call | tf_op jit(solution)/shard_map/prepare/pallas_call | solution.py:131
  14.2 8.9 %all-to-all-start = ((bf16[64,8,128]{2,1,0:T(8,128)(2,1)}), bf16[64,8,128]{2,1,0:T(8,128)(2,1)S(1)}, u32[]{:S(2)}, u32[]{:S(2)}) async-start(bf16[64,8,128]{2,1,0:T(8,128)(2,1)} %get-tuple-element.17), calls=%async_computation | async-start | bytes 262144 | tf_op jit(solution)/shard_map/all_to_all | solution.py:478
  23.1 0.0 collective-permute-done.pair
  23.1 0.0 collective-permute-done.1.other
  23.1 0.0 copy-done
  23.1 8.2 %denoise.1 = (f32[32,16,128]{2,1,0:T(8,128)S(1)}, f32[16,128]{1,0:T(8,128)S(1)}) custom-call(s32[32]{0:T(128)S(4)} %get-tuple-element.16.starts, bf16[16,4,16,256]{3,2,1,0:T(8,128)(2,1)S(1)} %copy-done, bf16[16,4,16,256]{3,2,1,0:T(8,128)(2,1)S(1)} %collective-permute-done.pair, bf16[16,4,16,256]{3,2,1,0:T(8,128)(2,1)S(1)} %collective-permute-done.1.other, ...), custom_call_target="tpu_custom_call" | custom-call | tf_op jit(solution)/shard_map/denoise/pallas_call | solution.py:251
  31.3 2.9 %all-to-all-done.prior = bf16[64,8,128]{2,1,0:T(8,128)(2,1)S(1)} async-done(((bf16[64,8,128]{2,1,0:T(8,128)(2,1)}), bf16[64,8,128]{2,1,0:T(8,128)(2,1)S(1)}, u32[]{:S(2)}, u32[]{:S(2)}) %all-to-all-start) | async-done | bytes 131104 | tf_op jit(solution)/shard_map/all_to_all | solution.py:478
  34.2 0.6 combine.1
  34.8 0.0 copy-start.1
  34.8 18.3 %all_to_all.15.gathered = bf16[64,8,128]{2,1,0:T(8,128)(2,1)S(1)} all-to-all(bf16[64,8,128]{2,1,0:T(8,128)(2,1)S(1)} %get-tuple-element.22), channel_id=1, replica_groups=mesh['frames'=8,'bricks'=64] {'bricks'}, dimensions={0} | all-to-all | bytes 262144 | tf_op jit(solution)/shard_map/all_to_all | solution.py:481
  53.1 0.0 copy-done.1
  53.1 0.9 %update.1 = (f32[16,32]{1,0:T(8,128)S(1)}, f32[8,40,128]{2,1,0:T(8,128)S(1)}) custom-call(bf16[64,8,128]{2,1,0:T(8,128)(2,1)S(1)} %all-to-all-done.prior, bf16[64,8,128]{2,1,0:T(8,128)(2,1)S(1)} %all_to_all.15.gathered, s32[32,128]{1,0:T(8,128)S(1)} %get-tuple-element.18.labels, bf16[16,32]{1,0:T(8,128)(2,1)S(1)} %copy-done.1, ...), custom_call_target="tpu_custom_call" | custom-call | tf_op jit(solution)/shard_map/update/pallas_call | solution.py:393
  54.1 15.2 %all_to_all.16.shared = f32[8,40,128]{2,1,0:T(8,128)S(1)} all-to-all(f32[8,40,128]{2,1,0:T(8,128)S(1)} %get-tuple-element.25), channel_id=1, replica_groups=mesh['frames'=8,'bricks'=64] {'frames'}, dimensions={0} | all-to-all | bytes 327680 | tf_op jit(solution)/shard_map/all_to_all | solution.py:485
  69.3 1.8 %finish.1 = (bf16[32,16384]{1,0:T(8,128)(2,1)}, f32[16,32]{1,0:T(8,128)}) custom-call(s32[32]{0:T(128)S(4)} %get-tuple-element.16.starts, f32[8,40,128]{2,1,0:T(8,128)S(1)} %all_to_all.16.shared, bf16[32,32,128]{2,1,0:T(8,128)(2,1)S(1)} %get-tuple-element.26.windows, f32[32,128]{1,0:T(8,128)S(1)} %get-tuple-element.19.compact, ...), custom_call_target="tpu_custom_call" | custom-call | tf_op jit(solution)/shard_map/finish/pallas_call | solution.py:448
Async XLA Ops:
  0.6 22.4 %collective-permute-start = (bf16[16,4,16,256]{3,2,1,0:T(8,128)(2,1)}, bf16[16,4,16,256]{3,2,1,0:T(8,128)(2,1)S(1)}, u32[]{:S(2)}, u32[]{:S(2)}) collective-permute-start(bf16[16,4,16,256]{3,2,1,0:T(8,128)(2,1)} %rec.1), channel_id=1, source_target_pairs={{0,1},{2,3},{4,5},{6,7},{8,9},{10,11},{12,13},{14,15},{16,17},{18,... | collective-permute-start | bytes 1572872 | tf_op jit(solution)/shard_map/ppermute | solution.py:466
  9.4 13.7 %collective-permute-start.1 = (bf16[16,4,16,256]{3,2,1,0:T(8,128)(2,1)}, bf16[16,4,16,256]{3,2,1,0:T(8,128)(2,1)S(1)}, u32[]{:S(2)}, u32[]{:S(2)}) collective-permute-start(bf16[16,4,16,256]{3,2,1,0:T(8,128)(2,1)} %rec.1), channel_id=1, source_target_pairs={{1,2},{3,4},{5,6},{7,8},{9,10},{11,12},{13,14},{15,16},{17,18},{19... | collective-permute-start | bytes 1572872 | tf_op jit(solution)/shard_map/ppermute | solution.py:465
  11.3 11.8 %copy-start = (bf16[16,4,16,256]{3,2,1,0:T(8,128)(2,1)S(1)}, bf16[16,4,16,256]{3,2,1,0:T(8,128)(2,1)}, u32[]{:S(2)}) copy-start(bf16[16,4,16,256]{3,2,1,0:T(8,128)(2,1)} %rec.1) | copy-start | bytes 1572868
  14.2 20.0 %all-to-all-start = ((bf16[64,8,128]{2,1,0:T(8,128)(2,1)}), bf16[64,8,128]{2,1,0:T(8,128)(2,1)S(1)}, u32[]{:S(2)}, u32[]{:S(2)}) async-start(bf16[64,8,128]{2,1,0:T(8,128)(2,1)} %get-tuple-element.17), calls=%async_computation | async-start | bytes 262144 | tf_op jit(solution)/shard_map/all_to_all | solution.py:478
  34.8 18.3 %copy-start.1 = (bf16[16,32]{1,0:T(8,128)(2,1)S(1)}, bf16[16,32]{1,0:T(8,128)(2,1)}, u32[]{:S(2)}) copy-start(bf16[16,32]{1,0:T(8,128)(2,1)} %traces.3) | copy-start | bytes 3076

commit v7 on v6

--- a/solution.py
+++ b/solution.py
@@ -11,6 +11,7 @@
 LANES = 128
 SUBLANES = 8
 F32 = jnp.float32
+MARK_SCALE = 16384.0
 BF16 = jnp.bfloat16
 VMEM = pl.BlockSpec(memory_space=pltpu.VMEM)
 SMEM = pl.BlockSpec(memory_space=pltpu.SMEM)
@@ -90,8 +91,8 @@
     acc = jnp.zeros((blocks, LANES), BF16)
     for t in range(1, tiles):
         cell = foot[:, t * LANES : (t + 1) * LANES]
-        acc = acc + jnp.where(cell > 0, jnp.asarray(t, BF16), jnp.asarray(0, BF16))
-    tile_of = acc.astype(F32)
+        acc = jnp.maximum(acc, jnp.minimum(cell, jnp.asarray(t / MARK_SCALE, BF16)))
+    tile_of = acc.astype(F32) * MARK_SCALE
     lowest = jnp.min(tile_of, axis=1, keepdims=True)
     highest = jnp.max(tile_of, axis=1, keepdims=True)
     first_tile = jnp.where(highest - lowest > 1.5, highest, lowest)
@@ -435,12 +436,15 @@
     current = compact[...]
     stepped = jnp.maximum(current + (product - spread) / norm, 0.0)
     stepped = jnp.where(current > 0, stepped, 0.0)
+    height = 2 * SUBLANES
     for k in range(blocks):
         first, second, offset = split_run(starts[k], tiles)
-        for index, part in ((first, lane >= offset), (second, lane < offset)):
+        group = slice(k // height * height, k // height * height + height)
+        chosen = row[group] == k
+        for index, part in ((first, lane[group] >= offset), (second, lane[group] < offset)):
             at = lane_tile(index)
-            old = out[:, at].astype(F32)
-            out[:, at] = jnp.where((row == k) & part, stepped, old).astype(out.dtype)
+            old = out[group, at].astype(F32)
+            out[group, at] = jnp.where(chosen & part, stepped[group], old).astype(out.dtype)
 
 
 def finish(starts, shared, windows, compact, fresh, voxels):
@@ -462,8 +466,8 @@
     count = lax.axis_size("bricks")
     across = [(i, i + 1) for i in range(1, count - 1, 2)]
     within = [(i, i + 1) for i in range(0, count, 2)]
+    pair = lax.ppermute(recording, "bricks", within + [(b, a) for a, b in within])
     other = lax.ppermute(recording, "bricks", across + [(b, a) for a, b in across])
-    pair = lax.ppermute(recording, "bricks", within + [(b, a) for a, b in within])
     return pair, other
 
 

time: 71.4 us -> 71.4 us (level)
  transfers between devices with their start and end apart: 3 -> 3, of which waited for: 1 -> 1; matrix products, arithmetic and copies ran while one was open for 0% -> 0% of each run, Pallas kernels for 16% -> 15%
where the time goes in v7:
time: 71.4 us; the launch traced here: 71 us
  blocking collectives  33.6 us (47%)
  starting transfers between devices  19.6 us (27%)
  Pallas kernels  14.3 us (20%)
  waiting for transfers between devices  2.88 us (4%)
    all_to_all x1, blocking collectives, shards(): gathered = lax.all_to_all(partials, 'bricks', 0, 0)  18.3 us
    all_to_all x1, blocking collectives, shards(): shared = lax.all_to_all(sent, 'frames', 0, 0)  15.3 us
    all_to_all x1, starting transfers between devices, shards(): prior = lax.all_to_all(piece, 'bricks', 0, 0)  8.9 us
    ppermute x1, starting transfers between devices, swapped(): lax.ppermute(recording, 'bricks', within + [(b, a) for a, b in within])  8.75 us
    pallas_call x1, Pallas kernels, denoise_windows(): pl.pallas_call(denoise_kernel, in_specs=[SMEM, VMEM, VMEM, VMEM, VMEM], o...  8.19 us
    all_to_all x1, waiting for transfers between devices, shards(): prior = lax.all_to_all(piece, 'bricks', 0, 0)  2.87 us
    pallas_call x1, Pallas kernels, prepare(): pl.pallas_call(prepare_kernel, in_specs=[VMEM] * 4, out_specs=[SMEM, VMEM...  2.77 us
    ppermute x1, starting transfers between devices, swapped(): lax.ppermute(recording, 'bricks', across + [(b, a) for a, b in across])  1.92 us
  transfers between devices with their start and end apart: 3, of which 1 were waited for; matrix products, arithmetic and copies ran while one was open for 0% of the time, Pallas kernels for 15%

profile of v7, /device:TPU:1, one launch (start us, length us, event | category | flops | bytes accessed | tf_op | source)
XLA Modules:
  0.0 71.0 jit_solution(10133634054510379568)
XLA Ops:
  0.6 8.7 %collective-permute-start = (bf16[16,4,16,256]{3,2,1,0:T(8,128)(2,1)}, bf16[16,4,16,256]{3,2,1,0:T(8,128)(2,1)S(1)}, u32[]{:S(2)}, u32[]{:S(2)}) collective-permute-start(bf16[16,4,16,256]{3,2,1,0:T(8,128)(2,1)} %rec.1), channel_id=1, source_target_pairs={{0,1},{2,3},{4,5},{6,7},{8,9},{10,11},{12,13},{14,15},{16,17},{18,... | collective-permute-start | bytes 1572872 | tf_op jit(solution)/shard_map/ppermute | solution.py:469
  9.4 1.9 %collective-permute-start.1 = (bf16[16,4,16,256]{3,2,1,0:T(8,128)(2,1)}, bf16[16,4,16,256]{3,2,1,0:T(8,128)(2,1)S(1)}, u32[]{:S(2)}, u32[]{:S(2)}) collective-permute-start(bf16[16,4,16,256]{3,2,1,0:T(8,128)(2,1)} %rec.1), channel_id=1, source_target_pairs={{1,2},{3,4},{5,6},{7,8},{9,10},{11,12},{13,14},{15,16},{17,18},{19... | collective-permute-start | bytes 1572872 | tf_op jit(solution)/shard_map/ppermute | solution.py:470
  11.3 0.0 copy-start
  11.3 2.8 %prepare.1 = (s32[32]{0:T(128)S(4)}, bf16[32,32,128]{2,1,0:T(8,128)(2,1)S(1)}, f32[32,128]{1,0:T(8,128)S(1)}, f32[32,128]{1,0:T(8,128)S(1)}, s32[32,128]{1,0:T(8,128)S(1)}, /*index=5*/bf16[64,8,128]{2,1,0:T(8,128)(2,1)}) custom-call(s32[1,32]{1,0:T(1,128)} %bitcast.2, s32[1,32]{1,0:T(1,128)} %bitcast.3, bf16[16,32]{1,0:T(8,128)(2,1)} %traces.3, ...), custom_call_target="tpu_custom_call" | custom-call | tf_op jit(solution)/shard_map/prepare/pallas_call | solution.py:132
  14.1 8.9 %all-to-all-start = ((bf16[64,8,128]{2,1,0:T(8,128)(2,1)}), bf16[64,8,128]{2,1,0:T(8,128)(2,1)S(1)}, u32[]{:S(2)}, u32[]{:S(2)}) async-start(bf16[64,8,128]{2,1,0:T(8,128)(2,1)} %get-tuple-element.17), calls=%async_computation | async-start | bytes 262144 | tf_op jit(solution)/shard_map/all_to_all | solution.py:482
  23.0 0.0 collective-permute-done.pair
  23.0 0.0 collective-permute-done.1.other
  23.0 0.0 copy-done
  23.0 8.2 %denoise.1 = (f32[32,16,128]{2,1,0:T(8,128)S(1)}, f32[16,128]{1,0:T(8,128)S(1)}) custom-call(s32[32]{0:T(128)S(4)} %get-tuple-element.16.starts, bf16[16,4,16,256]{3,2,1,0:T(8,128)(2,1)S(1)} %copy-done, bf16[16,4,16,256]{3,2,1,0:T(8,128)(2,1)S(1)} %collective-permute-done.pair, bf16[16,4,16,256]{3,2,1,0:T(8,128)(2,1)S(1)} %collective-permute-done.1.other, ...), custom_call_target="tpu_custom_call" | custom-call | tf_op jit(solution)/shard_map/denoise/pallas_call | solution.py:252
  31.2 2.9 %all-to-all-done.prior = bf16[64,8,128]{2,1,0:T(8,128)(2,1)S(1)} async-done(((bf16[64,8,128]{2,1,0:T(8,128)(2,1)}), bf16[64,8,128]{2,1,0:T(8,128)(2,1)S(1)}, u32[]{:S(2)}, u32[]{:S(2)}) %all-to-all-start) | async-done | bytes 131104 | tf_op jit(solution)/shard_map/all_to_all | solution.py:482
  34.1 0.6 combine.1
  34.7 0.0 copy-start.1
  34.7 18.3 %all_to_all.15.gathered = bf16[64,8,128]{2,1,0:T(8,128)(2,1)S(1)} all-to-all(bf16[64,8,128]{2,1,0:T(8,128)(2,1)S(1)} %get-tuple-element.22), channel_id=1, replica_groups=mesh['frames'=8,'bricks'=64] {'bricks'}, dimensions={0} | all-to-all | bytes 262144 | tf_op jit(solution)/shard_map/all_to_all | solution.py:485
  53.0 0.0 copy-done.1
  53.0 0.9 %update.1 = (f32[16,32]{1,0:T(8,128)S(1)}, f32[8,40,128]{2,1,0:T(8,128)S(1)}) custom-call(bf16[64,8,128]{2,1,0:T(8,128)(2,1)S(1)} %all-to-all-done.prior, bf16[64,8,128]{2,1,0:T(8,128)(2,1)S(1)} %all_to_all.15.gathered, s32[32,128]{1,0:T(8,128)S(1)} %get-tuple-element.18.labels, bf16[16,32]{1,0:T(8,128)(2,1)S(1)} %copy-done.1, ...), custom_call_target="tpu_custom_call" | custom-call | tf_op jit(solution)/shard_map/update/pallas_call | solution.py:394
  54.0 15.3 %all_to_all.16.shared = f32[8,40,128]{2,1,0:T(8,128)S(1)} all-to-all(f32[8,40,128]{2,1,0:T(8,128)S(1)} %get-tuple-element.25), channel_id=1, replica_groups=mesh['frames'=8,'bricks'=64] {'frames'}, dimensions={0} | all-to-all | bytes 327680 | tf_op jit(solution)/shard_map/all_to_all | solution.py:489
  69.3 1.8 %finish.1 = (bf16[32,16384]{1,0:T(8,128)(2,1)}, f32[16,32]{1,0:T(8,128)}) custom-call(s32[32]{0:T(128)S(4)} %get-tuple-element.16.starts, f32[8,40,128]{2,1,0:T(8,128)S(1)} %all_to_all.16.shared, bf16[32,32,128]{2,1,0:T(8,128)(2,1)S(1)} %get-tuple-element.26.windows, f32[32,128]{1,0:T(8,128)S(1)} %get-tuple-element.19.compact, ...), custom_call_target="tpu_custom_call" | custom-call | tf_op jit(solution)/shard_map/finish/pallas_call | solution.py:452
Async XLA Ops:
  0.6 22.4 %collective-permute-start = (bf16[16,4,16,256]{3,2,1,0:T(8,128)(2,1)}, bf16[16,4,16,256]{3,2,1,0:T(8,128)(2,1)S(1)}, u32[]{:S(2)}, u32[]{:S(2)}) collective-permute-start(bf16[16,4,16,256]{3,2,1,0:T(8,128)(2,1)} %rec.1), channel_id=1, source_target_pairs={{0,1},{2,3},{4,5},{6,7},{8,9},{10,11},{12,13},{14,15},{16,17},{18,... | collective-permute-start | bytes 1572872 | tf_op jit(solution)/shard_map/ppermute | solution.py:469
  9.4 13.6 %collective-permute-start.1 = (bf16[16,4,16,256]{3,2,1,0:T(8,128)(2,1)}, bf16[16,4,16,256]{3,2,1,0:T(8,128)(2,1)S(1)}, u32[]{:S(2)}, u32[]{:S(2)}) collective-permute-start(bf16[16,4,16,256]{3,2,1,0:T(8,128)(2,1)} %rec.1), channel_id=1, source_target_pairs={{1,2},{3,4},{5,6},{7,8},{9,10},{11,12},{13,14},{15,16},{17,18},{19... | collective-permute-start | bytes 1572872 | tf_op jit(solution)/shard_map/ppermute | solution.py:470
  11.3 11.7 %copy-start = (bf16[16,4,16,256]{3,2,1,0:T(8,128)(2,1)S(1)}, bf16[16,4,16,256]{3,2,1,0:T(8,128)(2,1)}, u32[]{:S(2)}) copy-start(bf16[16,4,16,256]{3,2,1,0:T(8,128)(2,1)} %rec.1) | copy-start | bytes 1572868
  14.1 20.0 %all-to-all-start = ((bf16[64,8,128]{2,1,0:T(8,128)(2,1)}), bf16[64,8,128]{2,1,0:T(8,128)(2,1)S(1)}, u32[]{:S(2)}, u32[]{:S(2)}) async-start(bf16[64,8,128]{2,1,0:T(8,128)(2,1)} %get-tuple-element.17), calls=%async_computation | async-start | bytes 262144 | tf_op jit(solution)/shard_map/all_to_all | solution.py:482
  34.7 18.3 %copy-start.1 = (bf16[16,32]{1,0:T(8,128)(2,1)S(1)}, bf16[16,32]{1,0:T(8,128)(2,1)}, u32[]{:S(2)}) copy-start(bf16[16,32]{1,0:T(8,128)(2,1)} %traces.3) | copy-start | bytes 3076

commit v8 on v7

--- a/solution.py
+++ b/solution.py
@@ -150,8 +150,12 @@
     return difference / (1.0 + difference * difference)
 
 
-def relax(planes, masks):
-    first_row, last_row, first_col, last_col = masks
+PITCH = 32
+TOP = 8
+
+
+def relax(planes, masks, held, passed, base):
+    first_col, last_col = masks
     across = [
         [[flux_of(planes[i + 1][z][y] - planes[i][z][y]) for y in range(2)] for z in range(2)]
         for i in range(len(planes) - 1)
@@ -161,15 +165,19 @@
         u = planes[i]
         edge = [[flux_of(u[0][0]), flux_of(u[0][1])], [flux_of(u[1][0]), None]]
         total = [[across[i][z][y] - across[i - 1][z][y] for y in range(2)] for z in range(2)]
+        slot = (base + i - 1) * PITCH + TOP
         for y in range(2):
-            low = pltpu.roll(u[0][y], SUBLANES - 1, 0)
-            high = pltpu.roll(u[1][y], SUBLANES - 1, 0)
-            down_low = flux_of(jnp.where(last_row, high, low) - u[0][y])
-            down_high = flux_of(jnp.where(last_row, 0.0, high) - u[1][y])
-            up_low = pltpu.roll(down_low, 1, 0)
-            up_high = pltpu.roll(down_high, 1, 0)
-            total[0][y] = total[0][y] + (down_low - jnp.where(first_row, edge[0][y], up_low))
-            total[1][y] = total[1][y] + (down_high - jnp.where(first_row, up_low, up_high))
+            for z in range(2):
+                held[y, slot + z * SUBLANES : slot + (z + 1) * SUBLANES, :] = u[z][y]
+            passed[y, slot - 1 : slot, :] = edge[0][y][:1]
+            down = []
+            for z in range(2):
+                at = slot + z * SUBLANES
+                down.append(flux_of(held[y, at + 1 : at + 1 + SUBLANES, :] - u[z][y]))
+                passed[y, at : at + SUBLANES, :] = down[z]
+            for z in range(2):
+                at = slot + z * SUBLANES
+                total[z][y] = total[z][y] + (down[z] - passed[y, at - 1 : at - 1 + SUBLANES, :])
         for z in range(2):
             low = pltpu.roll(u[z][0], LANES - 1, 1)
             high = pltpu.roll(u[z][1], LANES - 1, 1)
@@ -195,22 +203,26 @@
     return [[cell * keep for cell in line] for line in plane]
 
 
-def denoise_kernel(starts, rec, pair, other, compact, voxel_windows, projected, field):
+def denoise_kernel(
+    starts, rec, pair, other, compact, voxel_windows, projected, field, held, passed
+):
     frames, planes, rows, _ = rec.shape
     width = 3
     position = lax.axis_index("bricks")
     low_keep = jnp.where(position > 0, 1.0, 0.0)
     high_keep = jnp.where(position < lax.axis_size("bricks") - 1, 1.0, 0.0)
-    row = iota((SUBLANES, LANES), 0)
     col = iota((SUBLANES, LANES), 1)
-    masks = (row == 0, row == SUBLANES - 1, col == 0, col == LANES - 1)
-
-    def one_frame(f, low, high):
+    masks = (col == 0, col == LANES - 1)
+    held[...] = jnp.zeros(held.shape, F32)
+
+    def one_frame(f, low, high, lane_of):
         u = [quarters(low[f, planes - width + i]) for i in range(width)]
         u = u + [quarters(rec[f, i]) for i in range(planes)]
         u = u + [quarters(high[f, i]) for i in range(width)]
+        base = lane_of * width * (planes + 2)
         for sweep in range(width):
-            u = relax(u, masks)
+            u = relax(u, masks, held, passed, base)
+            base += len(u)
             extra = width - 1 - sweep
             if extra:
                 u = (
@@ -229,7 +241,10 @@
 
         @pl.when(odd if is_odd else jnp.logical_not(odd))
         def _(low=low, high=high):
-            pl.loop(0, frames)(lambda f: one_frame(f, low, high))
+            @pl.loop(0, frames // 2)
+            def _(g):
+                one_frame(2 * g, low, high, 0)
+                one_frame(2 * g + 1, low, high, 1)
 
     blocks = compact.shape[0]
     tiles = planes * rows * 2
@@ -257,7 +272,11 @@
             pltpu.VMEM((blocks, frames, LANES), F32),
             pltpu.VMEM((frames, LANES), F32),
         ],
-        scratch_shapes=[pltpu.VMEM((2, frames * planes * rows, LANES), F32)],
+        scratch_shapes=[
+            pltpu.VMEM((2, frames * planes * rows, LANES), F32),
+            pltpu.VMEM((2, 6 * (planes + 2) * PITCH, LANES), F32),
+            pltpu.VMEM((2, 6 * (planes + 2) * PITCH, LANES), F32),
+        ],
         compiler_params=PARAMS,
         name="denoise",
     )(near_scalar(starts), near(recording), near(pair), near(other), near(compact))

time: 71.4 us -> 69.7 us (0.976)
  Pallas kernels: 14.3 us -> 12.7 us
  blocking collectives: 33.6 us -> 32 us
  waiting for transfers between devices: 2.88 us -> 4.46 us
    all_to_all x1, blocking collectives: 18.3 us -> 16.7 us  [shards(): gathered = lax.all_to_all(partials, 'bricks', 0, 0)]
    pallas_call x1, Pallas kernels: 8.19 us -> 6.6 us  [denoise_windows(): pl.pallas_call(denoise_kernel, in_specs=[SMEM, VMEM, VMEM, VMEM, VMEM], o...]
    all_to_all x1, waiting for transfers between devices: 2.87 us -> 4.46 us  [shards(): prior = lax.all_to_all(piece, 'bricks', 0, 0)]
  transfers between devices with their start and end apart: 3 -> 3, of which waited for: 1 -> 1; matrix products, arithmetic and copies ran while one was open for 0% -> 0% of each run, Pallas kernels for 15% -> 14%
where the time goes in v8:
time: 69.7 us; the launch traced here: 69.4 us
  blocking collectives  32 us (46%)
  starting transfers between devices  19.6 us (28%)
  Pallas kernels  12.7 us (18%)
  waiting for transfers between devices  4.46 us (6%)
  between operations  0.71 us (1%)
    all_to_all x1, blocking collectives, shards(): gathered = lax.all_to_all(partials, 'bricks', 0, 0)  16.7 us
    all_to_all x1, blocking collectives, shards(): shared = lax.all_to_all(sent, 'frames', 0, 0)  15.2 us
    all_to_all x1, starting transfers between devices, shards(): prior = lax.all_to_all(piece, 'bricks', 0, 0)  8.9 us
    ppermute x1, starting transfers between devices, swapped(): lax.ppermute(recording, 'bricks', within + [(b, a) for a, b in within])  8.75 us
    pallas_call x1, Pallas kernels, denoise_windows(): pl.pallas_call(denoise_kernel, in_specs=[SMEM, VMEM, VMEM, VMEM, VMEM], o...  6.6 us
    all_to_all x1, waiting for transfers between devices, shards(): prior = lax.all_to_all(piece, 'bricks', 0, 0)  4.46 us
    pallas_call x1, Pallas kernels, prepare(): pl.pallas_call(prepare_kernel, in_specs=[VMEM] * 4, out_specs=[SMEM, VMEM...  2.77 us
    ppermute x1, starting transfers between devices, swapped(): lax.ppermute(recording, 'bricks', across + [(b, a) for a, b in across])  1.92 us
  transfers between devices with their start and end apart: 3, of which 1 were waited for; matrix products, arithmetic and copies ran while one was open for 0% of the time, Pallas kernels for 14%

profile of v8, /device:TPU:1, one launch (start us, length us, event | category | flops | bytes accessed | tf_op | source)
XLA Modules:
  0.0 69.4 jit_solution(33454592413179523)
XLA Ops:
  0.6 8.7 %collective-permute-start = (bf16[16,4,16,256]{3,2,1,0:T(8,128)(2,1)}, bf16[16,4,16,256]{3,2,1,0:T(8,128)(2,1)S(1)}, u32[]{:S(2)}, u32[]{:S(2)}) collective-permute-start(bf16[16,4,16,256]{3,2,1,0:T(8,128)(2,1)} %rec.1), channel_id=1, source_target_pairs={{0,1},{2,3},{4,5},{6,7},{8,9},{10,11},{12,13},{14,15},{16,17},{18,... | collective-permute-start | bytes 1572872 | tf_op jit(solution)/shard_map/ppermute | solution.py:488
  9.4 1.9 %collective-permute-start.1 = (bf16[16,4,16,256]{3,2,1,0:T(8,128)(2,1)}, bf16[16,4,16,256]{3,2,1,0:T(8,128)(2,1)S(1)}, u32[]{:S(2)}, u32[]{:S(2)}) collective-permute-start(bf16[16,4,16,256]{3,2,1,0:T(8,128)(2,1)} %rec.1), channel_id=1, source_target_pairs={{1,2},{3,4},{5,6},{7,8},{9,10},{11,12},{13,14},{15,16},{17,18},{19... | collective-permute-start | bytes 1572872 | tf_op jit(solution)/shard_map/ppermute | solution.py:489
  11.3 0.0 copy-start
  11.3 2.8 %prepare.1 = (s32[32]{0:T(128)S(4)}, bf16[32,32,128]{2,1,0:T(8,128)(2,1)S(1)}, f32[32,128]{1,0:T(8,128)S(1)}, f32[32,128]{1,0:T(8,128)S(1)}, s32[32,128]{1,0:T(8,128)S(1)}, /*index=5*/bf16[64,8,128]{2,1,0:T(8,128)(2,1)}) custom-call(s32[1,32]{1,0:T(1,128)} %bitcast.2, s32[1,32]{1,0:T(1,128)} %bitcast.3, bf16[16,32]{1,0:T(8,128)(2,1)} %traces.3, ...), custom_call_target="tpu_custom_call" | custom-call | tf_op jit(solution)/shard_map/prepare/pallas_call | solution.py:132
  14.1 8.9 %all-to-all-start = ((bf16[64,8,128]{2,1,0:T(8,128)(2,1)}), bf16[64,8,128]{2,1,0:T(8,128)(2,1)S(1)}, u32[]{:S(2)}, u32[]{:S(2)}) async-start(bf16[64,8,128]{2,1,0:T(8,128)(2,1)} %get-tuple-element.17), calls=%async_computation | async-start | bytes 262144 | tf_op jit(solution)/shard_map/all_to_all | solution.py:501
  23.0 0.0 collective-permute-done.pair
  23.0 0.0 collective-permute-done.1.other
  23.0 0.0 copy-done
  23.0 6.6 %denoise.1 = (f32[32,16,128]{2,1,0:T(8,128)S(1)}, f32[16,128]{1,0:T(8,128)S(1)}) custom-call(s32[32]{0:T(128)S(4)} %get-tuple-element.16.starts, bf16[16,4,16,256]{3,2,1,0:T(8,128)(2,1)S(1)} %copy-done, bf16[16,4,16,256]{3,2,1,0:T(8,128)(2,1)S(1)} %collective-permute-done.pair, bf16[16,4,16,256]{3,2,1,0:T(8,128)(2,1)S(1)} %collective-permute-done.1.other, ...), custom_call_target="tpu_custom_call" | custom-call | tf_op jit(solution)/shard_map/denoise/pallas_call | solution.py:267
  29.6 4.5 %all-to-all-done.prior = bf16[64,8,128]{2,1,0:T(8,128)(2,1)S(1)} async-done(((bf16[64,8,128]{2,1,0:T(8,128)(2,1)}), bf16[64,8,128]{2,1,0:T(8,128)(2,1)S(1)}, u32[]{:S(2)}, u32[]{:S(2)}) %all-to-all-start) | async-done | bytes 131104 | tf_op jit(solution)/shard_map/all_to_all | solution.py:501
  34.1 0.6 combine.1
  34.7 0.0 copy-start.1
  34.7 16.7 %all_to_all.15.gathered = bf16[64,8,128]{2,1,0:T(8,128)(2,1)S(1)} all-to-all(bf16[64,8,128]{2,1,0:T(8,128)(2,1)S(1)} %get-tuple-element.22), channel_id=1, replica_groups=mesh['frames'=8,'bricks'=64] {'bricks'}, dimensions={0} | all-to-all | bytes 262144 | tf_op jit(solution)/shard_map/all_to_all | solution.py:504
  51.4 0.0 copy-done.1
  51.4 0.9 %update.1 = (f32[16,32]{1,0:T(8,128)S(1)}, f32[8,40,128]{2,1,0:T(8,128)S(1)}) custom-call(bf16[64,8,128]{2,1,0:T(8,128)(2,1)S(1)} %all-to-all-done.prior, bf16[64,8,128]{2,1,0:T(8,128)(2,1)S(1)} %all_to_all.15.gathered, s32[32,128]{1,0:T(8,128)S(1)} %get-tuple-element.18.labels, bf16[16,32]{1,0:T(8,128)(2,1)S(1)} %copy-done.1, ...), custom_call_target="tpu_custom_call" | custom-call | tf_op jit(solution)/shard_map/update/pallas_call | solution.py:413
  52.4 15.2 %all_to_all.16.shared = f32[8,40,128]{2,1,0:T(8,128)S(1)} all-to-all(f32[8,40,128]{2,1,0:T(8,128)S(1)} %get-tuple-element.25), channel_id=1, replica_groups=mesh['frames'=8,'bricks'=64] {'frames'}, dimensions={0} | all-to-all | bytes 327680 | tf_op jit(solution)/shard_map/all_to_all | solution.py:508
  67.6 1.8 %finish.1 = (bf16[32,16384]{1,0:T(8,128)(2,1)}, f32[16,32]{1,0:T(8,128)}) custom-call(s32[32]{0:T(128)S(4)} %get-tuple-element.16.starts, f32[8,40,128]{2,1,0:T(8,128)S(1)} %all_to_all.16.shared, bf16[32,32,128]{2,1,0:T(8,128)(2,1)S(1)} %get-tuple-element.26.windows, f32[32,128]{1,0:T(8,128)S(1)} %get-tuple-element.19.compact, ...), custom_call_target="tpu_custom_call" | custom-call | tf_op jit(solution)/shard_map/finish/pallas_call | solution.py:471
Async XLA Ops:
  0.6 22.4 %collective-permute-start = (bf16[16,4,16,256]{3,2,1,0:T(8,128)(2,1)}, bf16[16,4,16,256]{3,2,1,0:T(8,128)(2,1)S(1)}, u32[]{:S(2)}, u32[]{:S(2)}) collective-permute-start(bf16[16,4,16,256]{3,2,1,0:T(8,128)(2,1)} %rec.1), channel_id=1, source_target_pairs={{0,1},{2,3},{4,5},{6,7},{8,9},{10,11},{12,13},{14,15},{16,17},{18,... | collective-permute-start | bytes 1572872 | tf_op jit(solution)/shard_map/ppermute | solution.py:488
  9.4 13.6 %collective-permute-start.1 = (bf16[16,4,16,256]{3,2,1,0:T(8,128)(2,1)}, bf16[16,4,16,256]{3,2,1,0:T(8,128)(2,1)S(1)}, u32[]{:S(2)}, u32[]{:S(2)}) collective-permute-start(bf16[16,4,16,256]{3,2,1,0:T(8,128)(2,1)} %rec.1), channel_id=1, source_target_pairs={{1,2},{3,4},{5,6},{7,8},{9,10},{11,12},{13,14},{15,16},{17,18},{19... | collective-permute-start | bytes 1572872 | tf_op jit(solution)/shard_map/ppermute | solution.py:489
  11.3 11.7 %copy-start = (bf16[16,4,16,256]{3,2,1,0:T(8,128)(2,1)S(1)}, bf16[16,4,16,256]{3,2,1,0:T(8,128)(2,1)}, u32[]{:S(2)}) copy-start(bf16[16,4,16,256]{3,2,1,0:T(8,128)(2,1)} %rec.1) | copy-start | bytes 1572868
  14.1 20.0 %all-to-all-start = ((bf16[64,8,128]{2,1,0:T(8,128)(2,1)}), bf16[64,8,128]{2,1,0:T(8,128)(2,1)S(1)}, u32[]{:S(2)}, u32[]{:S(2)}) async-start(bf16[64,8,128]{2,1,0:T(8,128)(2,1)} %get-tuple-element.17), calls=%async_computation | async-start | bytes 262144 | tf_op jit(solution)/shard_map/all_to_all | solution.py:501
  34.7 16.7 %copy-start.1 = (bf16[16,32]{1,0:T(8,128)(2,1)S(1)}, bf16[16,32]{1,0:T(8,128)(2,1)}, u32[]{:S(2)}) copy-start(bf16[16,32]{1,0:T(8,128)(2,1)} %traces.3) | copy-start | bytes 3076

commit v9 on v8

--- a/solution.py
+++ b/solution.py
@@ -85,13 +85,16 @@
     return jnp.concatenate(rows + rows, axis=0) + jnp.where(lane < half, 0.0, moved)
 
 
-def prepare_kernel(owner, slot, traces, foot, starts, windows, compact, corr, labels, piece):
+def prepare_kernel(
+    owner, slot, traces, foot, starts, windows, compact, corr, labels, places, piece
+):
     blocks, voxels = foot.shape
     tiles = voxels // LANES
     acc = jnp.zeros((blocks, LANES), BF16)
     for t in range(1, tiles):
         cell = foot[:, t * LANES : (t + 1) * LANES]
         acc = jnp.maximum(acc, jnp.minimum(cell, jnp.asarray(t / MARK_SCALE, BF16)))
+    places[...] = acc
     tile_of = acc.astype(F32) * MARK_SCALE
     lowest = jnp.min(tile_of, axis=1, keepdims=True)
     highest = jnp.max(tile_of, axis=1, keepdims=True)
@@ -132,13 +135,14 @@
     return pl.pallas_call(
         prepare_kernel,
         in_specs=[VMEM] * 4,
-        out_specs=[SMEM, VMEM, VMEM, VMEM, VMEM, VMEM],
+        out_specs=[SMEM] + [VMEM] * 6,
         out_shape=[
             pltpu.SMEM((blocks,), jnp.int32),
             pltpu.VMEM((blocks, blocks, LANES), BF16),
             pltpu.VMEM((blocks, LANES), F32),
             pltpu.VMEM((blocks, LANES), F32),
             pltpu.VMEM((blocks, LANES), jnp.int32),
+            pltpu.VMEM((blocks, LANES), BF16),
             pltpu.VMEM((owners, SUBLANES, LANES), BF16),
         ],
         compiler_params=PARAMS,
@@ -152,6 +156,7 @@
 
 PITCH = 32
 TOP = 8
+AT_ONCE = 2
 
 
 def relax(planes, masks, held, passed, base):
@@ -241,10 +246,10 @@
 
         @pl.when(odd if is_odd else jnp.logical_not(odd))
         def _(low=low, high=high):
-            @pl.loop(0, frames // 2)
+            @pl.loop(0, frames // AT_ONCE)
             def _(g):
-                one_frame(2 * g, low, high, 0)
-                one_frame(2 * g + 1, low, high, 1)
+                for part in range(AT_ONCE):
+                    one_frame(AT_ONCE * g + part, low, high, part)
 
     blocks = compact.shape[0]
     tiles = planes * rows * 2
@@ -274,8 +279,8 @@
         ],
         scratch_shapes=[
             pltpu.VMEM((2, frames * planes * rows, LANES), F32),
-            pltpu.VMEM((2, 6 * (planes + 2) * PITCH, LANES), F32),
-            pltpu.VMEM((2, 6 * (planes + 2) * PITCH, LANES), F32),
+            pltpu.VMEM((2, 3 * AT_ONCE * (planes + 2) * PITCH, LANES), F32),
+            pltpu.VMEM((2, 3 * AT_ONCE * (planes + 2) * PITCH, LANES), F32),
         ],
         compiler_params=PARAMS,
         name="denoise",
@@ -402,10 +407,11 @@
     )
     for k in range(blocks):
         line = jnp.sum(voxel_windows[k] * slots[:, k : k + 1], axis=0, keepdims=True)
-        for g in range(sent.shape[0]):
-            sent[g, k : k + 1, :] = line
-    for g in range(sent.shape[0]):
-        sent[g, blocks : blocks + SUBLANES, :] = packed
+        sent[0, k : k + 1, :] = line
+    sent[0, blocks : blocks + SUBLANES, :] = packed
+    whole = sent[0]
+    for g in range(1, sent.shape[0]):
+        sent[g] = whole
 
 
 def update(prior, gathered, labels, traces, slot_prior, voxel_windows, groups):
@@ -430,14 +436,13 @@
     )
 
 
-def finish_kernel(starts, shared, windows, compact, fresh, out, traces_new):
+def finish_kernel(places, shared, windows, compact, fresh, out, traces_new):
     traces_new[...] = fresh[...]
     blocks, voxels = out.shape
     tiles = voxels // LANES
     groups = shared.shape[0]
     lane = iota((blocks, LANES), 1)
     row = iota((blocks, LANES), 0)
-    out[...] = jnp.zeros(out.shape, out.dtype)
     product = shared[0, :blocks, :]
     for g in range(1, groups):
         product = product + shared[g, :blocks, :]
@@ -455,22 +460,19 @@
     current = compact[...]
     stepped = jnp.maximum(current + (product - spread) / norm, 0.0)
     stepped = jnp.where(current > 0, stepped, 0.0)
-    height = 2 * SUBLANES
-    for k in range(blocks):
-        first, second, offset = split_run(starts[k], tiles)
-        group = slice(k // height * height, k // height * height + height)
-        chosen = row[group] == k
-        for index, part in ((first, lane[group] >= offset), (second, lane[group] < offset)):
-            at = lane_tile(index)
-            old = out[group, at].astype(F32)
-            out[group, at] = jnp.where(chosen & part, stepped[group], old).astype(out.dtype)
-
-
-def finish(starts, shared, windows, compact, fresh, voxels):
+    final = stepped.astype(out.dtype)
+    nothing = jnp.zeros(final.shape, out.dtype)
+    place = places[...]
+    for t in range(tiles):
+        here = place == jnp.asarray(t / MARK_SCALE, BF16)
+        out[:, t * LANES : (t + 1) * LANES] = jnp.where(here, final, nothing)
+
+
+def finish(places, shared, windows, compact, fresh, voxels):
     blocks = windows.shape[0]
     return pl.pallas_call(
         finish_kernel,
-        in_specs=[SMEM, VMEM, VMEM, VMEM, VMEM],
+        in_specs=[VMEM] * 5,
         out_specs=[VMEM, VMEM],
         out_shape=[
             jax.ShapeDtypeStruct((blocks, voxels), BF16),
@@ -478,7 +480,7 @@
         ],
         compiler_params=PARAMS,
         name="finish",
-    )(near_scalar(starts), near(shared), near(windows), near(compact), near(fresh))
+    )(near(places), near(shared), near(windows), near(compact), near(fresh))
 
 
 def swapped(recording):
@@ -497,7 +499,9 @@
     pair, other = swapped(recording)
     owner = block_owner.T
     slot = block_slot[None, :]
-    starts, windows, compact, corr, labels, piece = prepare(owner, slot, traces, footprints, owners)
+    starts, windows, compact, corr, labels, places, piece = prepare(
+        owner, slot, traces, footprints, owners
+    )
     prior = lax.all_to_all(piece, "bricks", 0, 0)
     voxel_windows, projected = denoise_windows(starts, recording, pair, other, compact)
     partials, slot_prior = combine(prior, labels, projected, corr)
@@ -506,7 +510,7 @@
         prior, gathered, labels, traces, slot_prior, voxel_windows, groups
     )
     shared = lax.all_to_all(sent, "frames", 0, 0)
-    footprints_new, traces_new = finish(starts, shared, windows, compact, fresh, voxels)
+    footprints_new, traces_new = finish(places, shared, windows, compact, fresh, voxels)
     return (traces_new, footprints_new)
 
 

time: 69.7 us -> 69.6 us (level)
  no operation moved by 1% of the time
where the time goes in v9:
time: 69.6 us; the launch traced here: 69.3 us
  blocking collectives  31.9 us (46%)
  starting transfers between devices  19.6 us (28%)
  Pallas kernels  12.6 us (18%)
  waiting for transfers between devices  4.46 us (6%)
  between operations  0.71 us (1%)
    all_to_all x1, blocking collectives, shards(): gathered = lax.all_to_all(partials, 'bricks', 0, 0)  16.7 us
    all_to_all x1, blocking collectives, shards(): shared = lax.all_to_all(sent, 'frames', 0, 0)  15.2 us
    all_to_all x1, starting transfers between devices, shards(): prior = lax.all_to_all(piece, 'bricks', 0, 0)  8.9 us
    ppermute x1, starting transfers between devices, swapped(): lax.ppermute(recording, 'bricks', within + [(b, a) for a, b in within])  8.75 us
    pallas_call x1, Pallas kernels, denoise_windows(): pl.pallas_call(denoise_kernel, in_specs=[SMEM, VMEM, VMEM, VMEM, VMEM], o...  6.6 us
    all_to_all x1, waiting for transfers between devices, shards(): prior = lax.all_to_all(piece, 'bricks', 0, 0)  4.46 us
    pallas_call x1, Pallas kernels, prepare(): pl.pallas_call(prepare_kernel, in_specs=[VMEM] * 4, out_specs=[SMEM] + [V...  2.77 us
    ppermute x1, starting transfers between devices, swapped(): lax.ppermute(recording, 'bricks', across + [(b, a) for a, b in across])  1.92 us
  transfers between devices with their start and end apart: 3, of which 1 were waited for; matrix products, arithmetic and copies ran while one was open for 0% of the time, Pallas kernels for 14%

profile of v9, /device:TPU:1, one launch (start us, length us, event | category | flops | bytes accessed | tf_op | source)
XLA Modules:
  0.0 69.3 jit_solution(9981121154491454064)
XLA Ops:
  0.6 8.7 %collective-permute-start = (bf16[16,4,16,256]{3,2,1,0:T(8,128)(2,1)}, bf16[16,4,16,256]{3,2,1,0:T(8,128)(2,1)S(1)}, u32[]{:S(2)}, u32[]{:S(2)}) collective-permute-start(bf16[16,4,16,256]{3,2,1,0:T(8,128)(2,1)} %rec.1), channel_id=1, source_target_pairs={{0,1},{2,3},{4,5},{6,7},{8,9},{10,11},{12,13},{14,15},{16,17},{18,... | collective-permute-start | bytes 1572872 | tf_op jit(solution)/shard_map/ppermute | solution.py:490
  9.4 1.9 %collective-permute-start.1 = (bf16[16,4,16,256]{3,2,1,0:T(8,128)(2,1)}, bf16[16,4,16,256]{3,2,1,0:T(8,128)(2,1)S(1)}, u32[]{:S(2)}, u32[]{:S(2)}) collective-permute-start(bf16[16,4,16,256]{3,2,1,0:T(8,128)(2,1)} %rec.1), channel_id=1, source_target_pairs={{1,2},{3,4},{5,6},{7,8},{9,10},{11,12},{13,14},{15,16},{17,18},{19... | collective-permute-start | bytes 1572872 | tf_op jit(solution)/shard_map/ppermute | solution.py:491
  11.3 0.0 copy-start
  11.3 2.8 %prepare.1 = (s32[32]{0:T(128)S(4)}, bf16[32,32,128]{2,1,0:T(8,128)(2,1)S(1)}, f32[32,128]{1,0:T(8,128)S(1)}, f32[32,128]{1,0:T(8,128)S(1)}, s32[32,128]{1,0:T(8...) custom-call(s32[1,32]{1,0:T(1,128)} %bitcast.2, s32[1,32]{1,0:T(1,128)} %bitcast.3, ...), custom_call_target="tpu_custom_call" | custom-call | tf_op jit(solution)/shard_map/prepare/pallas_call | solution.py:135
  14.1 8.9 %all-to-all-start = ((bf16[64,8,128]{2,1,0:T(8,128)(2,1)}), bf16[64,8,128]{2,1,0:T(8,128)(2,1)S(1)}, u32[]{:S(2)}, u32[]{:S(2)}) async-start(bf16[64,8,128]{2,1,0:T(8,128)(2,1)} %get-tuple-element.18), calls=%async_computation | async-start | bytes 262144 | tf_op jit(solution)/shard_map/all_to_all | solution.py:505
  23.0 0.0 collective-permute-done.pair
  23.0 0.0 collective-permute-done.1.other
  23.0 0.0 copy-done
  23.0 6.6 %denoise.1 = (f32[32,16,128]{2,1,0:T(8,128)S(1)}, f32[16,128]{1,0:T(8,128)S(1)}) custom-call(s32[32]{0:T(128)S(4)} %get-tuple-element.20.starts, bf16[16,4,16,256]{3,2,1,0:T(8,128)(2,1)S(1)} %copy-done, bf16[16,4,16,256]{3,2,1,0:T(8,128)(2,1)S(1)} %collective-permute-done.pair, bf16[16,4,16,256]{3,2,1,0:T(8,128)(2,1)S(1)} %collective-permute-done.1.other, ...), custom_call_target="tpu_custom_call" | custom-call | tf_op jit(solution)/shard_map/denoise/pallas_call | solution.py:272
  29.6 4.5 %all-to-all-done.prior = bf16[64,8,128]{2,1,0:T(8,128)(2,1)S(1)} async-done(((bf16[64,8,128]{2,1,0:T(8,128)(2,1)}), bf16[64,8,128]{2,1,0:T(8,128)(2,1)S(1)}, u32[]{:S(2)}, u32[]{:S(2)}) %all-to-all-start) | async-done | bytes 131104 | tf_op jit(solution)/shard_map/all_to_all | solution.py:505
  34.1 0.6 combine.1
  34.7 0.0 copy-start.1
  34.7 16.7 %all_to_all.15.gathered = bf16[64,8,128]{2,1,0:T(8,128)(2,1)S(1)} all-to-all(bf16[64,8,128]{2,1,0:T(8,128)(2,1)S(1)} %get-tuple-element.24), channel_id=1, replica_groups=mesh['frames'=8,'bricks'=64] {'bricks'}, dimensions={0} | all-to-all | bytes 262144 | tf_op jit(solution)/shard_map/all_to_all | solution.py:508
  51.4 0.0 copy-done.1
  51.4 0.9 %update.1 = (f32[16,32]{1,0:T(8,128)S(1)}, f32[8,40,128]{2,1,0:T(8,128)S(1)}) custom-call(bf16[64,8,128]{2,1,0:T(8,128)(2,1)S(1)} %all-to-all-done.prior, bf16[64,8,128]{2,1,0:T(8,128)(2,1)S(1)} %all_to_all.15.gathered, s32[32,128]{1,0:T(8,128)S(1)} %get-tuple-element.19.labels, bf16[16,32]{1,0:T(8,128)(2,1)S(1)} %copy-done.1, ...), custom_call_target="tpu_custom_call" | custom-call | tf_op jit(solution)/shard_map/update/pallas_call | solution.py:419
  52.3 15.2 %all_to_all.16.shared = f32[8,40,128]{2,1,0:T(8,128)S(1)} all-to-all(f32[8,40,128]{2,1,0:T(8,128)S(1)} %get-tuple-element.27), channel_id=1, replica_groups=mesh['frames'=8,'bricks'=64] {'frames'}, dimensions={0} | all-to-all | bytes 327680 | tf_op jit(solution)/shard_map/all_to_all | solution.py:512
  67.6 1.7 %finish.1 = (bf16[32,16384]{1,0:T(8,128)(2,1)}, f32[16,32]{1,0:T(8,128)}) custom-call(bf16[32,128]{1,0:T(8,128)(2,1)S(1)} %get-tuple-element.17.places, f32[8,40,128]{2,1,0:T(8,128)S(1)} %all_to_all.16.shared, bf16[32,32,128]{2,1,0:T(8,128)(2,1)S(1)} %get-tuple-element.28.windows, f32[32,128]{1,0:T(8,128)S(1)} %get-tuple-element.21.compact, ...), custom_call_target="tpu_custom_call" | custom-call | tf_op jit(solution)/shard_map/finish/pallas_call | solution.py:473
Async XLA Ops:
  0.6 22.4 %collective-permute-start = (bf16[16,4,16,256]{3,2,1,0:T(8,128)(2,1)}, bf16[16,4,16,256]{3,2,1,0:T(8,128)(2,1)S(1)}, u32[]{:S(2)}, u32[]{:S(2)}) collective-permute-start(bf16[16,4,16,256]{3,2,1,0:T(8,128)(2,1)} %rec.1), channel_id=1, source_target_pairs={{0,1},{2,3},{4,5},{6,7},{8,9},{10,11},{12,13},{14,15},{16,17},{18,... | collective-permute-start | bytes 1572872 | tf_op jit(solution)/shard_map/ppermute | solution.py:490
  9.4 13.6 %collective-permute-start.1 = (bf16[16,4,16,256]{3,2,1,0:T(8,128)(2,1)}, bf16[16,4,16,256]{3,2,1,0:T(8,128)(2,1)S(1)}, u32[]{:S(2)}, u32[]{:S(2)}) collective-permute-start(bf16[16,4,16,256]{3,2,1,0:T(8,128)(2,1)} %rec.1), channel_id=1, source_target_pairs={{1,2},{3,4},{5,6},{7,8},{9,10},{11,12},{13,14},{15,16},{17,18},{19... | collective-permute-start | bytes 1572872 | tf_op jit(solution)/shard_map/ppermute | solution.py:491
  11.3 11.7 %copy-start = (bf16[16,4,16,256]{3,2,1,0:T(8,128)(2,1)S(1)}, bf16[16,4,16,256]{3,2,1,0:T(8,128)(2,1)}, u32[]{:S(2)}) copy-start(bf16[16,4,16,256]{3,2,1,0:T(8,128)(2,1)} %rec.1) | copy-start | bytes 1572868
  14.1 20.0 %all-to-all-start = ((bf16[64,8,128]{2,1,0:T(8,128)(2,1)}), bf16[64,8,128]{2,1,0:T(8,128)(2,1)S(1)}, u32[]{:S(2)}, u32[]{:S(2)}) async-start(bf16[64,8,128]{2,1,0:T(8,128)(2,1)} %get-tuple-element.18), calls=%async_computation | async-start | bytes 262144 | tf_op jit(solution)/shard_map/all_to_all | solution.py:505
  34.7 16.7 %copy-start.1 = (bf16[16,32]{1,0:T(8,128)(2,1)S(1)}, bf16[16,32]{1,0:T(8,128)(2,1)}, u32[]{:S(2)}) copy-start(bf16[16,32]{1,0:T(8,128)(2,1)} %traces.3) | copy-start | bytes 3076
